TPU v7x, 512 devices: a whole 4x4x16 slice. The times are simulated.
512 devices in a mesh: dp: 16 (over y, x), expert: 32 (over z, core).
Axes of the slice: x: 4, y: 4, z: 16, core: 2. Of those that a mesh axis runs over, the one named last changes fastest.
Arguments:
- query_rows: bfloat16 [32, 2048, 2048], P('dp', 'expert'), may hold values from -4 to 4
- key_rows: bfloat16 [32, 2048, 256], P('dp', 'expert'), may hold values from -4 to 4
- value_rows: bfloat16 [32, 2048, 256], P('dp', 'expert'), may hold values from -6 to 6
- gate_logits: bfloat16 [32, 2048, 2048], P('dp', 'expert'), may hold values from -6 to 6
- gated_grad: bfloat16 [32, 2048, 2048], P('dp', 'expert'), may hold values from -6 to 6
- moe_input: bfloat16 [65536, 2048], P(('dp', 'expert')), may hold values from -6 to 6
- out_grad: bfloat16 [65536, 2048], P(('dp', 'expert')), may hold values from -24 to 24
- routes: int32 [65536, 10], P(('dp', 'expert')), may hold values from 0 to 511, as said below
- route_weights: bfloat16 [65536, 10], P(('dp', 'expert')), may hold values from 0.019897461 to 0.29882812
- gate_proj: bfloat16 [32, 2048, 256], P('expert', 'dp'), may hold values from -0.125 to 0.125
- up_proj: bfloat16 [32, 2048, 256], P('expert', 'dp'), may hold values from -0.125 to 0.125
- down_proj: bfloat16 [32, 256, 2048], P('expert', None, 'dp'), may hold values from -0.375 to 0.375
Outputs:
- query_grad: bfloat16 [32, 2048, 2048], P('dp', 'expert')
- key_grad: bfloat16 [32, 2048, 256], P('dp', 'expert')
- value_grad: bfloat16 [32, 2048, 256], P('dp', 'expert')
- gate_grad: bfloat16 [32, 2048, 2048], P('dp', 'expert')
- input_grad: bfloat16 [65536, 2048], P(('dp', 'expert'))
- route_grad: bfloat16 [65536, 10], P(('dp', 'expert'))
- gate_proj_grad: float32 [32, 2048, 256], P('expert', 'dp')
- up_proj_grad: float32 [32, 2048, 256], P('expert', 'dp')
- down_proj_grad: float32 [32, 256, 2048], P('expert', None, 'dp')
Inputs may be any that keep to these rules, and one draw needn't show every extreme that they name: `routes`: each token names 10 different experts. A token names at most one expert below 32; the 128 tokens of one block name each such expert at most 2 times, and in every data group one expert below 32 is named exactly 2 times by every block of the group.
All inputs are finite; a program needn't handle non-finite values.
Results may differ from a plain program's by a relative error of at most 0.035.
Values may be sent and summed in bfloat16 or wider, within the bound.
A program may use at most 64 MiB of HBM per device.

v0:
```python
import jax
import jax.numpy as jnp
from jax import lax
from jax.sharding import PartitionSpec as P

HEADS = 8
HEAD = 256
CAP = 2


def keep_state(run_state):
    return run_state


def block_scores(queries, keys_block, block_start, first_position, score_scale):
    scores = (
        jnp.einsum("sphd,srd->shpr", queries, keys_block, preferred_element_type=jnp.float32)
        * score_scale
    )
    query_pos = first_position + jnp.arange(queries.shape[1])
    key_pos = block_start + jnp.arange(keys_block.shape[1])
    allowed = key_pos[None, :] <= query_pos[:, None]
    return (scores, allowed[None, None])


def shards(
    query_rows,
    key_rows,
    value_rows,
    gate_logits,
    gated_grad,
    moe_input,
    out_grad,
    routes,
    route_weights,
    gate_proj,
    up_proj,
    down_proj,
):
    seq_count, shard_len, row_width = query_rows.shape
    devices = lax.axis_size("expert")
    position = lax.axis_index("expert")
    first_position = position * shard_len
    last_position = first_position + shard_len - 1
    total_len = shard_len * devices
    block_len = min(total_len, max(shard_len, 128))
    block_count = total_len // block_len
    shards_per_block = block_len // shard_len
    score_scale = HEAD ** (-0.5)
    queries = query_rows.reshape(seq_count, shard_len, HEADS, HEAD)
    packed = jnp.concatenate([key_rows, value_rows], axis=2)
    gathered = lax.all_gather(packed, "expert", axis=1, tiled=True)

    def take_block(block_index):
        block_start = block_index * block_len
        key_piece = lax.dynamic_slice_in_dim(gathered, block_start, block_len, 1)
        return (block_start, key_piece[:, :, :HEAD], key_piece[:, :, HEAD:])

    def max_step(block_index, loop_carry):
        block_start, keys_block, values_block = take_block(block_index)

        def max_update(run_state):
            prior_max, prior_sum = run_state
            scores, allowed = block_scores(
                queries, keys_block, block_start, first_position, score_scale
            )
            masked = jnp.where(allowed, scores, -jnp.inf)
            new_max = jnp.maximum(prior_max, jnp.max(masked, axis=3))
            new_sum = prior_sum * jnp.exp(prior_max - new_max) + jnp.sum(
                jnp.exp(masked - new_max[..., None]), axis=3
            )
            return (new_max, new_sum)

        return lax.cond(block_start <= last_position, max_update, keep_state, loop_carry)

    stat_shape = (seq_count, HEADS, shard_len)
    run_max, run_sum = lax.fori_loop(
        0,
        block_count,
        max_step,
        (jnp.full(stat_shape, -jnp.inf, jnp.float32), jnp.zeros(stat_shape, jnp.float32)),
    )
    log_total = run_max + jnp.log(run_sum)

    def context_step(block_index, loop_carry):
        block_start, keys_block, values_block = take_block(block_index)

        def context_update(running_total):
            scores, allowed = block_scores(
                queries, keys_block, block_start, first_position, score_scale
            )
            exact_probs = jnp.where(allowed, jnp.exp(scores - log_total[..., None]), 0.0)
            return running_total + jnp.einsum(
                "shpr,srd->sphd",
                exact_probs.astype(jnp.bfloat16),
                values_block,
                preferred_element_type=jnp.float32,
            )

        return lax.cond(block_start <= last_position, context_update, keep_state, loop_carry)

    context = lax.fori_loop(
        0, block_count, context_step, jnp.zeros((seq_count, shard_len, HEADS, HEAD), jnp.float32)
    )
    sigmoid_gate = jax.nn.sigmoid(gate_logits.astype(jnp.float32)).reshape(
        seq_count, shard_len, HEADS, HEAD
    )
    upstream = gated_grad.astype(jnp.float32).reshape(seq_count, shard_len, HEADS, HEAD)
    context_grad = (upstream * sigmoid_gate).astype(jnp.bfloat16)
    gate_grad = (
        (upstream * context * sigmoid_gate * (1.0 - sigmoid_gate))
        .astype(jnp.bfloat16)
        .reshape(seq_count, shard_len, row_width)
    )
    grad_dot = jnp.transpose(jnp.sum(context_grad.astype(jnp.float32) * context, axis=3), (0, 2, 1))

    def grad_step(block_index, loop_carry):
        block_start, keys_block, values_block = take_block(block_index)

        def grad_update(run_state):
            query_total, pair_buffer = run_state
            scores, allowed = block_scores(
                queries, keys_block, block_start, first_position, score_scale
            )
            exact_probs = jnp.where(allowed, jnp.exp(scores - log_total[..., None]), 0.0)
            probs_low = exact_probs.astype(jnp.bfloat16)
            prob_grad = jnp.einsum(
                "sphd,srd->shpr", context_grad, values_block, preferred_element_type=jnp.float32
            )
            score_grad = (exact_probs * (prob_grad - grad_dot[..., None]) * score_scale).astype(
                jnp.bfloat16
            )
            query_total = query_total + jnp.einsum(
                "shpr,srd->sphd", score_grad, keys_block, preferred_element_type=jnp.float32
            )
            key_part = jnp.einsum(
                "shpr,sphd->srd", score_grad, queries, preferred_element_type=jnp.float32
            ).astype(jnp.bfloat16)
            value_part = jnp.einsum(
                "shpr,sphd->srd", probs_low, context_grad, preferred_element_type=jnp.float32
            ).astype(jnp.bfloat16)
            pair_block = jnp.concatenate([key_part, value_part], axis=2)
            pair_block = jnp.moveaxis(
                pair_block.reshape(seq_count, shards_per_block, shard_len, 2 * HEAD), 1, 0
            )
            pair_buffer = lax.dynamic_update_slice_in_dim(
                pair_buffer, pair_block, block_start // shard_len, 0
            )
            return (query_total, pair_buffer)

        return lax.cond(block_start <= last_position, grad_update, keep_state, loop_carry)

    query_total, pair_buffer = lax.fori_loop(
        0,
        block_count,
        grad_step,
        (
            jnp.zeros((seq_count, shard_len, HEADS, HEAD), jnp.float32),
            jnp.zeros((devices, seq_count, shard_len, 2 * HEAD), jnp.bfloat16),
        ),
    )
    query_grad = query_total.astype(jnp.bfloat16).reshape(seq_count, shard_len, row_width)
    token_count, model_width = moe_input.shape
    live_slot = routes < devices
    has_live = jnp.any(live_slot, axis=1)
    live_expert = jnp.sum(jnp.where(live_slot, routes, 0), axis=1)
    token_weight = jnp.sum(jnp.where(live_slot, route_weights.astype(jnp.float32), 0.0), axis=1)
    member = (live_expert[:, None] == jnp.arange(devices)[None, :]) & has_live[:, None]
    earlier = (jnp.arange(token_count)[None, :] < jnp.arange(token_count)[:, None]).astype(
        jnp.bfloat16
    )
    before = jnp.dot(earlier, member.astype(jnp.bfloat16), preferred_element_type=jnp.float32)
    slot_rank = jnp.sum(jnp.where(member, before, 0.0), axis=1)
    placed = member.T[:, None, :] & (
        slot_rank[None, None, :] == jnp.arange(CAP)[None, :, None].astype(jnp.float32)
    )
    dispatch_mat = placed.reshape(devices * CAP, token_count).astype(jnp.bfloat16)
    rows_send = (
        jnp.dot(dispatch_mat, moe_input, preferred_element_type=jnp.float32)
        .astype(jnp.bfloat16)
        .reshape(devices, CAP, model_width)
    )
    grads_send = (
        jnp.dot(dispatch_mat, out_grad, preferred_element_type=jnp.float32)
        .astype(jnp.bfloat16)
        .reshape(devices, CAP, model_width)
    )
    weights_send = jnp.sum(jnp.where(placed, token_weight[None, None, :], 0.0), axis=2).astype(
        jnp.bfloat16
    )
    gate_full, up_full, down_full = (
        lax.all_gather(gate_proj, "dp", axis=1, tiled=True),
        lax.all_gather(up_proj, "dp", axis=1, tiled=True),
        lax.all_gather(down_proj, "dp", axis=2, tiled=True),
    )
    gate_mat = gate_full[0]
    up_mat = up_full[0]
    down_mat = down_full[0]
    rows_in, grads_in, weights_in = (
        lax.all_to_all(rows_send, "expert", split_axis=0, concat_axis=0, tiled=True),
        lax.all_to_all(grads_send, "expert", split_axis=0, concat_axis=0, tiled=True),
        lax.all_to_all(weights_send, "expert", split_axis=0, concat_axis=0, tiled=True),
    )
    flat_rows = rows_in.reshape(devices * CAP, model_width)
    flat_grads = grads_in.reshape(devices * CAP, model_width)
    gate_pre = jnp.dot(flat_rows, gate_mat, preferred_element_type=jnp.float32)
    up_pre = jnp.dot(flat_rows, up_mat, preferred_element_type=jnp.float32)
    sigmoid_pre = jax.nn.sigmoid(gate_pre)
    silu_value = gate_pre * sigmoid_pre
    hidden = (silu_value * up_pre).astype(jnp.bfloat16)
    expert_out = jnp.dot(hidden, down_mat, preferred_element_type=jnp.float32)
    weight_back = jnp.sum(expert_out * flat_grads.astype(jnp.float32), axis=1).astype(jnp.bfloat16)
    scaled_grad = (
        weights_in.reshape(-1)[:, None].astype(jnp.float32) * flat_grads.astype(jnp.float32)
    ).astype(jnp.bfloat16)
    contract_last = (((1,), (1,)), ((), ()))
    hidden_grad = lax.dot_general(
        scaled_grad, down_mat, contract_last, preferred_element_type=jnp.float32
    )
    slope = sigmoid_pre * (1.0 + gate_pre * (1.0 - sigmoid_pre))
    gate_rows = (hidden_grad * up_pre * slope).astype(jnp.bfloat16)
    up_rows = (hidden_grad * silu_value).astype(jnp.bfloat16)
    input_rows = (
        lax.dot_general(gate_rows, gate_mat, contract_last, preferred_element_type=jnp.float32)
        + lax.dot_general(up_rows, up_mat, contract_last, preferred_element_type=jnp.float32)
    ).astype(jnp.bfloat16)
    hidden_width = hidden.shape[1]
    contract_first = (((0,), (0,)), ((), ()))
    summed = lax.psum_scatter(
        jnp.concatenate(
            [
                lax.dot_general(
                    flat_rows, gate_rows, contract_first, preferred_element_type=jnp.float32
                ),
                lax.dot_general(
                    flat_rows, up_rows, contract_first, preferred_element_type=jnp.float32
                ),
                lax.dot_general(
                    scaled_grad, hidden, contract_first, preferred_element_type=jnp.float32
                ),
            ],
            axis=1,
        ).astype(jnp.bfloat16),
        "dp",
        scatter_dimension=0,
        tiled=True,
    ).astype(jnp.float32)
    gate_proj_grad = summed[:, :hidden_width][None]
    up_proj_grad = summed[:, hidden_width : 2 * hidden_width][None]
    down_proj_grad = jnp.transpose(summed[:, 2 * hidden_width :])[None]
    pairs_back, input_back, weights_back = (
        lax.all_to_all(pair_buffer, "expert", split_axis=0, concat_axis=0, tiled=True),
        lax.all_to_all(
            input_rows.reshape(devices, CAP, model_width),
            "expert",
            split_axis=0,
            concat_axis=0,
            tiled=True,
        ),
        lax.all_to_all(
            weight_back.reshape(devices, CAP), "expert", split_axis=0, concat_axis=0, tiled=True
        ),
    )
    pair_total = jnp.sum(pairs_back.astype(jnp.float32), axis=0).astype(jnp.bfloat16)
    key_grad = pair_total[:, :, :HEAD]
    value_grad = pair_total[:, :, HEAD:]
    input_grad = lax.dot_general(
        dispatch_mat,
        input_back.reshape(devices * CAP, model_width),
        contract_first,
        preferred_element_type=jnp.float32,
    ).astype(jnp.bfloat16)
    token_back = jnp.sum(
        dispatch_mat.astype(jnp.float32) * weights_back.reshape(-1).astype(jnp.float32)[:, None],
        axis=0,
    )
    route_grad = jnp.where(live_slot, token_back[:, None], 0.0).astype(jnp.bfloat16)
    return (
        query_grad,
        key_grad,
        value_grad,
        gate_grad,
        input_grad,
        route_grad,
        gate_proj_grad,
        up_proj_grad,
        down_proj_grad,
    )


def solution(mesh):
    return jax.shard_map(
        shards,
        mesh=mesh,
        in_specs=(
            P("dp", "expert", None),
            P("dp", "expert", None),
            P("dp", "expert", None),
            P("dp", "expert", None),
            P("dp", "expert", None),
            P(("dp", "expert"), None),
            P(("dp", "expert"), None),
            P(("dp", "expert"), None),
            P(("dp", "expert"), None),
            P("expert", "dp", None),
            P("expert", "dp", None),
            P("expert", None, "dp"),
        ),
        out_specs=(
            P("dp", "expert", None),
            P("dp", "expert", None),
            P("dp", "expert", None),
            P("dp", "expert", None),
            P(("dp", "expert"), None),
            P(("dp", "expert"), None),
            P("expert", "dp", None),
            P("expert", "dp", None),
            P("expert", None, "dp"),
        ),
        check_vma=False,
    )
```

profile of v0, /device:TPU:1, one launch (start us, length us, event | category | flops | bytes accessed | tf_op | source)
XLA Modules:
  0.0 625.2 jit_solution(12488926935791719670)
XLA Ops:
  7.2 0.7 all-gather.11.cloned.1.call-update
  8.0 0.7 all-gather.9.cloned.1.call-update
  8.7 0.7 all-gather.7.cloned.1.call-update
  9.5 1.5 pad_maximum_fusion.2
  11.0 0.7 select_reduce_fusion.1
  11.8 0.7 select_reduce_fusion.2
  13.7 0.9 reshape.306
  14.6 16.7 %all-to-all-start.3 = ((bf16[32,2,2048]{2,1,0:T(2,128)(2,1)}), bf16[32,2,2048]{2,1,0:T(2,128)(2,1)S(1)}, u32[]{:S(2)}, u32[]{:S(2)}) async-start(bf16[32,2,2048]{2,1,0:T(2,128)(2,1)} %reshape.306), calls=%async_computation.3 | async-start | bytes 524288 | tf_op jit(solution)/shard_map/all_to_all | solution.py:200
  31.3 1.3 convolution_convert_fusion.4
  32.6 0.9 reshape.305
  33.5 19.8 %all-to-all-done.3 = bf16[32,2,2048]{2,1,0:T(2,128)(2,1)S(1)} async-done(((bf16[32,2,2048]{2,1,0:T(2,128)(2,1)}), bf16[32,2,2048]{2,1,0:T(2,128)(2,1)S(1)}, u32[]{:S(2)}, u32[]{:S(2)}) %all-to-all-start.3) | async-done | bytes 262176 | tf_op jit(solution)/shard_map/all_to_all | solution.py:200
  53.3 4.5 all-to-all-start.2
  58.0 21.9 %all-to-all-done.2 = bf16[32,2,2048]{2,1,0:T(2,128)(2,1)S(1)} async-done(((bf16[32,2,2048]{2,1,0:T(2,128)(2,1)}), bf16[32,2,2048]{2,1,0:T(2,128)(2,1)S(1)}, u32[]{:S(2)}, u32[]{:S(2)}) %all-to-all-start.2) | async-done | bytes 262176 | tf_op jit(solution)/shard_map/all_to_all | solution.py:201
  80.0 1.7 fusion.41
  81.7 51.7 %all-gather.9.cloned.1.call-done = bf16[1,2048,256]{2,1,0:T(8,128)(2,1)} async-done(((bf16[1,128,256]{2,1,0:T(8,128)(2,1)}), bf16[1,2048,256]{2,1,0:T(8,128)(2,1)}) %all-gather.9.cloned.1.call-update) | async-done | bytes 1048592 | tf_op jit(solution)/shard_map/all_gather | solution.py:193
  133.4 2.2 multiply_convert_fusion.3
  135.6 58.8 %all-gather.7.cloned.1.call-done = bf16[1,256,2048]{2,1,0:T(8,128)(2,1)} async-done(((bf16[1,256,128]{2,1,0:T(8,128)(2,1)}), bf16[1,256,2048]{2,1,0:T(8,128)(2,1)}) %all-gather.7.cloned.1.call-update) | async-done | bytes 1048592 | tf_op jit(solution)/shard_map/all_gather | solution.py:194
  194.5 1.6 fusion.34
  196.1 0.7 convert_element_type.223
  196.8 14.4 %all-to-all-start.5 = ((bf16[32,1,2]{2,1,0:T(2,128)(2,1)}), bf16[32,1,2]{2,1,0:T(2,128)(2,1)S(1)}, u32[]{:S(2)}, u32[]{:S(2)}) async-start(bf16[32,1,2]{2,1,0:T(2,128)(2,1)} %convert_element_type.223), calls=%async_computation.5 | async-start | bytes 32768 | tf_op jit(solution)/shard_map/all_to_all | solution.py:260
  211.2 11.7 %all-to-all-done.5 = bf16[32,1,2]{2,1,0:T(2,128)(2,1)S(1)} async-done(((bf16[32,1,2]{2,1,0:T(2,128)(2,1)}), bf16[32,1,2]{2,1,0:T(2,128)(2,1)S(1)}, u32[]{:S(2)}, u32[]{:S(2)}) %all-to-all-start.5) | async-done | bytes 160 | tf_op jit(solution)/shard_map/all_to_all | solution.py:260
  223.1 0.6 multiply_reduce_fusion.1
  223.9 0.7 copy.74
  224.6 4.4 all-to-all-start.1
  229.0 1.1 copy.106
  230.1 10.7 %all-to-all-done.1 = bf16[32,1,2]{2,1,0:T(2,128)(2,1)S(1)} async-done(((bf16[32,1,2]{2,1,0:T(2,128)(2,1)}), bf16[32,1,2]{2,1,0:T(2,128)(2,1)S(1)}, u32[]{:S(2)}, u32[]{:S(2)}) %all-to-all-start.1) | async-done | bytes 160 | tf_op jit(solution)/shard_map/all_to_all | solution.py:202
  240.9 1.9 multiply_convert_fusion.1
  242.8 1.8 convert_element_type.199
  244.6 1.7 multiply_convert_fusion.4
  247.3 0.9 reshape.308
  248.2 5.1 all-to-all-start.4
  253.4 1.3 add_divide_fusion
  255.0 2.1 copy.96
  257.2 21.7 %all-gather.5.cloned.1.call-done = bf16[2,2048,512]{2,1,0:T(8,128)(2,1)} async-done(((bf16[2,64,512]{2,1,0:T(8,128)(2,1)}), bf16[2,2048,512]{2,1,0:T(8,128)(2,1)}) %all-gather.5.cloned.1.call-update) | async-done | bytes 4194320 | tf_op jit(solution)/shard_map/all_gather | solution.py:52
  278.8 2.4 while.46
  278.8 1.8 conditional.6
  278.9 1.3 fusion.59
  281.4 2.2 while.47
  281.4 1.6 conditional.7
  281.5 1.4 fusion.3
  283.6 3.3 multiply_reduce_fusion
  287.0 0.9 copy.69
  288.0 2.5 broadcast_in_dim.117
  290.5 5.4 while.48
  290.5 5.1 conditional.8
  290.6 1.2 fusion.24
  291.9 1.2 fusion.25
  293.1 1.2 fusion.17
  295.0 0.7 constant_dynamic-update-slice_fusion
  296.0 4.6 copy.71
  300.6 131.2 %all-to-all-start = ((bf16[32,2,64,512]{3,2,1,0:T(8,128)(2,1)}), bf16[32,2,64,512]{3,2,1,0:T(8,128)(2,1)}, u32[]{:S(2)}, u32[]{:S(2)}) async-start(bf16[32,2,64,512]{3,2,1,0:T(8,128)(2,1)} %copy.71), calls=%async_computation | async-start | bytes 8388608 | tf_op jit(solution)/shard_map/all_to_all | solution.py:252
  433.7 1.9 pad_maximum_fusion.1
  435.6 4.7 copy.92
  441.0 2.1 fusion.32
  443.2 0.8 copy.95
  444.0 1.0 reshape.304
  445.0 86.4 %reduce-scatter.4.cloned.1.call-done = bf16[128,768]{1,0:T(8,128)(2,1)} async-done(((bf16[2048,768]{1,0:T(8,128)(2,1)}), bf16[128,768]{1,0:T(8,128)(2,1)}) %reduce-scatter.4.cloned.1.call-update) | async-done | bytes 196624
  531.4 1.1 copy.93
  532.6 0.7 slice_bitcast_fusion
  533.2 0.8 copy.82
  534.0 0.8 copy.83
  534.7 80.4 %all-to-all-done = bf16[32,2,64,512]{3,2,1,0:T(8,128)(2,1)} async-done(((bf16[32,2,64,512]{3,2,1,0:T(8,128)(2,1)}), bf16[32,2,64,512]{3,2,1,0:T(8,128)(2,1)}, u32[]{:S(2)}, u32[]{:S(2)}) %all-to-all-start) | async-done | bytes 4194336 | tf_op jit(solution)/shard_map/all_to_all | solution.py:252
  615.1 2.9 reduce_sum.87
  618.0 0.7 fusion.60
  (130 shorter events, 7.7 us)
Async XLA Ops:
  7.2 6.3 %copy-start = (bf16[128,2048]{1,0:T(8,128)(2,1)S(1)}, bf16[128,2048]{1,0:T(8,128)(2,1)}, u32[]{:S(2)}) copy-start(bf16[128,2048]{1,0:T(8,128)(2,1)} %param.29) | copy-start | bytes 1572868
  7.2 72.8 %all-gather.11.cloned.1.call-start = ((), (), s32[]{:S(2)}) async-start(), calls=%async_computation.10 | async-start | bytes 1114112 | tf_op jit(solution)/shard_map/all_gather | solution.py:192
  7.9 125.4 %all-gather.9.cloned.1.call-start = ((), (), s32[]{:S(2)}) async-start(), calls=%async_computation.9 | async-start | bytes 1114112 | tf_op jit(solution)/shard_map/all_gather | solution.py:193
  8.7 185.8 %all-gather.7.cloned.1.call-start = ((), (), s32[]{:S(2)}) async-start(), calls=%async_computation.8 | async-start | bytes 1114112 | tf_op jit(solution)/shard_map/all_gather | solution.py:194
  9.4 269.4 %all-gather.5.cloned.1.call-start = ((), (), s32[]{:S(2)}) async-start(), calls=%async_computation.7 | async-start | bytes 4325376 | tf_op jit(solution)/shard_map/all_gather | solution.py:52
  11.8 1.0 copy-start.11
  12.8 0.6 copy-start.9
  14.6 38.8 %all-to-all-start.3 = ((bf16[32,2,2048]{2,1,0:T(2,128)(2,1)}), bf16[32,2,2048]{2,1,0:T(2,128)(2,1)S(1)}, u32[]{:S(2)}, u32[]{:S(2)}) async-start(bf16[32,2,2048]{2,1,0:T(2,128)(2,1)} %reshape.306), calls=%async_computation.3 | async-start | bytes 524288 | tf_op jit(solution)/shard_map/all_to_all | solution.py:200
  53.3 26.5 %all-to-all-start.2 = ((bf16[32,2,2048]{2,1,0:T(2,128)(2,1)}), bf16[32,2,2048]{2,1,0:T(2,128)(2,1)S(1)}, u32[]{:S(2)}, u32[]{:S(2)}) async-start(bf16[32,2,2048]{2,1,0:T(2,128)(2,1)} %reshape.305), calls=%async_computation.2 | async-start | bytes 524288 | tf_op jit(solution)/shard_map/all_to_all | solution.py:201
  79.9 1.8 copy-start.5
  79.9 149.1 %copy-start.1 = (f32[64,2048]{1,0:T(8,128)}, f32[64,2048]{1,0:T(8,128)S(1)}, u32[]{:S(2)}) copy-start(f32[64,2048]{1,0:T(8,128)S(1)} %reshape.312) | copy-start | bytes 1572868
  80.0 166.3 %copy-start.4 = (bf16[1,2048,256]{2,1,0:T(8,128)(2,1)S(1)}, bf16[1,2048,256]{2,1,0:T(8,128)(2,1)}, u32[]{:S(2)}) copy-start(bf16[1,2048,256]{2,1,0:T(8,128)(2,1)} %all-gather.11.cloned.1.call-done) | copy-start | bytes 3145732
  133.4 113.5 %copy-start.3 = (bf16[1,2048,256]{2,1,0:T(8,128)(2,1)S(1)}, bf16[1,2048,256]{2,1,0:T(8,128)(2,1)}, u32[]{:S(2)}) copy-start(bf16[1,2048,256]{2,1,0:T(8,128)(2,1)} %all-gather.9.cloned.1.call-done) | copy-start | bytes 3145732
  196.8 26.1 %all-to-all-start.5 = ((bf16[32,1,2]{2,1,0:T(2,128)(2,1)}), bf16[32,1,2]{2,1,0:T(2,128)(2,1)S(1)}, u32[]{:S(2)}, u32[]{:S(2)}) async-start(bf16[32,1,2]{2,1,0:T(2,128)(2,1)} %convert_element_type.223), calls=%async_computation.5 | async-start | bytes 32768 | tf_op jit(solution)/shard_map/all_to_all | solution.py:260
  224.6 16.3 %all-to-all-start.1 = ((bf16[32,1,2]{2,1,0:T(2,128)(2,1)}), bf16[32,1,2]{2,1,0:T(2,128)(2,1)S(1)}, u32[]{:S(2)}, u32[]{:S(2)}) async-start(bf16[32,1,2]{2,1,0:T(2,128)(2,1)} %copy.74), calls=%async_computation.1 | async-start | bytes 32768 | tf_op jit(solution)/shard_map/all_to_all | solution.py:202
  246.3 0.6 copy-start.7
  248.2 52.4 %all-to-all-start.4 = ((bf16[32,2,2048]{2,1,0:T(2,128)(2,1)}), bf16[32,2,2048]{2,1,0:T(2,128)(2,1)}, u32[]{:S(2)}, u32[]{:S(2)}) async-start(bf16[32,2,2048]{2,1,0:T(2,128)(2,1)} %reshape.308), calls=%async_computation.4 | async-start | bytes 524288 | tf_op jit(solution)/shard_map/all_to_all | solution.py:253
  300.6 132.1 %copy-start.8 = (bf16[64,256]{1,0:T(8,128)(2,1)S(1)}, bf16[64,256]{1,0:T(8,128)(2,1)}, u32[]{:S(2)}) copy-start(bf16[64,256]{1,0:T(8,128)(2,1)} %copy-done.7) | copy-start | bytes 98308
  300.6 132.6 %copy-start.2 = (f32[64,2048]{1,0:T(8,128)S(1)}, f32[64,2048]{1,0:T(8,128)}, u32[]{:S(2)}) copy-start(f32[64,2048]{1,0:T(8,128)} %copy-done.1) | copy-start | bytes 1572868
  300.6 314.5 %all-to-all-start = ((bf16[32,2,64,512]{3,2,1,0:T(8,128)(2,1)}), bf16[32,2,64,512]{3,2,1,0:T(8,128)(2,1)}, u32[]{:S(2)}, u32[]{:S(2)}) async-start(bf16[32,2,64,512]{3,2,1,0:T(8,128)(2,1)} %copy.71), calls=%async_computation | async-start | bytes 8388608 | tf_op jit(solution)/shard_map/all_to_all | solution.py:252
  431.9 99.6 %reduce-scatter.4.cloned.1.call-start = ((), (), s32[]{:S(2)}) async-start(), calls=%async_computation.11 | async-start | bytes 3342336
  435.6 4.8 copy-start.12
  435.6 4.8 copy-start.13
  435.6 5.4 copy-start.10
  440.4 3.6 copy-start.6
Sparse Core Ops, SparseCore 0:
  11.0 62.0 all-gather.10
  76.2 57.1 all-gather.8
  136.4 58.0 all-gather.6
  197.0 81.7 all-gather.4
  440.5 90.8 reduce-scatter.3
where the time goes:
time: 634 us; the launch traced here: 625 us
  waiting for transfers between devices  365 us (58%)
  starting transfers between devices  177 us (28%)
  local copies, waits for them, and re-layouts  30.5 us (5%)
  matrix products  20.3 us (3%)
  other arithmetic  16.5 us (3%)
  between operations  14.2 us (2%)
    all_to_all x1, starting transfers between devices, shards(): lax.all_to_all(pair_buffer, 'expert', split_axis=0, concat_axis=0, tiled=...  131 us
    unnamed x6, waiting for transfers between devices  88.5 us
    all_to_all x1, waiting for transfers between devices, shards(): lax.all_to_all(pair_buffer, 'expert', split_axis=0, concat_axis=0, tiled=...  80.4 us
    all_gather x1, waiting for transfers between devices, shards(): lax.all_gather(down_proj, 'dp', axis=2, tiled=True)  58.8 us
    all_gather x1, waiting for transfers between devices, shards(): lax.all_gather(up_proj, 'dp', axis=1, tiled=True)  51.7 us
    all_to_all x1, waiting for transfers between devices, shards(): lax.all_to_all(grads_send, 'expert', split_axis=0, concat_axis=0, tiled=T...  21.9 us
    all_gather x1, waiting for transfers between devices, shards(): gathered = lax.all_gather(packed, 'expert', axis=1, tiled=True)  21.7 us
    all_to_all x1, waiting for transfers between devices, shards(): lax.all_to_all(rows_send, 'expert', split_axis=0, concat_axis=0, tiled=True)  19.8 us
  transfers between devices with their start and end apart: 11, of which 9 were waited for; matrix products, arithmetic and copies ran while one was open for 10% of the time, Pallas kernels for 0%

commit v1 on v0

--- a/solution.py
+++ b/solution.py
@@ -175,6 +175,8 @@
         slot_rank[None, None, :] == jnp.arange(CAP)[None, :, None].astype(jnp.float32)
     )
     dispatch_mat = placed.reshape(devices * CAP, token_count).astype(jnp.bfloat16)
+    model_cols = model_width
+    pad_cols = 128
     rows_send = (
         jnp.dot(dispatch_mat, moe_input, preferred_element_type=jnp.float32)
         .astype(jnp.bfloat16)
@@ -188,19 +190,26 @@
     weights_send = jnp.sum(jnp.where(placed, token_weight[None, None, :], 0.0), axis=2).astype(
         jnp.bfloat16
     )
-    gate_full, up_full, down_full = (
-        lax.all_gather(gate_proj, "dp", axis=1, tiled=True),
-        lax.all_gather(up_proj, "dp", axis=1, tiled=True),
-        lax.all_gather(down_proj, "dp", axis=2, tiled=True),
-    )
-    gate_mat = gate_full[0]
-    up_mat = up_full[0]
-    down_mat = down_full[0]
-    rows_in, grads_in, weights_in = (
-        lax.all_to_all(rows_send, "expert", split_axis=0, concat_axis=0, tiled=True),
-        lax.all_to_all(grads_send, "expert", split_axis=0, concat_axis=0, tiled=True),
-        lax.all_to_all(weights_send, "expert", split_axis=0, concat_axis=0, tiled=True),
-    )
+    send_all = jnp.concatenate(
+        [
+            rows_send,
+            grads_send,
+            jnp.broadcast_to(weights_send[:, :, None], (devices, CAP, pad_cols)),
+        ],
+        axis=2,
+    )
+    hidden_cols = gate_proj.shape[2]
+    weight_cat = jnp.concatenate(
+        [gate_proj, up_proj, jnp.transpose(down_proj, (0, 2, 1))], axis=2
+    )
+    weight_full = lax.all_gather(weight_cat, "dp", axis=1, tiled=True)[0]
+    gate_mat = weight_full[:, :hidden_cols]
+    up_mat = weight_full[:, hidden_cols : 2 * hidden_cols]
+    down_mat = jnp.transpose(weight_full[:, 2 * hidden_cols :])
+    recv_all = lax.all_to_all(send_all, "expert", split_axis=0, concat_axis=0, tiled=True)
+    rows_in = recv_all[:, :, :model_cols]
+    grads_in = recv_all[:, :, model_cols : 2 * model_cols]
+    weights_in = recv_all[:, :, 2 * model_cols]
     flat_rows = rows_in.reshape(devices * CAP, model_width)
     flat_grads = grads_in.reshape(devices * CAP, model_width)
     gate_pre = jnp.dot(flat_rows, gate_mat, preferred_element_type=jnp.float32)
@@ -248,22 +257,24 @@
     gate_proj_grad = summed[:, :hidden_width][None]
     up_proj_grad = summed[:, hidden_width : 2 * hidden_width][None]
     down_proj_grad = jnp.transpose(summed[:, 2 * hidden_width :])[None]
-    pairs_back, input_back, weights_back = (
-        lax.all_to_all(pair_buffer, "expert", split_axis=0, concat_axis=0, tiled=True),
-        lax.all_to_all(
-            input_rows.reshape(devices, CAP, model_width),
-            "expert",
-            split_axis=0,
-            concat_axis=0,
-            tiled=True,
-        ),
-        lax.all_to_all(
-            weight_back.reshape(devices, CAP), "expert", split_axis=0, concat_axis=0, tiled=True
-        ),
-    )
-    pair_total = jnp.sum(pairs_back.astype(jnp.float32), axis=0).astype(jnp.bfloat16)
+    pair_total = lax.psum_scatter(pair_buffer, "expert", scatter_dimension=0, tiled=True)[0]
     key_grad = pair_total[:, :, :HEAD]
     value_grad = pair_total[:, :, HEAD:]
+    back_all = lax.all_to_all(
+        jnp.concatenate(
+            [
+                input_rows.reshape(devices, CAP, model_width),
+                jnp.broadcast_to(weight_back.reshape(devices, CAP, 1), (devices, CAP, pad_cols)),
+            ],
+            axis=2,
+        ),
+        "expert",
+        split_axis=0,
+        concat_axis=0,
+        tiled=True,
+    )
+    input_back = back_all[:, :, :model_width]
+    weights_back = back_all[:, :, model_width]
     input_grad = lax.dot_general(
         dispatch_mat,
         input_back.reshape(devices * CAP, model_width),

time: 634 us -> 432 us (0.68)
  waiting for transfers between devices: 365 us -> 145 us
  blocking collectives: 0 us -> 207 us
  starting transfers between devices: 177 us -> 0.16 us
    all_to_all x0 -> x2, blocking collectives: none -> 207 us  [the longest x1 156 us: shards(): lax.all_to_all(jnp.concatenate([input_rows.reshape(devices, CAP, model_wi...]
    all_to_all x6 -> x0, starting transfers between devices: 176 us -> none  [the longest x1 131 us: shards(): lax.all_to_all(pair_buffer, 'expert', split_axis=0, concat_axis=0, tiled=...]
    all_to_all x6 -> x0, waiting for transfers between devices: 145 us -> none  [the longest x1 80.4 us: shards(): lax.all_to_all(pair_buffer, 'expert', split_axis=0, concat_axis=0, tiled=...]
    all_gather x3 -> x1, waiting for transfers between devices: 111 us -> 14.7 us  [shards(): weight_full = lax.all_gather(weight_cat, 'dp', axis=1, tiled=True)[0]]
    unnamed x6 -> x5, waiting for transfers between devices: 88.5 us -> 0.07 us
    reduce_scatter x0 -> x1, waiting for transfers between devices: none -> 68.3 us  [shards(): lax.psum_scatter(pair_buffer, 'expert', scatter_dimension=0, tiled=True)[0]]
    all_gather x1, waiting for transfers between devices: 21.7 us -> 62.2 us  [shards(): gathered = lax.all_gather(packed, 'expert', axis=1, tiled=True)]
  transfers between devices with their start and end apart: 11 -> 4, of which waited for: 9 -> 3; matrix products, arithmetic and copies ran while one was open for 10% -> 13% of each run, Pallas kernels for 0% -> 0%
where the time goes in v1:
time: 432 us; the launch traced here: 428 us
  blocking collectives  207 us (48%)
  waiting for transfers between devices  145 us (34%)
  local copies, waits for them, and re-layouts  26.1 us (6%)
  matrix products  21 us (5%)
  between operations  14.1 us (3%)
  other arithmetic  12.9 us (3%)
    all_to_all x1, blocking collectives, shards(): lax.all_to_all(jnp.concatenate([input_rows.reshape(devices, CAP, model_wi...  156 us
    reduce_scatter x1, waiting for transfers between devices, shards(): lax.psum_scatter(pair_buffer, 'expert', scatter_dimension=0, tiled=True)[0]  68.3 us
    all_gather x1, waiting for transfers between devices, shards(): gathered = lax.all_gather(packed, 'expert', axis=1, tiled=True)  62.2 us
    all_to_all x1, blocking collectives, shards(): lax.all_to_all(send_all, 'expert', split_axis=0, concat_axis=0, tiled=True)  50.8 us
    all_gather x1, waiting for transfers between devices, shards(): weight_full = lax.all_gather(weight_cat, 'dp', axis=1, tiled=True)[0]  14.7 us
    unnamed x23, local copies, waits for them, and re-layouts  12.1 us
  transfers between devices with their start and end apart: 4, of which 3 were waited for; matrix products, arithmetic and copies ran while one was open for 13% of the time, Pallas kernels for 0%

profile of v1, /device:TPU:1, one launch (start us, length us, event | category | flops | bytes accessed | tf_op | source)
XLA Modules:
  0.0 428.3 jit_solution(17144311811786326233)
XLA Ops:
  7.2 1.0 copy.76
  8.2 1.0 copy.75
  9.2 1.5 pad_maximum_fusion.4
  10.8 1.5 pad_maximum_fusion.5
  12.4 0.7 fusion.72
  13.2 0.7 select_reduce_fusion.1
  14.2 0.2 convolution_convert_fusion.3
  14.4 0.2 reshape.279
  14.6 1.3 convolution_convert_fusion.4
  15.9 0.2 reshape.278
  16.1 0.7 select_reduce_fusion
  16.9 0.5 pad_maximum_fusion.2
  17.4 50.8 %all_to_all.10 = bf16[32,2,4224]{2,1,0:T(2,128)(2,1)S(1)} all-to-all(bf16[32,2,4224]{2,1,0:T(2,128)(2,1)S(1)} %pad_maximum_fusion.2), channel_id=1, replica_groups=mesh['dp'=16,'expert'=32] {'expert'}, dimensions={0} | all-to-all | bytes 1081344 | tf_op jit(solution)/shard_map/all_to_all | solution.py:209
  68.2 0.4 fusion.75
  68.5 0.4 reshape.285
  69.2 14.7 %all-gather.5.cloned.1.call-done = bf16[1,2048,768]{1,2,0:T(8,128)(2,1)} async-done(((bf16[1,128,768]{1,2,0:T(8,128)(2,1)}), bf16[1,2048,768]{1,2,0:T(8,128)(2,1)}) %all-gather.5.cloned.1.call-update) | async-done | bytes 3145744 | tf_op jit(solution)/shard_map/all_gather | solution.py:205
  83.9 1.7 fusion.41
  85.6 1.7 fusion.44
  87.3 1.7 multiply_convert_fusion.2
  89.0 0.5 convolution_convert_fusion.1
  89.4 0.5 convolution_convert_fusion.2
  89.9 0.5 convolution_convert_fusion
  90.4 1.8 pad_maximum_fusion.1
  92.2 4.7 %copy.90 = bf16[2048,768]{1,0:T(8,128)(2,1)} copy(bf16[2048,768]{0,1:T(8,128)(2,1)} %pad_maximum_fusion.1) | data formatting | bytes 6291456
  97.1 0.3 add_divide_fusion
  97.4 0.3 copy.97
  97.8 0.2 copy-done.5
  98.0 1.1 copy.96
  99.1 62.2 %all-gather.3.cloned.1.call-done = bf16[2,2048,512]{2,1,0:T(8,128)(2,1)} async-done(((bf16[2,64,512]{2,1,0:T(8,128)(2,1)}), bf16[2,2048,512]{2,1,0:T(8,128)(2,1)}) %all-gather.3.cloned.1.call-update) | async-done | bytes 4194320 | tf_op jit(solution)/shard_map/all_gather | solution.py:52
  161.3 2.4 while.46
  161.3 1.8 conditional.6
  161.4 1.3 fusion.74
  162.7 0.4 exponential_reduce_fusion
  163.8 2.2 while.47
  163.9 1.6 conditional.7
  164.0 1.4 fusion.3
  166.0 2.7 multiply_reduce_fusion
  169.0 2.5 broadcast_in_dim.128
  171.5 5.5 %while.48 = (s32[]{:T(128)}, f32[2,64,8,256]{3,1,2,0:T(8,128)S(1)}, bf16[32,2,64,512]{3,2,0,1:T(8,128)(2,1)}, s32[]{:T(128)}, s32[]{:T(128)}, /*index=5*/bf16[2,...) while((s32[]{:T(128)}, f32[2,64,8,256]{3,1,2,0:T(8,128)S(1)}, ...), condition=%wide.region_14.15_spmd, body=%wide.region_11.14_spmd.sunk | while | flops 337518784 | bytes 8284160 | solution.py:153
  171.5 5.1 %conditional.8 = ((f32[2,64,8,256]{3,1,2,0:T(8,128)S(1)}, bf16[32,2,64,512]{3,2,0,1:T(8,128)(2,1)})) conditional(s32[]{:T(128)} %convert_element_type.228, (f32[2,64,8,256]{3,1,2,0:T(8,128)S(1)}, bf16[32,2,64,512]{3,2,0,1:T(8,128)(2,1)}) %tuple.151, (s32[]{:T(128)}, s32[]{:T(128)}, bf16[2,2048,512]{2,1,0:T(8,128)(2,1)}, ...), branch_computations={%region_12.12_spmd, %region_13.13_spmd} | conditional | flops 337518784 | bytes 8283921 | solution.py:151
  171.6 1.2 fusion.24
  172.8 1.2 fusion.25
  174.1 1.2 fusion.17
  175.3 0.3 fusion.27
  175.6 0.3 fusion.26
  175.9 0.7 constant_dynamic-update-slice_fusion
  177.0 4.6 %copy.73 = bf16[32,2,64,512]{3,2,1,0:T(8,128)(2,1)} copy(bf16[32,2,64,512]{3,2,0,1:T(8,128)(2,1)} %get-tuple-element.680) | data formatting | bytes 8388608 | tf_op jit(solution)/shard_map/while | solution.py:153
  181.6 1.0 copy-done.2
  182.6 1.6 fusion.34
  184.4 1.6 fusion.39
  186.0 1.5 fusion.33
  187.5 0.2 reshape.281
  187.8 0.3 pad_maximum_fusion.3
  188.1 156.4 %all_to_all.11 = bf16[32,2,2176]{2,1,0:T(2,128)(2,1)S(1)} all-to-all(bf16[32,2,2176]{2,1,0:T(2,128)(2,1)S(1)} %pad_maximum_fusion.3), channel_id=1, replica_groups=mesh['dp'=16,'expert'=32] {'expert'}, dimensions={0} | all-to-all | bytes 557056 | tf_op jit(solution)/shard_map/all_to_all | solution.py:263
  345.0 0.6 select_convert_fusion
  345.6 1.1 fusion.32
  346.8 0.8 copy.95
  347.6 1.0 reshape.277
  348.7 1.1 copy.91
  349.8 0.7 slice_bitcast_fusion
  350.5 0.8 copy.81
  351.2 0.8 copy.82
  352.0 68.3 %reduce-scatter.5.cloned.1.call-done = bf16[1,2,64,512]{3,2,1,0:T(8,128)(2,1)} async-done(((bf16[32,2,64,512]{3,2,1,0:T(8,128)(2,1)}), bf16[1,2,64,512]{3,2,1,0:T(8,128)(2,1)}) %reduce-scatter.5.cloned.1.call-update) | async-done | bytes 131088 | tf_op jit(solution)/shard_map/reduce_scatter | solution.py:260
  420.3 1.5 fusion.76
  (107 shorter events, 2.9 us)
Async XLA Ops:
  7.2 7.0 %copy-start = (bf16[128,2048]{1,0:T(8,128)(2,1)S(1)}, bf16[128,2048]{1,0:T(8,128)(2,1)}, u32[]{:S(2)}) copy-start(bf16[128,2048]{1,0:T(8,128)(2,1)} %param.30) | copy-start | bytes 1572868
  7.2 76.7 %all-gather.5.cloned.1.call-start = ((), (), s32[]{:S(2)}) async-start(), calls=%async_computation.6 | async-start | bytes 3342336 | tf_op jit(solution)/shard_map/all_gather | solution.py:205
  10.8 150.5 %all-gather.3.cloned.1.call-start = ((), (), s32[]{:S(2)}) async-start(), calls=%async_computation.4 | async-start | bytes 4325376 | tf_op jit(solution)/shard_map/all_gather | solution.py:52
  12.4 336.3 %reduce-scatter.7.cloned.1.call-start = ((), (), s32[]{:S(2)}) async-start(), calls=%async_computation.7 | async-start | bytes 3342336
  68.9 21.5 %copy-start.1 = (f32[64,2048]{1,0:T(8,128)}, f32[64,2048]{1,0:T(8,128)S(1)}, u32[]{:S(2)}) copy-start(f32[64,2048]{1,0:T(8,128)S(1)} %reshape.285) | copy-start | bytes 1572868
  92.2 4.8 %copy-start.6 = (bf16[2,64,2048]{2,1,0:T(8,128)(2,1)S(1)}, bf16[2,64,2048]{2,1,0:T(8,128)(2,1)}, u32[]{:S(2)}) copy-start(bf16[2,64,2048]{2,1,0:T(8,128)(2,1)} %param.24) | copy-start | bytes 1572868
  92.2 4.9 %copy-start.4 = (bf16[2,64,2048]{2,1,0:T(8,128)(2,1)S(1)}, bf16[2,64,2048]{2,1,0:T(8,128)(2,1)}, u32[]{:S(2)}) copy-start(bf16[2,64,2048]{2,1,0:T(8,128)(2,1)} %param.27) | copy-start | bytes 1572868
  97.0 1.0 copy-start.5
  97.0 323.3 %reduce-scatter.5.cloned.1.call-start = ((), (), s32[]{:S(2)}) async-start(), calls=%async_computation.5 | async-start | bytes 4325376 | tf_op jit(solution)/shard_map/reduce_scatter | solution.py:260
  181.6 1.0 copy-start.2
  184.4 163.3 %copy-start.3 = (bf16[2,64,8,256]{3,2,1,0:T(8,128)(2,1)S(1)}, bf16[2,64,8,256]{3,2,1,0:T(8,128)(2,1)}, u32[]{:S(2)}) copy-start(bf16[2,64,8,256]{3,2,1,0:T(8,128)(2,1)} %get-tuple-element.843) | copy-start | bytes 1572868
Sparse Core Ops, SparseCore 0:
  11.6 72.2 all-gather.4
  86.6 74.5 all-gather.2
  165.5 86.1 reduce-scatter.6
  254.4 165.8 reduce-scatter.4

commit v2 on v1

--- a/solution.py
+++ b/solution.py
@@ -6,21 +6,6 @@
 HEADS = 8
 HEAD = 256
 CAP = 2
-
-
-def keep_state(run_state):
-    return run_state
-
-
-def block_scores(queries, keys_block, block_start, first_position, score_scale):
-    scores = (
-        jnp.einsum("sphd,srd->shpr", queries, keys_block, preferred_element_type=jnp.float32)
-        * score_scale
-    )
-    query_pos = first_position + jnp.arange(queries.shape[1])
-    key_pos = block_start + jnp.arange(keys_block.shape[1])
-    allowed = key_pos[None, :] <= query_pos[:, None]
-    return (scores, allowed[None, None])
 
 
 def shards(
@@ -43,64 +28,27 @@
     first_position = position * shard_len
     last_position = first_position + shard_len - 1
     total_len = shard_len * devices
-    block_len = min(total_len, max(shard_len, 128))
-    block_count = total_len // block_len
-    shards_per_block = block_len // shard_len
     score_scale = HEAD ** (-0.5)
     queries = query_rows.reshape(seq_count, shard_len, HEADS, HEAD)
     packed = jnp.concatenate([key_rows, value_rows], axis=2)
     gathered = lax.all_gather(packed, "expert", axis=1, tiled=True)
 
-    def take_block(block_index):
-        block_start = block_index * block_len
-        key_piece = lax.dynamic_slice_in_dim(gathered, block_start, block_len, 1)
-        return (block_start, key_piece[:, :, :HEAD], key_piece[:, :, HEAD:])
-
-    def max_step(block_index, loop_carry):
-        block_start, keys_block, values_block = take_block(block_index)
-
-        def max_update(run_state):
-            prior_max, prior_sum = run_state
-            scores, allowed = block_scores(
-                queries, keys_block, block_start, first_position, score_scale
-            )
-            masked = jnp.where(allowed, scores, -jnp.inf)
-            new_max = jnp.maximum(prior_max, jnp.max(masked, axis=3))
-            new_sum = prior_sum * jnp.exp(prior_max - new_max) + jnp.sum(
-                jnp.exp(masked - new_max[..., None]), axis=3
-            )
-            return (new_max, new_sum)
-
-        return lax.cond(block_start <= last_position, max_update, keep_state, loop_carry)
-
-    stat_shape = (seq_count, HEADS, shard_len)
-    run_max, run_sum = lax.fori_loop(
-        0,
-        block_count,
-        max_step,
-        (jnp.full(stat_shape, -jnp.inf, jnp.float32), jnp.zeros(stat_shape, jnp.float32)),
-    )
-    log_total = run_max + jnp.log(run_sum)
-
-    def context_step(block_index, loop_carry):
-        block_start, keys_block, values_block = take_block(block_index)
-
-        def context_update(running_total):
-            scores, allowed = block_scores(
-                queries, keys_block, block_start, first_position, score_scale
-            )
-            exact_probs = jnp.where(allowed, jnp.exp(scores - log_total[..., None]), 0.0)
-            return running_total + jnp.einsum(
-                "shpr,srd->sphd",
-                exact_probs.astype(jnp.bfloat16),
-                values_block,
-                preferred_element_type=jnp.float32,
-            )
-
-        return lax.cond(block_start <= last_position, context_update, keep_state, loop_carry)
-
-    context = lax.fori_loop(
-        0, block_count, context_step, jnp.zeros((seq_count, shard_len, HEADS, HEAD), jnp.float32)
+    keys_all = gathered[:, :, :HEAD]
+    values_all = gathered[:, :, HEAD:]
+    scores = (
+        jnp.einsum("sphd,srd->shpr", queries, keys_all, preferred_element_type=jnp.float32)
+        * score_scale
+    )
+    query_pos = first_position + jnp.arange(shard_len)
+    key_pos = jnp.arange(total_len)
+    allowed = (key_pos[None, :] <= query_pos[:, None])[None, None]
+    masked = jnp.where(allowed, scores, -jnp.inf)
+    row_max = jnp.max(masked, axis=3, keepdims=True)
+    log_total = row_max + jnp.log(jnp.sum(jnp.exp(masked - row_max), axis=3, keepdims=True))
+    exact_probs = jnp.where(allowed, jnp.exp(scores - log_total), 0.0)
+    probs_low = exact_probs.astype(jnp.bfloat16)
+    context = jnp.einsum(
+        "shpr,srd->sphd", probs_low, values_all, preferred_element_type=jnp.float32
     )
     sigmoid_gate = jax.nn.sigmoid(gate_logits.astype(jnp.float32)).reshape(
         seq_count, shard_len, HEADS, HEAD
@@ -113,51 +61,29 @@
         .reshape(seq_count, shard_len, row_width)
     )
     grad_dot = jnp.transpose(jnp.sum(context_grad.astype(jnp.float32) * context, axis=3), (0, 2, 1))
-
-    def grad_step(block_index, loop_carry):
-        block_start, keys_block, values_block = take_block(block_index)
-
-        def grad_update(run_state):
-            query_total, pair_buffer = run_state
-            scores, allowed = block_scores(
-                queries, keys_block, block_start, first_position, score_scale
-            )
-            exact_probs = jnp.where(allowed, jnp.exp(scores - log_total[..., None]), 0.0)
-            probs_low = exact_probs.astype(jnp.bfloat16)
-            prob_grad = jnp.einsum(
-                "sphd,srd->shpr", context_grad, values_block, preferred_element_type=jnp.float32
-            )
-            score_grad = (exact_probs * (prob_grad - grad_dot[..., None]) * score_scale).astype(
-                jnp.bfloat16
-            )
-            query_total = query_total + jnp.einsum(
-                "shpr,srd->sphd", score_grad, keys_block, preferred_element_type=jnp.float32
-            )
-            key_part = jnp.einsum(
-                "shpr,sphd->srd", score_grad, queries, preferred_element_type=jnp.float32
-            ).astype(jnp.bfloat16)
-            value_part = jnp.einsum(
-                "shpr,sphd->srd", probs_low, context_grad, preferred_element_type=jnp.float32
-            ).astype(jnp.bfloat16)
-            pair_block = jnp.concatenate([key_part, value_part], axis=2)
-            pair_block = jnp.moveaxis(
-                pair_block.reshape(seq_count, shards_per_block, shard_len, 2 * HEAD), 1, 0
-            )
-            pair_buffer = lax.dynamic_update_slice_in_dim(
-                pair_buffer, pair_block, block_start // shard_len, 0
-            )
-            return (query_total, pair_buffer)
-
-        return lax.cond(block_start <= last_position, grad_update, keep_state, loop_carry)
-
-    query_total, pair_buffer = lax.fori_loop(
-        0,
-        block_count,
-        grad_step,
-        (
-            jnp.zeros((seq_count, shard_len, HEADS, HEAD), jnp.float32),
-            jnp.zeros((devices, seq_count, shard_len, 2 * HEAD), jnp.bfloat16),
-        ),
+    prob_grad = jnp.einsum(
+        "sphd,srd->shpr", context_grad, values_all, preferred_element_type=jnp.float32
+    )
+    score_grad = (exact_probs * (prob_grad - grad_dot[..., None]) * score_scale).astype(
+        jnp.bfloat16
+    )
+    query_total = jnp.einsum(
+        "shpr,srd->sphd", score_grad, keys_all, preferred_element_type=jnp.float32
+    )
+    key_part = jnp.einsum(
+        "shpr,sphd->srd", score_grad, queries, preferred_element_type=jnp.float32
+    ).astype(jnp.bfloat16)
+    value_part = jnp.einsum(
+        "shpr,sphd->srd", probs_low, context_grad, preferred_element_type=jnp.float32
+    ).astype(jnp.bfloat16)
+    pair_buffer = lax.optimization_barrier(
+        jnp.moveaxis(
+            jnp.concatenate([key_part, value_part], axis=2).reshape(
+                seq_count, devices, shard_len, 2 * HEAD
+            ),
+            1,
+            0,
+        )
     )
     query_grad = query_total.astype(jnp.bfloat16).reshape(seq_count, shard_len, row_width)
     token_count, model_width = moe_input.shape

time: 432 us -> 510 us (1.18)
  waiting for transfers between devices: 145 us -> 392 us
  blocking collectives: 207 us -> 0 us
  starting transfers between devices: 0.16 us -> 31 us
  matrix products: 21 us -> 29.9 us
    unnamed x5 -> x6, waiting for transfers between devices: 0.07 us -> 259 us
    all_to_all x2 -> x0, blocking collectives: 207 us -> none  [the longest x1 156 us: shards(): lax.all_to_all(jnp.concatenate([input_rows.reshape(devices, CAP, model_wi...]
    reduce_scatter x1 -> x0, waiting for transfers between devices: 68.3 us -> none  [shards(): lax.psum_scatter(pair_buffer, 'expert', scatter_dimension=0, tiled=True)[0]]
    all_to_all x0 -> x2, starting transfers between devices: none -> 30.6 us  [the longest x1 16.8 us: shards(): lax.all_to_all(send_all, 'expert', split_axis=0, concat_axis=0, tiled=True)]
    all_gather x1, waiting for transfers between devices: 14.7 us -> 42 us  [shards(): weight_full = lax.all_gather(weight_cat, 'dp', axis=1, tiled=True)[0]]
    all_to_all x0 -> x2, waiting for transfers between devices: none -> 22.9 us  [the longest x1 22.9 us: shards(): lax.all_to_all(jnp.concatenate([input_rows.reshape(devices, CAP, model_wi...]
    dot_general x7 -> x6, matrix products: 6.98 us -> 16 us  [the longest x1 4.09 us: shards(): jnp.einsum('shpr,srd->sphd', score_grad, keys_all, preferred_element_type...]
    concatenate x0 -> x1, local copies, waits for them, and re-layouts: none -> 6.31 us  [shards(): jnp.concatenate([key_part, value_part], axis=2)]
  transfers between devices with their start and end apart: 4 -> 6, of which waited for: 3 -> 5; matrix products, arithmetic and copies ran while one was open for 13% -> 13% of each run, Pallas kernels for 0% -> 0%
where the time goes in v2:
time: 510 us; the launch traced here: 508 us
  waiting for transfers between devices  392 us (77%)
  starting transfers between devices  31 us (6%)
  matrix products  29.9 us (6%)
  local copies, waits for them, and re-layouts  23.4 us (5%)
  other arithmetic  17.9 us (4%)
  between operations  14.1 us (3%)
    unnamed x6, waiting for transfers between devices  259 us
    all_gather x1, waiting for transfers between devices, shards(): gathered = lax.all_gather(packed, 'expert', axis=1, tiled=True)  67.6 us
    all_gather x1, waiting for transfers between devices, shards(): weight_full = lax.all_gather(weight_cat, 'dp', axis=1, tiled=True)[0]  42 us
    all_to_all x1, waiting for transfers between devices, shards(): lax.all_to_all(jnp.concatenate([input_rows.reshape(devices, CAP, model_wi...  22.9 us
    all_to_all x1, starting transfers between devices, shards(): lax.all_to_all(send_all, 'expert', split_axis=0, concat_axis=0, tiled=True)  16.8 us
    all_to_all x1, starting transfers between devices, shards(): lax.all_to_all(jnp.concatenate([input_rows.reshape(devices, CAP, model_wi...  13.9 us
    unnamed x20, local copies, waits for them, and re-layouts  10.8 us
  transfers between devices with their start and end apart: 6, of which 5 were waited for; matrix products, arithmetic and copies ran while one was open for 13% of the time, Pallas kernels for 0%

profile of v2, /device:TPU:1, one launch (start us, length us, event | category | flops | bytes accessed | tf_op | source)
XLA Modules:
  0.0 508.2 jit_solution(316245542062219788)
XLA Ops:
  7.2 1.6 pad_maximum_fusion.5
  8.9 1.0 copy.80
  9.9 1.0 copy.79
  10.9 1.5 pad_maximum_fusion.4
  12.4 0.7 fusion.64
  13.1 0.7 select_reduce_fusion.1
  13.9 0.2 fusion.16
  14.0 0.7 select_reduce_fusion
  14.9 0.1 fusion.40
  15.0 0.2 convolution_convert_fusion.3
  15.2 0.2 reshape.200
  15.4 1.3 convolution_convert_fusion.4
  16.7 0.2 reshape.199
  16.9 1.3 pad_maximum_fusion.2
  18.2 16.8 %all-to-all-start = ((bf16[32,2,4224]{2,1,0:T(2,128)(2,1)}), bf16[32,2,4224]{2,1,0:T(2,128)(2,1)S(1)}, u32[]{:S(2)}, u32[]{:S(2)}) async-start(bf16[32,2,4224]{2,1,0:T(2,128)(2,1)} %pad_maximum_fusion.2), calls=%async_computation | async-start | bytes 1081344 | tf_op jit(solution)/shard_map/all_to_all | solution.py:135
  35.1 0.1 iota_compare_fusion
  35.3 2.3 add_divide_fusion
  37.6 67.6 %all-gather.3.cloned.1.call-done = bf16[2,2048,512]{2,1,0:T(8,128)(2,1)} async-done(((bf16[2,64,512]{2,1,0:T(8,128)(2,1)}), bf16[2,2048,512]{2,1,0:T(8,128)(2,1)}) %all-gather.3.cloned.1.call-update) | async-done | bytes 4194320 | tf_op jit(solution)/shard_map/all_gather | solution.py:34
  105.1 3.1 fusion.5
  108.3 2.2 exponential_reduce_fusion
  110.5 0.3 copy-done.5
  110.8 2.1 multiply_reduce_fusion
  112.9 3.2 fusion.2
  116.1 1.3 bitcast_convert_fusion.1
  117.4 2.2 bitcast_convert_fusion
  119.6 2.3 pad_maximum_fusion
  121.9 6.3 %copy.74 = bf16[2,2048,512]{2,1,0:T(8,128)(2,1)} copy(bf16[2,2048,512]{1,2,0:T(8,128)(2,1)} %pad_maximum_fusion) | data formatting | bytes 8388608 | tf_op jit(solution)/shard_map/concatenate | solution.py:81
  128.2 0.2 reduce-scatter.7.cloned.1.call-start
  128.4 0.4 fusion.66
  128.8 0.4 reshape.206
  129.4 0.1 reshape.205
  129.5 42.0 %all-gather.5.cloned.1.call-done = bf16[1,2048,768]{1,2,0:T(8,128)(2,1)} async-done(((bf16[1,128,768]{1,2,0:T(8,128)(2,1)}), bf16[1,2048,768]{1,2,0:T(8,128)(2,1)}) %all-gather.5.cloned.1.call-update) | async-done | bytes 3145744 | tf_op jit(solution)/shard_map/all_gather | solution.py:131
  171.5 1.7 fusion.22
  173.2 1.7 fusion.25
  174.8 1.7 multiply_convert_fusion.2
  176.5 0.5 convolution_convert_fusion.1
  177.0 0.5 convolution_convert_fusion.2
  177.5 0.5 convolution_convert_fusion
  178.0 1.8 pad_maximum_fusion.1
  179.8 4.7 copy.93
  184.5 1.6 fusion.15
  186.2 0.1 convert_element_type.153
  186.3 1.5 fusion.20
  187.8 1.5 fusion.8
  189.4 0.2 reshape.202
  189.6 1.0 pad_maximum_fusion.3
  190.6 13.9 %all-to-all-start.1 = ((bf16[32,2,2176]{2,1,0:T(2,128)(2,1)}), bf16[32,2,2176]{2,1,0:T(2,128)(2,1)S(1)}, u32[]{:S(2)}, u32[]{:S(2)}) async-start(bf16[32,2,2176]{2,1,0:T(2,128)(2,1)} %pad_maximum_fusion.3), calls=%async_computation.1 | async-start | bytes 557056 | tf_op jit(solution)/shard_map/all_to_all | solution.py:189
  204.5 1.3 dynamic-slice
  205.8 22.9 %all-to-all-done.1 = bf16[32,2,2176]{2,1,0:T(2,128)(2,1)S(1)} async-done(((bf16[32,2,2176]{2,1,0:T(2,128)(2,1)}), bf16[32,2,2176]{2,1,0:T(2,128)(2,1)S(1)}, u32[]{:S(2)}, u32[]{:S(2)}) %all-to-all-start.1) | async-done | bytes 278560 | tf_op jit(solution)/shard_map/all_to_all | solution.py:189
  228.9 0.2 slice.70
  229.1 0.1 multiply_reduce_fusion.1
  229.2 0.6 select_convert_fusion
  229.8 1.1 fusion.7
  230.9 4.1 fusion.14
  235.0 0.8 copy.100
  235.9 0.8 copy.101
  236.7 168.4 %all-reduce.3.cloned.1.call-done = bf16[32,2,64,512]{3,2,0,1:T(8,128)(2,1)} async-done(((bf16[32,2,64,512]{3,2,0,1:T(8,128)(2,1)}), bf16[32,2,64,512]{3,2,0,1:T(8,128)(2,1)}) %all-reduce.3.cloned.1.call-update) | async-done | bytes 4194320
  405.1 1.6 dynamic-slice_bitcast_fusion
  406.7 0.7 fusion.67
  407.3 91.0 %reduce-scatter.7.cloned.1.call-done = bf16[128,768]{1,0:T(8,128)(2,1)} async-done(((bf16[2048,768]{1,0:T(8,128)(2,1)}), bf16[128,768]{1,0:T(8,128)(2,1)}) %reduce-scatter.7.cloned.1.call-update) | async-done | bytes 196624
  498.3 1.1 copy.94
  499.5 0.7 slice_bitcast_fusion.12
  500.1 0.8 copy.85
  500.9 0.8 copy.86
  (35 shorter events, 1.0 us)
Async XLA Ops:
  7.2 7.8 %copy-start = (bf16[128,2048]{1,0:T(8,128)(2,1)S(1)}, bf16[128,2048]{1,0:T(8,128)(2,1)}, u32[]{:S(2)}) copy-start(bf16[128,2048]{1,0:T(8,128)(2,1)} %param.18) | copy-start | bytes 1572868
  7.2 27.8 %copy-start.3 = (bf16[2,64,2048]{2,1,0:T(8,128)(2,1)S(1)}, bf16[2,64,2048]{2,1,0:T(8,128)(2,1)}, u32[]{:S(2)}) copy-start(bf16[2,64,2048]{2,1,0:T(8,128)(2,1)} %param.16) | copy-start | bytes 1572868
  7.2 97.9 %all-gather.3.cloned.1.call-start = ((), (), s32[]{:S(2)}) async-start(), calls=%async_computation.3 | async-start | bytes 4325376 | tf_op jit(solution)/shard_map/all_gather | solution.py:34
  8.9 162.6 %all-gather.5.cloned.1.call-start = ((), (), s32[]{:S(2)}) async-start(), calls=%async_computation.4 | async-start | bytes 3342336 | tf_op jit(solution)/shard_map/all_gather | solution.py:131
  18.2 110.3 %all-to-all-start = ((bf16[32,2,4224]{2,1,0:T(2,128)(2,1)}), bf16[32,2,4224]{2,1,0:T(2,128)(2,1)S(1)}, u32[]{:S(2)}, u32[]{:S(2)}) async-start(bf16[32,2,4224]{2,1,0:T(2,128)(2,1)} %pad_maximum_fusion.2), calls=%async_computation | async-start | bytes 1081344 | tf_op jit(solution)/shard_map/all_to_all | solution.py:135
  34.9 370.2 %all-reduce.3.cloned.1.call-start = ((), (), s32[]{:S(2)}) async-start(), calls=%async_computation.6 | async-start | bytes 8388608
  108.3 2.3 copy-start.2
  108.3 2.5 copy-start.5
  112.9 3.2 copy-start.4
  116.1 3.5 copy-start.1
  128.2 370.1 %reduce-scatter.7.cloned.1.call-start = ((), (), s32[]{:S(2)}) async-start(), calls=%async_computation.5 | async-start | bytes 3342336
  190.6 38.0 %all-to-all-start.1 = ((bf16[32,2,2176]{2,1,0:T(2,128)(2,1)}), bf16[32,2,2176]{2,1,0:T(2,128)(2,1)S(1)}, u32[]{:S(2)}, u32[]{:S(2)}) async-start(bf16[32,2,2176]{2,1,0:T(2,128)(2,1)} %pad_maximum_fusion.3), calls=%async_computation.1 | async-start | bytes 557056 | tf_op jit(solution)/shard_map/all_to_all | solution.py:189
Sparse Core Ops, SparseCore 0:
  10.8 94.3 all-gather.2
  108.7 62.7 all-gather.4
  173.9 231.2 all-reduce.2
  409.2 89.1 reduce-scatter.6

commit v3 on v2

--- a/solution.py
+++ b/solution.py
@@ -1,11 +1,75 @@
 import jax
 import jax.numpy as jnp
 from jax import lax
+from jax.experimental import pallas as pl
+from jax.experimental.pallas import tpu as pltpu
 from jax.sharding import PartitionSpec as P
 
 HEADS = 8
 HEAD = 256
 CAP = 2
+
+
+def pair_return_kernel(parts_ref, out_ref, landing, send_sems, recv_sems):
+    devices = parts_ref.shape[0]
+    me = lax.axis_index("expert")
+    row = lax.axis_index("dp")
+    mesh_ids = pl.DeviceIdType.MESH
+
+    def peer_copy(block, slot, peer):
+        return pltpu.make_async_remote_copy(
+            src_ref=parts_ref.at[block],
+            dst_ref=landing.at[slot],
+            send_sem=send_sems.at[block],
+            recv_sem=recv_sems.at[slot],
+            device_id=(row, peer),
+            device_id_type=mesh_ids,
+        )
+
+    barrier = pltpu.get_barrier_semaphore()
+
+    def greet(step, carry):
+        peer = lax.rem(me + 1 + step, devices)
+        pl.semaphore_signal(barrier, inc=1, device_id=(row, peer), device_id_type=mesh_ids)
+        return carry
+
+    lax.fori_loop(0, devices - 1, greet, 0)
+    pl.semaphore_wait(barrier, devices - 1)
+
+    def send(block, carry):
+        peer_copy(block, me, block).start()
+        return carry
+
+    lax.fori_loop(0, me, send, 0)
+
+    def receive(source, total):
+        peer_copy(source, source, source).wait_recv()
+        return total + landing[source].astype(jnp.float32)
+
+    total = lax.fori_loop(me + 1, devices, receive, parts_ref[me].astype(jnp.float32))
+    out_ref[...] = total.astype(out_ref.dtype)
+
+    def finish(block, carry):
+        peer_copy(block, me, block).wait_send()
+        return carry
+
+    lax.fori_loop(0, me, finish, 0)
+
+
+def pair_return(pair_buffer):
+    devices = pair_buffer.shape[0]
+    return pl.pallas_call(
+        pair_return_kernel,
+        out_shape=jax.ShapeDtypeStruct(pair_buffer.shape[1:], pair_buffer.dtype),
+        in_specs=[pl.BlockSpec(memory_space=pltpu.VMEM)],
+        out_specs=pl.BlockSpec(memory_space=pltpu.VMEM),
+        scratch_shapes=[
+            pltpu.VMEM(pair_buffer.shape, pair_buffer.dtype),
+            pltpu.SemaphoreType.DMA((devices,)),
+            pltpu.SemaphoreType.DMA((devices,)),
+        ],
+        compiler_params=pltpu.CompilerParams(collective_id=0, has_side_effects=True),
+    )(pair_buffer)
 
 
 def shards(
@@ -76,7 +140,7 @@
     value_part = jnp.einsum(
         "shpr,sphd->srd", probs_low, context_grad, preferred_element_type=jnp.float32
     ).astype(jnp.bfloat16)
-    pair_buffer = lax.optimization_barrier(
+    pair_buffer = (
         jnp.moveaxis(
             jnp.concatenate([key_part, value_part], axis=2).reshape(
                 seq_count, devices, shard_len, 2 * HEAD
@@ -183,7 +247,7 @@
     gate_proj_grad = summed[:, :hidden_width][None]
     up_proj_grad = summed[:, hidden_width : 2 * hidden_width][None]
     down_proj_grad = jnp.transpose(summed[:, 2 * hidden_width :])[None]
-    pair_total = lax.psum_scatter(pair_buffer, "expert", scatter_dimension=0, tiled=True)[0]
+    pair_total = pair_return(pair_buffer)
     key_grad = pair_total[:, :, :HEAD]
     value_grad = pair_total[:, :, HEAD:]
     back_all = lax.all_to_all(

time: 510 us -> 402 us (0.79)
  the two profiles are of different devices: /device:TPU:1 before, /device:TPU:199 now
where the time goes in v3:
time: 402 us; the launch traced here: 401 us
  Pallas kernels  196 us (49%)
  waiting for transfers between devices  93.3 us (23%)
  starting transfers between devices  27.2 us (7%)
  matrix products  27 us (7%)
  local copies, waits for them, and re-layouts  26.2 us (7%)
  other arithmetic  16.8 us (4%)
  between operations  14.1 us (4%)
    pallas_call x1, Pallas kernels, pair_return(): pl.pallas_call(pair_return_kernel, out_shape=jax.ShapeDtypeStruct(pair_bu...  196 us
    all_gather x1, waiting for transfers between devices, shards(): gathered = lax.all_gather(packed, 'expert', axis=1, tiled=True)  36.4 us
    all_to_all x1, waiting for transfers between devices, shards(): lax.all_to_all(send_all, 'expert', split_axis=0, concat_axis=0, tiled=True)  26.3 us
    all_gather x1, waiting for transfers between devices, shards(): weight_full = lax.all_gather(weight_cat, 'dp', axis=1, tiled=True)[0]  20.3 us
    all_to_all x1, starting transfers between devices, shards(): lax.all_to_all(jnp.concatenate([input_rows.reshape(devices, CAP, model_wi...  13.5 us
    all_to_all x1, starting transfers between devices, shards(): lax.all_to_all(send_all, 'expert', split_axis=0, concat_axis=0, tiled=True)  13.4 us
    all_to_all x1, waiting for transfers between devices, shards(): lax.all_to_all(jnp.concatenate([input_rows.reshape(devices, CAP, model_wi...  10.3 us
    unnamed x19, local copies, waits for them, and re-layouts  9.72 us
  transfers between devices with their start and end apart: 5, of which 4 were waited for; matrix products, arithmetic and copies ran while one was open for 16% of the time, Pallas kernels for 49%

profile of v3, /device:TPU:199, one launch (start us, length us, event | category | flops | bytes accessed | tf_op | source)
XLA Modules:
  0.0 400.9 jit_solution(9191527763411678806)
XLA Ops:
  7.2 1.0 copy.82
  8.3 1.0 copy.81
  9.2 1.5 pad_maximum_fusion.4
  10.8 1.5 pad_maximum_fusion.5
  12.4 0.7 fusion.64
  13.1 0.7 select_reduce_fusion.1
  13.9 0.2 fusion.16
  14.2 0.2 convolution_convert_fusion.3
  14.4 0.2 reshape.200
  14.6 1.3 convolution_convert_fusion.4
  15.9 0.2 reshape.199
  16.1 0.7 select_reduce_fusion
  16.8 0.1 fusion.40
  16.9 1.3 pad_maximum_fusion.2
  18.2 13.4 %all-to-all-start = ((bf16[32,2,4224]{2,1,0:T(2,128)(2,1)}), bf16[32,2,4224]{2,1,0:T(2,128)(2,1)S(1)}, u32[]{:S(2)}, u32[]{:S(2)}) async-start(bf16[32,2,4224]{2,1,0:T(2,128)(2,1)} %pad_maximum_fusion.2), calls=%async_computation | async-start | bytes 1081344 | tf_op jit(solution)/shard_map/all_to_all | solution.py:199
  31.7 1.3 add_divide_fusion
  32.9 26.3 %all-to-all-done = bf16[32,2,4224]{2,1,0:T(2,128)(2,1)S(1)} async-done(((bf16[32,2,4224]{2,1,0:T(2,128)(2,1)}), bf16[32,2,4224]{2,1,0:T(2,128)(2,1)S(1)}, u32[]{:S(2)}, u32[]{:S(2)}) %all-to-all-start) | async-done | bytes 540704 | tf_op jit(solution)/shard_map/all_to_all | solution.py:199
  59.2 0.4 fusion.66
  59.6 0.4 reshape.206
  60.0 0.1 convert_reduce_fusion
  60.1 0.1 reshape.205
  60.3 20.3 %all-gather.5.cloned.1.call-done = bf16[1,2048,768]{1,2,0:T(8,128)(2,1)} async-done(((bf16[1,128,768]{1,2,0:T(8,128)(2,1)}), bf16[1,2048,768]{1,2,0:T(8,128)(2,1)}) %all-gather.5.cloned.1.call-update) | async-done | bytes 3145744 | tf_op jit(solution)/shard_map/all_gather | solution.py:195
  80.6 1.7 fusion.22
  82.2 1.7 fusion.25
  83.9 1.7 multiply_convert_fusion.2
  85.6 1.6 fusion.15
  87.2 0.1 convert_element_type.153
  87.4 1.5 fusion.20
  88.9 1.5 fusion.8
  90.4 0.2 reshape.202
  90.7 1.0 pad_maximum_fusion.3
  91.7 13.5 %all-to-all-start.1 = ((bf16[32,2,2176]{2,1,0:T(2,128)(2,1)}), bf16[32,2,2176]{2,1,0:T(2,128)(2,1)S(1)}, u32[]{:S(2)}, u32[]{:S(2)}) async-start(bf16[32,2,2176]{2,1,0:T(2,128)(2,1)} %pad_maximum_fusion.3), calls=%async_computation.1 | async-start | bytes 557056 | tf_op jit(solution)/shard_map/all_to_all | solution.py:253
  105.2 0.2 reduce-scatter.4.cloned.1.call-start
  105.4 0.5 convolution_convert_fusion.1
  105.9 0.5 convolution_convert_fusion.2
  106.4 0.5 convolution_convert_fusion
  106.9 1.8 pad_maximum_fusion.1
  108.7 4.8 %copy.93 = bf16[2048,768]{1,0:T(8,128)(2,1)} copy(bf16[2048,768]{0,1:T(8,128)(2,1)} %pad_maximum_fusion.1) | data formatting | bytes 6291456
  113.5 0.1 iota_compare_fusion
  113.8 10.3 %all-to-all-done.1 = bf16[32,2,2176]{2,1,0:T(2,128)(2,1)S(1)} async-done(((bf16[32,2,2176]{2,1,0:T(2,128)(2,1)}), bf16[32,2,2176]{2,1,0:T(2,128)(2,1)S(1)}, u32[]{:S(2)}, u32[]{:S(2)}) %all-to-all-start.1) | async-done | bytes 278560 | tf_op jit(solution)/shard_map/all_to_all | solution.py:253
  124.3 0.2 slice.68
  124.5 0.1 multiply_reduce_fusion.1
  124.6 0.6 select_convert_fusion
  125.2 1.1 fusion.7
  126.4 36.4 %all-gather.3.cloned.1.call-done = bf16[2,2048,512]{2,1,0:T(8,128)(2,1)} async-done(((bf16[2,64,512]{2,1,0:T(8,128)(2,1)}), bf16[2,2048,512]{2,1,0:T(8,128)(2,1)}) %all-gather.3.cloned.1.call-update) | async-done | bytes 4194320 | tf_op jit(solution)/shard_map/all_gather | solution.py:98
  162.7 3.1 fusion.5
  165.8 2.2 exponential_reduce_fusion
  168.1 0.3 copy-done.5
  168.3 2.1 multiply_reduce_fusion
  170.4 3.2 fusion.2
  173.6 1.2 fusion.14
  174.8 0.8 copy.100
  175.7 1.3 bitcast_convert_fusion.1
  177.0 2.2 bitcast_convert_fusion
  179.2 2.3 pad_maximum_fusion
  181.5 6.2 %copy.75 = bf16[2,2048,512]{2,1,0:T(8,128)(2,1)} copy(bf16[2,2048,512]{1,2,0:T(8,128)(2,1)} %pad_maximum_fusion) | data formatting | bytes 8388608 | tf_op jit(solution)/shard_map/concatenate | solution.py:145
  187.7 4.7 %copy.127 = bf16[2,32,64,512]{3,2,0,1:T(8,128)(2,1)} copy(bf16[2,32,64,512]{3,2,1,0:T(8,128)(2,1)} %bitcast.140) | data formatting | bytes 8388608 | tf_op jit(solution)/shard_map/reshape | solution.py:145
  192.4 196.3 %shard_map.187 = bf16[2,64,512]{2,1,0:T(8,128)(2,1)} custom-call(bf16[32,2,64,512]{3,2,1,0:T(8,128)(2,1)} %bitcast.141), custom_call_target="tpu_custom_call" | custom-call | tf_op jit(solution)/shard_map/pallas_call | solution.py:61
  388.7 0.8 copy.101
  389.5 1.5 fusion.67
  391.0 1.1 copy.94
  392.2 0.7 slice_bitcast_fusion.12
  392.9 0.8 copy.87
  393.6 0.8 copy.88
  (32 shorter events, 0.8 us)
Async XLA Ops:
  7.2 7.0 %copy-start = (bf16[128,2048]{1,0:T(8,128)(2,1)S(1)}, bf16[128,2048]{1,0:T(8,128)(2,1)}, u32[]{:S(2)}) copy-start(bf16[128,2048]{1,0:T(8,128)(2,1)} %param.18) | copy-start | bytes 1572868
  7.2 24.5 %copy-start.2 = (bf16[2,64,2048]{2,1,0:T(8,128)(2,1)S(1)}, bf16[2,64,2048]{2,1,0:T(8,128)(2,1)}, u32[]{:S(2)}) copy-start(bf16[2,64,2048]{2,1,0:T(8,128)(2,1)} %param.15) | copy-start | bytes 1572868
  7.2 73.4 %all-gather.5.cloned.1.call-start = ((), (), s32[]{:S(2)}) async-start(), calls=%async_computation.4 | async-start | bytes 3342336 | tf_op jit(solution)/shard_map/all_gather | solution.py:195
  10.8 151.9 %all-gather.3.cloned.1.call-start = ((), (), s32[]{:S(2)}) async-start(), calls=%async_computation.3 | async-start | bytes 4325376 | tf_op jit(solution)/shard_map/all_gather | solution.py:98
  18.2 40.9 %all-to-all-start = ((bf16[32,2,4224]{2,1,0:T(2,128)(2,1)}), bf16[32,2,4224]{2,1,0:T(2,128)(2,1)S(1)}, u32[]{:S(2)}, u32[]{:S(2)}) async-start(bf16[32,2,4224]{2,1,0:T(2,128)(2,1)} %pad_maximum_fusion.2), calls=%async_computation | async-start | bytes 1081344 | tf_op jit(solution)/shard_map/all_to_all | solution.py:199
  91.7 32.4 %all-to-all-start.1 = ((bf16[32,2,2176]{2,1,0:T(2,128)(2,1)}), bf16[32,2,2176]{2,1,0:T(2,128)(2,1)S(1)}, u32[]{:S(2)}, u32[]{:S(2)}) async-start(bf16[32,2,2176]{2,1,0:T(2,128)(2,1)} %pad_maximum_fusion.3), calls=%async_computation.1 | async-start | bytes 557056 | tf_op jit(solution)/shard_map/all_to_all | solution.py:253
  105.2 285.8 %reduce-scatter.4.cloned.1.call-start = ((), (), s32[]{:S(2)}) async-start(), calls=%async_computation.5 | async-start | bytes 3342336
  108.7 4.9 %copy-start.3 = (bf16[2,64,2048]{2,1,0:T(8,128)(2,1)S(1)}, bf16[2,64,2048]{2,1,0:T(8,128)(2,1)}, u32[]{:S(2)}) copy-start(bf16[2,64,2048]{2,1,0:T(8,128)(2,1)} %param.16) | copy-start | bytes 1572868
  113.5 49.2 %copy-start.4 = (bf16[2,64,2048]{2,1,0:T(8,128)(2,1)S(1)}, bf16[2,64,2048]{2,1,0:T(8,128)(2,1)}, u32[]{:S(2)}) copy-start(bf16[2,64,2048]{2,1,0:T(8,128)(2,1)} %param.12) | copy-start | bytes 1572868
  165.8 2.3 copy-start.1
  165.8 2.5 copy-start.5
Sparse Core Ops, SparseCore 0:
  11.6 68.9 all-gather.4
  83.3 79.3 all-gather.2
  166.9 87.9 reduce-scatter.3

commit v4 on v2

--- a/solution.py
+++ b/solution.py
@@ -1,11 +1,98 @@
 import jax
 import jax.numpy as jnp
 from jax import lax
+from jax.experimental import pallas as pl
+from jax.experimental.pallas import tpu as pltpu
 from jax.sharding import PartitionSpec as P
 
 HEADS = 8
 HEAD = 256
 CAP = 2
+CHAIN_DTYPE = jnp.float32
+
+
+def pair_chain_kernel(parts_ref, out_ref, sendbuf, recvbuf, send_sems, recv_sems):
+    devices, seqs = parts_ref.shape[0], parts_ref.shape[1]
+    me = lax.axis_index("expert")
+    row = lax.axis_index("dp")
+    mesh_ids = pl.DeviceIdType.MESH
+    has_upper = me < devices - 1
+    is_top = me == devices - 1
+    upper = lax.rem(me + 1, devices)
+    lower = lax.rem(me + devices - 1, devices)
+
+    def link(block, seq, peer):
+        return pltpu.make_async_remote_copy(
+            src_ref=sendbuf.at[block, seq],
+            dst_ref=recvbuf.at[block, seq],
+            send_sem=send_sems.at[block, seq],
+            recv_sem=recv_sems.at[block, seq],
+            device_id=(row, peer),
+            device_id_type=mesh_ids,
+        )
+
+    barrier = pltpu.get_barrier_semaphore()
+    for peer in (upper, lower):
+        pl.semaphore_signal(barrier, inc=1, device_id=(row, peer), device_id_type=mesh_ids)
+    pl.semaphore_wait(barrier, 2)
+
+    for seq in range(seqs):
+
+        @pl.when(has_upper)
+        def _():
+            link(me, seq, upper).wait_recv()
+            out_ref[seq] = (
+                parts_ref[me, seq].astype(jnp.float32) + recvbuf[me, seq].astype(jnp.float32)
+            ).astype(out_ref.dtype)
+
+        @pl.when(is_top)
+        def _():
+            out_ref[seq] = parts_ref[me, seq]
+
+    def forward(step, carry):
+        block = me - 1 - step
+        for seq in range(seqs):
+
+            @pl.when(has_upper)
+            def _():
+                link(block, seq, upper).wait_recv()
+                sendbuf[block, seq] = (
+                    parts_ref[block, seq].astype(jnp.float32)
+                    + recvbuf[block, seq].astype(jnp.float32)
+                ).astype(sendbuf.dtype)
+
+            @pl.when(is_top)
+            def _():
+                sendbuf[block, seq] = parts_ref[block, seq].astype(sendbuf.dtype)
+
+            link(block, seq, lower).start()
+        return carry
+
+    lax.fori_loop(0, me, forward, 0)
+
+    def finish(step, carry):
+        block = me - 1 - step
+        for seq in range(seqs):
+            link(block, seq, lower).wait_send()
+        return carry
+
+    lax.fori_loop(0, me, finish, 0)
+
+
+def pair_return(pair_buffer):
+    return pl.pallas_call(
+        pair_chain_kernel,
+        out_shape=jax.ShapeDtypeStruct(pair_buffer.shape[1:], pair_buffer.dtype),
+        in_specs=[pl.BlockSpec(memory_space=pltpu.VMEM)],
+        out_specs=pl.BlockSpec(memory_space=pltpu.VMEM),
+        scratch_shapes=[
+            pltpu.VMEM(pair_buffer.shape, CHAIN_DTYPE),
+            pltpu.VMEM(pair_buffer.shape, CHAIN_DTYPE),
+            pltpu.SemaphoreType.DMA(pair_buffer.shape[:2]),
+            pltpu.SemaphoreType.DMA(pair_buffer.shape[:2]),
+        ],
+        compiler_params=pltpu.CompilerParams(collective_id=0, has_side_effects=True),
+    )(pair_buffer)
 
 
 def shards(
@@ -76,7 +163,7 @@
     value_part = jnp.einsum(
         "shpr,sphd->srd", probs_low, context_grad, preferred_element_type=jnp.float32
     ).astype(jnp.bfloat16)
-    pair_buffer = lax.optimization_barrier(
+    pair_buffer = (
         jnp.moveaxis(
             jnp.concatenate([key_part, value_part], axis=2).reshape(
                 seq_count, devices, shard_len, 2 * HEAD
@@ -128,6 +215,7 @@
     weight_cat = jnp.concatenate(
         [gate_proj, up_proj, jnp.transpose(down_proj, (0, 2, 1))], axis=2
     )
+    gathered, weight_cat = lax.optimization_barrier((gathered, weight_cat))
     weight_full = lax.all_gather(weight_cat, "dp", axis=1, tiled=True)[0]
     gate_mat = weight_full[:, :hidden_cols]
     up_mat = weight_full[:, hidden_cols : 2 * hidden_cols]
@@ -183,7 +271,7 @@
     gate_proj_grad = summed[:, :hidden_width][None]
     up_proj_grad = summed[:, hidden_width : 2 * hidden_width][None]
     down_proj_grad = jnp.transpose(summed[:, 2 * hidden_width :])[None]
-    pair_total = lax.psum_scatter(pair_buffer, "expert", scatter_dimension=0, tiled=True)[0]
+    pair_total = pair_return(pair_buffer)
     key_grad = pair_total[:, :, :HEAD]
     value_grad = pair_total[:, :, HEAD:]
     back_all = lax.all_to_all(

time: 510 us -> 408 us (0.80)
  waiting for transfers between devices: 392 us -> 121 us
  Pallas kernels: 0 us -> 163 us
  matrix products: 29.9 us -> 38.9 us
  starting transfers between devices: 31 us -> 22.5 us
    unnamed x6 -> x4, waiting for transfers between devices: 259 us -> 0.05 us
    pallas_call x0 -> x1, Pallas kernels: none -> 163 us  [pair_return(): pl.pallas_call(pair_chain_kernel, out_shape=jax.ShapeDtypeStruct(pair_buf...]
    all_to_all x1, waiting for transfers between devices: 0.01 us -> 31.4 us  [shards(): lax.all_to_all(send_all, 'expert', split_axis=0, concat_axis=0, tiled=True)]
    all_gather x1, waiting for transfers between devices: 42 us -> 11.5 us  [shards(): weight_full = lax.all_gather(weight_cat, 'dp', axis=1, tiled=True)[0]]
    all_to_all x1, waiting for transfers between devices: 22.9 us -> 0.01 us  [shards(): lax.all_to_all(jnp.concatenate([input_rows.reshape(devices, CAP, model_wi...]
    all_gather x1, waiting for transfers between devices: 67.6 us -> 77.9 us  [shards(): gathered = lax.all_gather(packed, 'expert', axis=1, tiled=True)]
    all_to_all x1, starting transfers between devices: 16.8 us -> 8.37 us  [shards(): lax.all_to_all(send_all, 'expert', split_axis=0, concat_axis=0, tiled=True)]
    unnamed x20 -> x29, local copies, waits for them, and re-layouts: 10.8 us -> 9.35 us
  transfers between devices with their start and end apart: 6 -> 5, of which waited for: 5 -> 3; matrix products, arithmetic and copies ran while one was open for 13% -> 17% of each run, Pallas kernels for 0% -> 40%
where the time goes in v4:
time: 408 us; the launch traced here: 406 us
  Pallas kernels  163 us (40%)
  waiting for transfers between devices  121 us (30%)
  matrix products  38.9 us (10%)
  local copies, waits for them, and re-layouts  25.8 us (6%)
  starting transfers between devices  22.5 us (6%)
  other arithmetic  20.7 us (5%)
  between operations  14.1 us (3%)
    pallas_call x1, Pallas kernels, pair_return(): pl.pallas_call(pair_chain_kernel, out_shape=jax.ShapeDtypeStruct(pair_buf...  163 us
    all_gather x1, waiting for transfers between devices, shards(): gathered = lax.all_gather(packed, 'expert', axis=1, tiled=True)  77.9 us
    all_to_all x1, waiting for transfers between devices, shards(): lax.all_to_all(send_all, 'expert', split_axis=0, concat_axis=0, tiled=True)  31.4 us
    all_to_all x1, starting transfers between devices, shards(): lax.all_to_all(jnp.concatenate([input_rows.reshape(devices, CAP, model_wi...  13.9 us
    all_gather x1, waiting for transfers between devices, shards(): weight_full = lax.all_gather(weight_cat, 'dp', axis=1, tiled=True)[0]  11.5 us
    unnamed x29, local copies, waits for them, and re-layouts  9.35 us
    all_to_all x1, starting transfers between devices, shards(): lax.all_to_all(send_all, 'expert', split_axis=0, concat_axis=0, tiled=True)  8.37 us
  transfers between devices with their start and end apart: 5, of which 3 were waited for; matrix products, arithmetic and copies ran while one was open for 17% of the time, Pallas kernels for 40%

profile of v4, /device:TPU:1, one launch (start us, length us, event | category | flops | bytes accessed | tf_op | source)
XLA Modules:
  0.0 406.3 jit_solution(17680009967960683709)
XLA Ops:
  7.3 1.6 pad_maximum_fusion.5
  9.0 1.0 copy.82
  9.9 1.0 copy.81
  10.9 1.5 pad_maximum_fusion.4
  12.4 77.9 %all-gather.3.cloned.1.call-done = bf16[2,2048,512]{2,1,0:T(8,128)(2,1)} async-done(((bf16[2,64,512]{2,1,0:T(8,128)(2,1)}), bf16[2,2048,512]{2,1,0:T(8,128)(2,1)}) %all-gather.3.cloned.1.call-update) | async-done | bytes 4194320 | tf_op jit(solution)/shard_map/all_gather | solution.py:121
  90.4 0.7 fusion.64
  91.1 0.7 select_reduce_fusion.1
  91.8 0.2 fusion.16
  92.1 0.2 convolution_convert_fusion.3
  92.4 0.2 reshape.200
  92.6 1.3 convolution_convert_fusion.4
  93.8 0.2 reshape.199
  94.0 0.7 select_reduce_fusion
  94.7 0.1 fusion.40
  94.8 1.3 pad_maximum_fusion.2
  96.2 8.4 %all-to-all-start = ((bf16[32,2,4224]{2,1,0:T(2,128)(2,1)}), bf16[32,2,4224]{2,1,0:T(2,128)(2,1)S(1)}, u32[]{:S(2)}, u32[]{:S(2)}) async-start(bf16[32,2,4224]{2,1,0:T(2,128)(2,1)} %pad_maximum_fusion.2), calls=%async_computation | async-start | bytes 1081344 | tf_op jit(solution)/shard_map/all_to_all | solution.py:223
  104.6 0.2 reduce-scatter.4.cloned.1.call-start
  104.8 1.1 reshape.203
  105.9 0.1 iota_compare_fusion
  106.1 1.3 add_divide_fusion
  107.4 31.4 %all-to-all-done = bf16[32,2,4224]{2,1,0:T(2,128)(2,1)S(1)} async-done(((bf16[32,2,4224]{2,1,0:T(2,128)(2,1)}), bf16[32,2,4224]{2,1,0:T(2,128)(2,1)S(1)}, u32[]{:S(2)}, u32[]{:S(2)}) %all-to-all-start) | async-done | bytes 540704 | tf_op jit(solution)/shard_map/all_to_all | solution.py:223
  138.8 0.4 fusion.66
  139.1 0.4 reshape.206
  139.5 0.1 reshape.201
  139.6 0.1 convert_reduce_fusion
  139.7 0.1 reshape.205
  139.8 6.3 %fusion.5 = (f32[2,8,64]{2,1,0:T(8,128)S(1)}, f32[2,2048,64,8]{1,2,3,0:T(8,128)}) fusion(pred[64,2048]{1,0:T(8,128)(4,1)S(1)} %iota_compare_fusion, bf16[2,8,8,8,256]{4,3,2,1,0:T(8,128)(2,1)} %bitcast.154, bf16[2,2048,512]{2,1,0:T(8,128)(2,1)} %all-gather.3.cloned.1.call-done), kind=kOutput, calls=%fused_computation.9 | convolution fusion | flops 1080032256 | bytes 11145216 | tf_op jit(solution)/shard_map/sphd,srd->shpr/dot_general | solution.py:126
  146.1 11.5 %all-gather.5.cloned.1.call-done = bf16[1,2048,768]{1,2,0:T(8,128)(2,1)} async-done(((bf16[1,128,768]{1,2,0:T(8,128)(2,1)}), bf16[1,2048,768]{1,2,0:T(8,128)(2,1)}) %all-gather.5.cloned.1.call-update) | async-done | bytes 3145744 | tf_op jit(solution)/shard_map/all_gather | solution.py:219
  157.6 1.7 fusion.22
  159.3 1.7 fusion.25
  161.0 1.7 multiply_convert_fusion.2
  162.6 0.5 convolution_convert_fusion
  163.2 0.5 convolution_convert_fusion.1
  163.6 0.5 convolution_convert_fusion.2
  164.1 1.9 pad_maximum_fusion.1
  166.0 4.7 %copy.93 = bf16[2048,768]{1,0:T(8,128)(2,1)} copy(bf16[2048,768]{0,1:T(8,128)(2,1)} %pad_maximum_fusion.1) | data formatting | bytes 6291456
  170.7 4.7 %exponential_reduce_fusion = f32[2,8,64]{2,1,0:T(8,128)S(1)} fusion(f32[2,2048,64,8]{1,2,3,0:T(8,128)} %get-tuple-element.63, f32[2,8,64]{2,1,0:T(8,128)S(1)} %get-tuple-element.62, pred[64,2048]{1,0:T(8,128)(4,1)S(1)} %iota_compare_fusion), kind=kLoop, calls=%fused_computation.8 | loop fusion | flops 8387584 | bytes 8527872 | tf_op jit(solution)/shard_map/reduce_sum | solution.py:134
  175.5 6.5 %multiply_reduce_fusion = (f32[2,64,8]{1,2,0:T(8,128)S(1)}, bf16[2,64,8,256]{3,1,2,0:T(8,128)(2,1)S(1)}, bf16[2,8,8,8,256]{4,3,2,1,0:T(8,128)(2,1)}) fusion(f32[2,8,8,8,256]{4,3,2,1,0:T(8,128)S(1)} %bitcast.151, f32[2,8,8,8,256]{4,3,2,1,0:T(8,128)S(1)} %bitcast.150, f32[2,2048,64,8]{1,2,3,0:T(8,128)} %get-tuple-element.63, ...), kind=kOutput, calls=%fused_computation.44 | convolution fusion | flops 1084750848 | bytes 13770752 | tf_op jit(solution)/shard_map/shpr,srd->sphd/dot_general | solution.py:137
  181.9 2.2 bitcast_convert_fusion
  184.1 4.5 %fusion.2 = bf16[2,8,64,2048]{3,2,1,0:T(8,128)(2,1)} fusion(f32[2,2048,64,8]{1,2,3,0:T(8,128)S(1)} %bitcast.143, bf16[2,64,8,256]{3,1,2,0:T(8,128)(2,1)S(1)} %get-tuple-element.50, f32[2,8,64]{2,1,0:T(8,128)S(1)} %bitcast.157, f32[2,8,64]{2,1,0:T(8,128)S(1)} %log_add_fusion, pred[64,2048]{1,0:T(8,128)(4,1)S(1)} %iota_compare_fusion, ...), kind=kOutput, calls=%fused_computation.3 | convolution fusion | flops 1088421888 | bytes 15351808 | tf_op jit(solution)/shard_map/sphd,srd->shpr/dot_general | solution.py:151
  188.6 1.6 fusion.15
  190.2 0.1 convert_element_type.153
  190.4 1.5 fusion.20
  191.9 1.5 fusion.8
  193.4 0.2 reshape.202
  193.7 1.0 pad_maximum_fusion.3
  194.7 13.9 %all-to-all-start.1 = ((bf16[32,2,2176]{2,1,0:T(2,128)(2,1)}), bf16[32,2,2176]{2,1,0:T(2,128)(2,1)S(1)}, u32[]{:S(2)}, u32[]{:S(2)}) async-start(bf16[32,2,2176]{2,1,0:T(2,128)(2,1)} %pad_maximum_fusion.3), calls=%async_computation.1 | async-start | bytes 557056 | tf_op jit(solution)/shard_map/all_to_all | solution.py:277
  208.6 4.3 %fusion.14 = bf16[2,8,8,8,256]{4,3,2,1,0:T(8,128)(2,1)S(1)} fusion(bf16[2,8,64,2048]{3,2,1,0:T(8,128)(2,1)} %fusion.2, bf16[2,2048,512]{2,1,0:T(8,128)(2,1)} %all-gather.3.cloned.1.call-done), kind=kOutput, calls=%fused_computation.33 | convolution fusion | flops 1074003968 | bytes 6815744 | tf_op jit(solution)/shard_map/shpr,srd->sphd/dot_general | solution.py:157
  212.9 0.8 copy.100
  213.7 1.3 bitcast_convert_fusion.1
  215.0 2.5 pad_maximum_fusion
  217.6 6.2 %copy.75 = bf16[2,2048,512]{2,1,0:T(8,128)(2,1)} copy(bf16[2,2048,512]{1,2,0:T(8,128)(2,1)} %pad_maximum_fusion) | data formatting | bytes 8388608 | tf_op jit(solution)/shard_map/concatenate | solution.py:168
  223.8 4.7 %copy.127 = bf16[2,32,64,512]{3,2,0,1:T(8,128)(2,1)} copy(bf16[2,32,64,512]{3,2,1,0:T(8,128)(2,1)} %bitcast.140) | data formatting | bytes 8388608 | tf_op jit(solution)/shard_map/reshape | solution.py:168
  228.5 163.3 %shard_map.187 = bf16[2,64,512]{2,1,0:T(8,128)(2,1)} custom-call(bf16[32,2,64,512]{3,2,1,0:T(8,128)(2,1)} %bitcast.141), custom_call_target="tpu_custom_call" | custom-call | tf_op jit(solution)/shard_map/pallas_call | solution.py:83
  391.8 0.8 copy.101
  392.6 1.5 fusion.67
  394.4 0.2 slice.68
  394.6 0.1 multiply_reduce_fusion.1
  394.7 0.6 select_convert_fusion
  395.3 1.1 fusion.7
  396.4 1.1 copy.94
  397.5 0.7 slice_bitcast_fusion.12
  398.2 0.8 copy.87
  399.0 0.8 copy.88
  (43 shorter events, 0.7 us)
Async XLA Ops:
  7.2 85.0 %copy-start = (bf16[128,2048]{1,0:T(8,128)(2,1)S(1)}, bf16[128,2048]{1,0:T(8,128)(2,1)}, u32[]{:S(2)}) copy-start(bf16[128,2048]{1,0:T(8,128)(2,1)} %param.18) | copy-start | bytes 1572868
  7.2 97.6 %copy-start.4 = (bf16[2,64,2048]{2,1,0:T(8,128)(2,1)S(1)}, bf16[2,64,2048]{2,1,0:T(8,128)(2,1)}, u32[]{:S(2)}) copy-start(bf16[2,64,2048]{2,1,0:T(8,128)(2,1)} %param.16) | copy-start | bytes 1572868
  7.2 98.9 %copy-start.5 = (bf16[2,64,2048]{2,1,0:T(8,128)(2,1)S(1)}, bf16[2,64,2048]{2,1,0:T(8,128)(2,1)}, u32[]{:S(2)}) copy-start(bf16[2,64,2048]{2,1,0:T(8,128)(2,1)} %param.15) | copy-start | bytes 1572868
  7.2 83.1 %all-gather.3.cloned.1.call-start = ((), (), s32[]{:S(2)}) async-start(), calls=%async_computation.3 | async-start | bytes 4325376 | tf_op jit(solution)/shard_map/all_gather | solution.py:121
  8.9 148.7 %all-gather.5.cloned.1.call-start = ((), (), s32[]{:S(2)}) async-start(), calls=%async_computation.4 | async-start | bytes 3342336 | tf_op jit(solution)/shard_map/all_gather | solution.py:219
  96.2 42.6 %all-to-all-start = ((bf16[32,2,4224]{2,1,0:T(2,128)(2,1)}), bf16[32,2,4224]{2,1,0:T(2,128)(2,1)S(1)}, u32[]{:S(2)}, u32[]{:S(2)}) async-start(bf16[32,2,4224]{2,1,0:T(2,128)(2,1)} %pad_maximum_fusion.2), calls=%async_computation | async-start | bytes 1081344 | tf_op jit(solution)/shard_map/all_to_all | solution.py:223
  104.6 291.9 %reduce-scatter.4.cloned.1.call-start = ((), (), s32[]{:S(2)}) async-start(), calls=%async_computation.5 | async-start | bytes 3342336
  170.7 4.7 %copy-start.2 = (f32[2,64,2048]{2,1,0:T(8,128)S(1)}, f32[2,64,2048]{2,1,0:T(8,128)}, u32[]{:S(2)}) copy-start(f32[2,64,2048]{2,1,0:T(8,128)} %reshape.203) | copy-start | bytes 3145732
  170.7 4.7 %copy-start.3 = (f32[2,64,2048]{2,1,0:T(8,128)S(1)}, f32[2,64,2048]{2,1,0:T(8,128)}, u32[]{:S(2)}) copy-start(f32[2,64,2048]{2,1,0:T(8,128)} %add_divide_fusion) | copy-start | bytes 3145732
  170.7 11.2 %slice-start = ((s8[8388608]{0:T(1024)(128)(4,1)}), s8[4194304]{0:T(1024)(128)(4,1)S(1)}, s32[]{:S(2)}) async-start(s8[8388608]{0:T(1024)(128)(4,1)} %bitcast.142), calls=%async_computation.6 | async-start | bytes 8388608
  175.4 6.5 %slice-start.1 = ((s8[8388608]{0:T(1024)(128)(4,1)}), s8[4194304]{0:T(1024)(128)(4,1)S(1)}, s32[]{:S(2)}) async-start(s8[8388608]{0:T(1024)(128)(4,1)} %bitcast.142), calls=%async_computation.7 | async-start | bytes 8388608
  181.9 2.2 copy-start.8
  194.7 199.4 %all-to-all-start.1 = ((bf16[32,2,2176]{2,1,0:T(2,128)(2,1)}), bf16[32,2,2176]{2,1,0:T(2,128)(2,1)S(1)}, u32[]{:S(2)}, u32[]{:S(2)}) async-start(bf16[32,2,2176]{2,1,0:T(2,128)(2,1)} %pad_maximum_fusion.3), calls=%async_computation.1 | async-start | bytes 557056 | tf_op jit(solution)/shard_map/all_to_all | solution.py:277
  208.6 5.2 %copy-start.1 = (bf16[2,8,64,2048]{3,2,1,0:T(8,128)(2,1)S(1)}, bf16[2,8,64,2048]{3,2,1,0:T(8,128)(2,1)}, u32[]{:S(2)}) copy-start(bf16[2,8,64,2048]{3,2,1,0:T(8,128)(2,1)} %fusion.2) | copy-start | bytes 12582916
  208.6 5.1 %copy-start.7 = (bf16[2,64,2048]{2,1,0:T(8,128)(2,1)S(1)}, bf16[2,64,2048]{2,1,0:T(8,128)(2,1)}, u32[]{:S(2)}) copy-start(bf16[2,64,2048]{2,1,0:T(8,128)(2,1)} %param.12) | copy-start | bytes 1572868
  228.5 163.3 %copy-start.6 = (bf16[2,8,8,8,256]{4,3,2,1,0:T(8,128)(2,1)S(1)}, bf16[2,8,8,8,256]{4,3,2,1,0:T(8,128)(2,1)}, u32[]{:S(2)}) copy-start(bf16[2,8,8,8,256]{4,3,2,1,0:T(8,128)(2,1)} %get-tuple-element.51) | copy-start | bytes 1572868
Sparse Core Ops, SparseCore 0:
  10.8 79.5 all-gather.2
  93.9 63.6 all-gather.4
  170.8 89.7 reduce-scatter.3

commit v5 on v4

--- a/solution.py
+++ b/solution.py
@@ -8,7 +8,7 @@
 HEADS = 8
 HEAD = 256
 CAP = 2
-CHAIN_DTYPE = jnp.float32
+CHAIN_DTYPE = jnp.bfloat16
 
 
 def pair_chain_kernel(parts_ref, out_ref, sendbuf, recvbuf, send_sems, recv_sems):
@@ -120,6 +120,57 @@
     packed = jnp.concatenate([key_rows, value_rows], axis=2)
     gathered = lax.all_gather(packed, "expert", axis=1, tiled=True)
 
+    token_count, model_width = moe_input.shape
+    live_slot = routes < devices
+    has_live = jnp.any(live_slot, axis=1)
+    live_expert = jnp.sum(jnp.where(live_slot, routes, 0), axis=1)
+    token_weight = jnp.sum(jnp.where(live_slot, route_weights.astype(jnp.float32), 0.0), axis=1)
+    member = (live_expert[:, None] == jnp.arange(devices)[None, :]) & has_live[:, None]
+    earlier = (jnp.arange(token_count)[None, :] < jnp.arange(token_count)[:, None]).astype(
+        jnp.bfloat16
+    )
+    before = jnp.dot(earlier, member.astype(jnp.bfloat16), preferred_element_type=jnp.float32)
+    slot_rank = jnp.sum(jnp.where(member, before, 0.0), axis=1)
+    placed = member.T[:, None, :] & (
+        slot_rank[None, None, :] == jnp.arange(CAP)[None, :, None].astype(jnp.float32)
+    )
+    dispatch_mat = placed.reshape(devices * CAP, token_count).astype(jnp.bfloat16)
+    model_cols = model_width
+    pad_cols = 128
+    rows_send = (
+        jnp.dot(dispatch_mat, moe_input, preferred_element_type=jnp.float32)
+        .astype(jnp.bfloat16)
+        .reshape(devices, CAP, model_width)
+    )
+    grads_send = (
+        jnp.dot(dispatch_mat, out_grad, preferred_element_type=jnp.float32)
+        .astype(jnp.bfloat16)
+        .reshape(devices, CAP, model_width)
+    )
+    weights_send = jnp.sum(jnp.where(placed, token_weight[None, None, :], 0.0), axis=2).astype(
+        jnp.bfloat16
+    )
+    send_all = jnp.concatenate(
+        [
+            rows_send,
+            grads_send,
+            jnp.broadcast_to(weights_send[:, :, None], (devices, CAP, pad_cols)),
+        ],
+        axis=2,
+    )
+    hidden_cols = gate_proj.shape[2]
+    weight_cat = jnp.concatenate(
+        [gate_proj, up_proj, jnp.transpose(down_proj, (0, 2, 1))], axis=2
+    )
+    recv_all = lax.all_to_all(send_all, "expert", split_axis=0, concat_axis=0, tiled=True)
+    gathered, recv_all, weight_cat = lax.optimization_barrier((gathered, recv_all, weight_cat))
+    rows_in = recv_all[:, :, :model_cols]
+    grads_in = recv_all[:, :, model_cols : 2 * model_cols]
+    weights_in = recv_all[:, :, 2 * model_cols]
+    weight_full = lax.all_gather(weight_cat, "dp", axis=1, tiled=True)[0]
+    gate_mat = weight_full[:, :hidden_cols]
+    up_mat = weight_full[:, hidden_cols : 2 * hidden_cols]
+    down_mat = jnp.transpose(weight_full[:, 2 * hidden_cols :])
     keys_all = gathered[:, :, :HEAD]
     values_all = gathered[:, :, HEAD:]
     scores = (
@@ -173,57 +224,6 @@
         )
     )
     query_grad = query_total.astype(jnp.bfloat16).reshape(seq_count, shard_len, row_width)
-    token_count, model_width = moe_input.shape
-    live_slot = routes < devices
-    has_live = jnp.any(live_slot, axis=1)
-    live_expert = jnp.sum(jnp.where(live_slot, routes, 0), axis=1)
-    token_weight = jnp.sum(jnp.where(live_slot, route_weights.astype(jnp.float32), 0.0), axis=1)
-    member = (live_expert[:, None] == jnp.arange(devices)[None, :]) & has_live[:, None]
-    earlier = (jnp.arange(token_count)[None, :] < jnp.arange(token_count)[:, None]).astype(
-        jnp.bfloat16
-    )
-    before = jnp.dot(earlier, member.astype(jnp.bfloat16), preferred_element_type=jnp.float32)
-    slot_rank = jnp.sum(jnp.where(member, before, 0.0), axis=1)
-    placed = member.T[:, None, :] & (
-        slot_rank[None, None, :] == jnp.arange(CAP)[None, :, None].astype(jnp.float32)
-    )
-    dispatch_mat = placed.reshape(devices * CAP, token_count).astype(jnp.bfloat16)
-    model_cols = model_width
-    pad_cols = 128
-    rows_send = (
-        jnp.dot(dispatch_mat, moe_input, preferred_element_type=jnp.float32)
-        .astype(jnp.bfloat16)
-        .reshape(devices, CAP, model_width)
-    )
-    grads_send = (
-        jnp.dot(dispatch_mat, out_grad, preferred_element_type=jnp.float32)
-        .astype(jnp.bfloat16)
-        .reshape(devices, CAP, model_width)
-    )
-    weights_send = jnp.sum(jnp.where(placed, token_weight[None, None, :], 0.0), axis=2).astype(
-        jnp.bfloat16
-    )
-    send_all = jnp.concatenate(
-        [
-            rows_send,
-            grads_send,
-            jnp.broadcast_to(weights_send[:, :, None], (devices, CAP, pad_cols)),
-        ],
-        axis=2,
-    )
-    hidden_cols = gate_proj.shape[2]
-    weight_cat = jnp.concatenate(
-        [gate_proj, up_proj, jnp.transpose(down_proj, (0, 2, 1))], axis=2
-    )
-    gathered, weight_cat = lax.optimization_barrier((gathered, weight_cat))
-    weight_full = lax.all_gather(weight_cat, "dp", axis=1, tiled=True)[0]
-    gate_mat = weight_full[:, :hidden_cols]
-    up_mat = weight_full[:, hidden_cols : 2 * hidden_cols]
-    down_mat = jnp.transpose(weight_full[:, 2 * hidden_cols :])
-    recv_all = lax.all_to_all(send_all, "expert", split_axis=0, concat_axis=0, tiled=True)
-    rows_in = recv_all[:, :, :model_cols]
-    grads_in = recv_all[:, :, model_cols : 2 * model_cols]
-    weights_in = recv_all[:, :, 2 * model_cols]
     flat_rows = rows_in.reshape(devices * CAP, model_width)
     flat_grads = grads_in.reshape(devices * CAP, model_width)
     gate_pre = jnp.dot(flat_rows, gate_mat, preferred_element_type=jnp.float32)

time: 408 us -> 368 us (0.902)
  Pallas kernels: 163 us -> 110 us
  starting transfers between devices: 22.5 us -> 30.9 us
  waiting for transfers between devices: 121 us -> 129 us
    pallas_call x1, Pallas kernels: 163 us -> 110 us  [pair_return(): pl.pallas_call(pair_chain_kernel, out_shape=jax.ShapeDtypeStruct(pair_buf...]
    all_gather x1, waiting for transfers between devices: 11.5 us -> 56.4 us  [shards(): weight_full = lax.all_gather(weight_cat, 'dp', axis=1, tiled=True)[0]]
    all_gather x1, waiting for transfers between devices: 77.9 us -> 33.4 us  [shards(): gathered = lax.all_gather(packed, 'expert', axis=1, tiled=True)]
    all_to_all x1, starting transfers between devices: 8.37 us -> 16.8 us  [shards(): lax.all_to_all(send_all, 'expert', split_axis=0, concat_axis=0, tiled=True)]
    all_to_all x1, waiting for transfers between devices: 31.4 us -> 39 us  [shards(): lax.all_to_all(send_all, 'expert', split_axis=0, concat_axis=0, tiled=True)]
    unnamed x29 -> x35, local copies, waits for them, and re-layouts: 9.35 us -> 7.69 us
  transfers between devices with their start and end apart: 5 -> 5, of which waited for: 3 -> 3; matrix products, arithmetic and copies ran while one was open for 17% -> 18% of each run, Pallas kernels for 40% -> 30%
where the time goes in v5:
time: 368 us; the launch traced here: 367 us
  waiting for transfers between devices  129 us (35%)
  Pallas kernels  110 us (30%)
  matrix products  38.9 us (11%)
  starting transfers between devices  30.9 us (8%)
  local copies, waits for them, and re-layouts  24.2 us (7%)
  other arithmetic  19.7 us (5%)
  between operations  14.2 us (4%)
    pallas_call x1, Pallas kernels, pair_return(): pl.pallas_call(pair_chain_kernel, out_shape=jax.ShapeDtypeStruct(pair_buf...  110 us
    all_gather x1, waiting for transfers between devices, shards(): weight_full = lax.all_gather(weight_cat, 'dp', axis=1, tiled=True)[0]  56.4 us
    all_to_all x1, waiting for transfers between devices, shards(): lax.all_to_all(send_all, 'expert', split_axis=0, concat_axis=0, tiled=True)  39 us
    all_gather x1, waiting for transfers between devices, shards(): gathered = lax.all_gather(packed, 'expert', axis=1, tiled=True)  33.4 us
    all_to_all x1, starting transfers between devices, shards(): lax.all_to_all(send_all, 'expert', split_axis=0, concat_axis=0, tiled=True)  16.8 us
    all_to_all x1, starting transfers between devices, shards(): lax.all_to_all(jnp.concatenate([input_rows.reshape(devices, CAP, model_wi...  13.9 us
    unnamed x35, local copies, waits for them, and re-layouts  7.69 us
  transfers between devices with their start and end apart: 5, of which 3 were waited for; matrix products, arithmetic and copies ran while one was open for 18% of the time, Pallas kernels for 30%

profile of v5, /device:TPU:1, one launch (start us, length us, event | category | flops | bytes accessed | tf_op | source)
XLA Modules:
  0.0 366.9 jit_solution(1686751590754419930)
XLA Ops:
  7.3 1.6 pad_maximum_fusion.5
  9.0 0.7 fusion.79
  9.7 0.7 select_reduce_fusion.1
  10.4 0.2 fusion.30
  10.7 0.2 convolution_convert_fusion.3
  11.0 0.2 reshape.193
  11.2 1.3 convolution_convert_fusion.4
  12.4 0.2 reshape.192
  12.6 0.7 select_reduce_fusion
  13.3 0.1 fusion.54
  13.4 1.3 pad_maximum_fusion.2
  14.7 16.8 %all-to-all-start = ((bf16[32,2,4224]{2,1,0:T(2,128)(2,1)}), bf16[32,2,4224]{2,1,0:T(2,128)(2,1)S(1)}, u32[]{:S(2)}, u32[]{:S(2)}) async-start(bf16[32,2,4224]{2,1,0:T(2,128)(2,1)} %pad_maximum_fusion.2), calls=%async_computation | async-start | bytes 1081344 | tf_op jit(solution)/shard_map/all_to_all | solution.py:165
  31.5 0.1 copy.71
  31.7 0.1 copy.70
  31.8 0.7 pad_maximum_fusion.4
  32.5 39.0 %all-to-all-done = bf16[32,2,4224]{2,1,0:T(2,128)(2,1)S(1)} async-done(((bf16[32,2,4224]{2,1,0:T(2,128)(2,1)}), bf16[32,2,4224]{2,1,0:T(2,128)(2,1)S(1)}, u32[]{:S(2)}, u32[]{:S(2)}) %all-to-all-start) | async-done | bytes 540704 | tf_op jit(solution)/shard_map/all_to_all | solution.py:165
  71.5 33.4 %all-gather.3.cloned.1.call-done = bf16[2,2048,512]{2,1,0:T(8,128)(2,1)} async-done(((bf16[2,64,512]{2,1,0:T(8,128)(2,1)}), bf16[2,2048,512]{2,1,0:T(8,128)(2,1)}) %all-gather.3.cloned.1.call-update) | async-done | bytes 4194320 | tf_op jit(solution)/shard_map/all_gather | solution.py:121
  104.9 0.2 reduce-scatter.4.cloned.1.call-start
  105.2 1.1 reshape.203
  106.3 0.1 iota_compare_fusion
  106.5 1.3 add_divide_fusion
  107.7 0.4 fusion.80
  108.1 0.4 reshape.206
  108.5 0.1 reshape.201
  108.6 0.1 convert_reduce_fusion
  108.7 0.1 reshape.205
  108.8 6.3 %fusion.5 = (f32[2,8,64]{2,1,0:T(8,128)S(1)}, f32[2,2048,64,8]{1,2,3,0:T(8,128)}) fusion(pred[64,2048]{1,0:T(8,128)(4,1)S(1)} %iota_compare_fusion, bf16[2,8,8,8,256]{4,3,2,1,0:T(8,128)(2,1)} %bitcast.156, bf16[2,2048,512]{2,1,0:T(8,128)(2,1)} %all-gather.3.cloned.1.call-done), kind=kOutput, calls=%fused_computation.9 | convolution fusion | flops 1080032256 | bytes 11145216 | tf_op jit(solution)/shard_map/sphd,srd->shpr/dot_general | solution.py:177
  115.1 56.4 %all-gather.5.cloned.1.call-done = bf16[1,2048,768]{1,2,0:T(8,128)(2,1)} async-done(((bf16[1,128,768]{1,2,0:T(8,128)(2,1)}), bf16[1,2048,768]{1,2,0:T(8,128)(2,1)}) %all-gather.5.cloned.1.call-update) | async-done | bytes 3145744 | tf_op jit(solution)/shard_map/all_gather | solution.py:170
  171.5 1.7 fusion.36
  173.2 1.7 fusion.39
  174.8 1.7 multiply_convert_fusion.2
  176.5 0.5 convolution_convert_fusion
  177.0 0.5 convolution_convert_fusion.1
  177.5 0.5 convolution_convert_fusion.2
  178.0 1.8 pad_maximum_fusion.1
  179.8 4.7 %copy.93 = bf16[2048,768]{1,0:T(8,128)(2,1)} copy(bf16[2048,768]{0,1:T(8,128)(2,1)} %pad_maximum_fusion.1) | data formatting | bytes 6291456
  184.5 4.7 %exponential_reduce_fusion = f32[2,8,64]{2,1,0:T(8,128)S(1)} fusion(f32[2,2048,64,8]{1,2,3,0:T(8,128)} %get-tuple-element.67, f32[2,8,64]{2,1,0:T(8,128)S(1)} %get-tuple-element.66, pred[64,2048]{1,0:T(8,128)(4,1)S(1)} %iota_compare_fusion), kind=kLoop, calls=%fused_computation.8 | loop fusion | flops 8387584 | bytes 8527872 | tf_op jit(solution)/shard_map/reduce_sum | solution.py:185
  189.3 6.5 %multiply_reduce_fusion = (f32[2,64,8]{1,2,0:T(8,128)S(1)}, bf16[2,64,8,256]{3,1,2,0:T(8,128)(2,1)S(1)}, bf16[2,8,8,8,256]{4,3,2,1,0:T(8,128)(2,1)}) fusion(f32[2,8,8,8,256]{4,3,2,1,0:T(8,128)S(1)} %bitcast.153, f32[2,8,8,8,256]{4,3,2,1,0:T(8,128)S(1)} %bitcast.152, f32[2,2048,64,8]{1,2,3,0:T(8,128)} %get-tuple-element.67, ...), kind=kOutput, calls=%fused_computation.50 | convolution fusion | flops 1084750848 | bytes 13770752 | tf_op jit(solution)/shard_map/shpr,srd->sphd/dot_general | solution.py:188
  195.7 2.2 bitcast_convert_fusion
  197.9 4.5 %fusion.2 = bf16[2,8,64,2048]{3,2,1,0:T(8,128)(2,1)} fusion(f32[2,2048,64,8]{1,2,3,0:T(8,128)S(1)} %bitcast.145, bf16[2,64,8,256]{3,1,2,0:T(8,128)(2,1)S(1)} %get-tuple-element.52, f32[2,8,64]{2,1,0:T(8,128)S(1)} %bitcast.159, f32[2,8,64]{2,1,0:T(8,128)S(1)} %log_add_fusion, pred[64,2048]{1,0:T(8,128)(4,1)S(1)} %iota_compare_fusion, ...), kind=kOutput, calls=%fused_computation.3 | convolution fusion | flops 1088421888 | bytes 15351808 | tf_op jit(solution)/shard_map/sphd,srd->shpr/dot_general | solution.py:202
  202.4 1.6 fusion.29
  204.1 0.1 convert_element_type.153
  204.2 1.5 fusion.34
  205.7 1.5 fusion.8
  207.3 0.2 reshape.202
  207.6 1.0 pad_maximum_fusion.3
  208.6 13.9 %all-to-all-start.1 = ((bf16[32,2,2176]{2,1,0:T(2,128)(2,1)}), bf16[32,2,2176]{2,1,0:T(2,128)(2,1)S(1)}, u32[]{:S(2)}, u32[]{:S(2)}) async-start(bf16[32,2,2176]{2,1,0:T(2,128)(2,1)} %pad_maximum_fusion.3), calls=%async_computation.1 | async-start | bytes 557056 | tf_op jit(solution)/shard_map/all_to_all | solution.py:277
  222.5 4.3 %fusion.26 = bf16[2,8,8,8,256]{4,3,2,1,0:T(8,128)(2,1)S(1)} fusion(bf16[2,8,64,2048]{3,2,1,0:T(8,128)(2,1)} %fusion.2, bf16[2,2048,512]{2,1,0:T(8,128)(2,1)} %all-gather.3.cloned.1.call-done), kind=kOutput, calls=%fused_computation.39 | convolution fusion | flops 1074003968 | bytes 6815744 | tf_op jit(solution)/shard_map/shpr,srd->sphd/dot_general | solution.py:208
  226.7 0.8 copy.100
  227.6 1.3 bitcast_convert_fusion.1
  228.9 2.5 pad_maximum_fusion
  231.4 6.2 %copy.77 = bf16[2,2048,512]{2,1,0:T(8,128)(2,1)} copy(bf16[2,2048,512]{1,2,0:T(8,128)(2,1)} %pad_maximum_fusion) | data formatting | bytes 8388608 | tf_op jit(solution)/shard_map/concatenate | solution.py:219
  237.7 4.7 %copy.127 = bf16[2,32,64,512]{3,2,0,1:T(8,128)(2,1)} copy(bf16[2,32,64,512]{3,2,1,0:T(8,128)(2,1)} %bitcast.142) | data formatting | bytes 8388608 | tf_op jit(solution)/shard_map/reshape | solution.py:219
  242.3 110.1 %shard_map.187 = bf16[2,64,512]{2,1,0:T(8,128)(2,1)} custom-call(bf16[32,2,64,512]{3,2,1,0:T(8,128)(2,1)} %bitcast.143), custom_call_target="tpu_custom_call" | custom-call | tf_op jit(solution)/shard_map/pallas_call | solution.py:83
  352.4 0.8 copy.101
  353.3 1.5 fusion.81
  355.0 0.2 slice.63
  355.2 0.1 multiply_reduce_fusion.1
  355.3 0.6 select_convert_fusion
  355.9 1.1 fusion.7
  357.1 1.1 copy.94
  358.2 0.7 slice_bitcast_fusion
  358.9 0.8 copy.87
  359.6 0.8 copy.88
  (49 shorter events, 0.7 us)
Async XLA Ops:
  7.2 3.6 copy-start
  7.2 24.3 %copy-start.8 = (bf16[1,128,256]{2,1,0:T(8,128)(2,1)S(1)}, bf16[1,128,256]{2,1,0:T(8,128)(2,1)}, u32[]{:S(2)}) copy-start(bf16[1,128,256]{2,1,0:T(8,128)(2,1)} %param.22) | copy-start | bytes 196612
  7.2 24.5 %copy-start.9 = (bf16[1,128,256]{2,1,0:T(8,128)(2,1)S(1)}, bf16[1,128,256]{2,1,0:T(8,128)(2,1)}, u32[]{:S(2)}) copy-start(bf16[1,128,256]{2,1,0:T(8,128)(2,1)} %param.21) | copy-start | bytes 196612
  7.2 24.6 %copy-start.10 = (bf16[1,256,128]{2,1,0:T(8,128)(2,1)S(1)}, bf16[1,256,128]{2,1,0:T(8,128)(2,1)}, u32[]{:S(2)}) copy-start(bf16[1,256,128]{2,1,0:T(8,128)(2,1)} %param.23) | copy-start | bytes 196612
  7.2 98.0 %copy-start.4 = (bf16[2,64,2048]{2,1,0:T(8,128)(2,1)S(1)}, bf16[2,64,2048]{2,1,0:T(8,128)(2,1)}, u32[]{:S(2)}) copy-start(bf16[2,64,2048]{2,1,0:T(8,128)(2,1)} %param.16) | copy-start | bytes 1572868
  7.2 99.2 %copy-start.5 = (bf16[2,64,2048]{2,1,0:T(8,128)(2,1)S(1)}, bf16[2,64,2048]{2,1,0:T(8,128)(2,1)}, u32[]{:S(2)}) copy-start(bf16[2,64,2048]{2,1,0:T(8,128)(2,1)} %param.15) | copy-start | bytes 1572868
  7.2 97.7 %all-gather.3.cloned.1.call-start = ((), (), s32[]{:S(2)}) async-start(), calls=%async_computation.3 | async-start | bytes 4325376 | tf_op jit(solution)/shard_map/all_gather | solution.py:121
  14.7 56.8 %all-to-all-start = ((bf16[32,2,4224]{2,1,0:T(2,128)(2,1)}), bf16[32,2,4224]{2,1,0:T(2,128)(2,1)S(1)}, u32[]{:S(2)}, u32[]{:S(2)}) async-start(bf16[32,2,4224]{2,1,0:T(2,128)(2,1)} %pad_maximum_fusion.2), calls=%async_computation | async-start | bytes 1081344 | tf_op jit(solution)/shard_map/all_to_all | solution.py:165
  31.5 140.0 %all-gather.5.cloned.1.call-start = ((), (), s32[]{:S(2)}) async-start(), calls=%async_computation.4 | async-start | bytes 3342336 | tf_op jit(solution)/shard_map/all_gather | solution.py:170
  104.9 252.1 %reduce-scatter.4.cloned.1.call-start = ((), (), s32[]{:S(2)}) async-start(), calls=%async_computation.5 | async-start | bytes 3342336
  184.5 4.7 %copy-start.2 = (f32[2,64,2048]{2,1,0:T(8,128)S(1)}, f32[2,64,2048]{2,1,0:T(8,128)}, u32[]{:S(2)}) copy-start(f32[2,64,2048]{2,1,0:T(8,128)} %reshape.203) | copy-start | bytes 3145732
  184.5 4.7 %copy-start.3 = (f32[2,64,2048]{2,1,0:T(8,128)S(1)}, f32[2,64,2048]{2,1,0:T(8,128)}, u32[]{:S(2)}) copy-start(f32[2,64,2048]{2,1,0:T(8,128)} %add_divide_fusion) | copy-start | bytes 3145732
  184.5 11.2 %slice-start = ((s8[8388608]{0:T(1024)(128)(4,1)}), s8[4194304]{0:T(1024)(128)(4,1)S(1)}, s32[]{:S(2)}) async-start(s8[8388608]{0:T(1024)(128)(4,1)} %bitcast.144), calls=%async_computation.6 | async-start | bytes 8388608
  189.3 6.5 %slice-start.1 = ((s8[8388608]{0:T(1024)(128)(4,1)}), s8[4194304]{0:T(1024)(128)(4,1)S(1)}, s32[]{:S(2)}) async-start(s8[8388608]{0:T(1024)(128)(4,1)} %bitcast.144), calls=%async_computation.7 | async-start | bytes 8388608
  195.7 2.2 copy-start.11
  208.6 146.3 %all-to-all-start.1 = ((bf16[32,2,2176]{2,1,0:T(2,128)(2,1)}), bf16[32,2,2176]{2,1,0:T(2,128)(2,1)S(1)}, u32[]{:S(2)}, u32[]{:S(2)}) async-start(bf16[32,2,2176]{2,1,0:T(2,128)(2,1)} %pad_maximum_fusion.3), calls=%async_computation.1 | async-start | bytes 557056 | tf_op jit(solution)/shard_map/all_to_all | solution.py:277
  222.4 5.2 %copy-start.1 = (bf16[2,8,64,2048]{3,2,1,0:T(8,128)(2,1)S(1)}, bf16[2,8,64,2048]{3,2,1,0:T(8,128)(2,1)}, u32[]{:S(2)}) copy-start(bf16[2,8,64,2048]{3,2,1,0:T(8,128)(2,1)} %fusion.2) | copy-start | bytes 12582916
  222.4 5.1 %copy-start.7 = (bf16[2,64,2048]{2,1,0:T(8,128)(2,1)S(1)}, bf16[2,64,2048]{2,1,0:T(8,128)(2,1)}, u32[]{:S(2)}) copy-start(bf16[2,64,2048]{2,1,0:T(8,128)(2,1)} %param.12) | copy-start | bytes 1572868
  242.3 110.1 %copy-start.6 = (bf16[2,8,8,8,256]{4,3,2,1,0:T(8,128)(2,1)S(1)}, bf16[2,8,8,8,256]{4,3,2,1,0:T(8,128)(2,1)}, u32[]{:S(2)}) copy-start(bf16[2,8,8,8,256]{4,3,2,1,0:T(8,128)(2,1)} %get-tuple-element.55) | copy-start | bytes 1572868
Sparse Core Ops, SparseCore 0:
  10.8 94.0 all-gather.2
  108.5 62.9 all-gather.4
  184.6 89.6 reduce-scatter.3

commit v6 on v5

--- a/solution.py
+++ b/solution.py
@@ -271,7 +271,10 @@
     gate_proj_grad = summed[:, :hidden_width][None]
     up_proj_grad = summed[:, hidden_width : 2 * hidden_width][None]
     down_proj_grad = jnp.transpose(summed[:, 2 * hidden_width :])[None]
-    pair_total = pair_return(pair_buffer)
+    chunks = 4
+    pair_total = pair_return(
+        pair_buffer.reshape(devices, chunks, seq_count * shard_len // chunks, 2 * HEAD)
+    ).reshape(seq_count, shard_len, 2 * HEAD)
     key_grad = pair_total[:, :, :HEAD]
     value_grad = pair_total[:, :, HEAD:]
     back_all = lax.all_to_all(

time: 368 us -> 363 us (0.986)
  Pallas kernels: 110 us -> 105 us
    pallas_call x1, Pallas kernels: 110 us -> 105 us  [pair_return(): pl.pallas_call(pair_chain_kernel, out_shape=jax.ShapeDtypeStruct(pair_buf...]
    reshape x1 -> x0, local copies, waits for them, and re-layouts: 4.69 us -> none  [shards(): jnp.concatenate([key_part, value_part], axis=2)]
    transpose x0 -> x1, local copies, waits for them, and re-layouts: none -> 4.69 us  [shards(): jnp.moveaxis(jnp.concatenate([key_part, value_part], axis=2).reshape(seq_...]
  transfers between devices with their start and end apart: 5 -> 5, of which waited for: 3 -> 3; matrix products, arithmetic and copies ran while one was open for 18% -> 18% of each run, Pallas kernels for 30% -> 29%
where the time goes in v6:
time: 363 us; the launch traced here: 362 us
  waiting for transfers between devices  129 us (36%)
  Pallas kernels  105 us (29%)
  matrix products  38.9 us (11%)
  starting transfers between devices  30.9 us (9%)
  local copies, waits for them, and re-layouts  24.2 us (7%)
  other arithmetic  19.7 us (5%)
  between operations  14.2 us (4%)
    pallas_call x1, Pallas kernels, pair_return(): pl.pallas_call(pair_chain_kernel, out_shape=jax.ShapeDtypeStruct(pair_buf...  105 us
    all_gather x1, waiting for transfers between devices, shards(): weight_full = lax.all_gather(weight_cat, 'dp', axis=1, tiled=True)[0]  56.4 us
    all_to_all x1, waiting for transfers between devices, shards(): lax.all_to_all(send_all, 'expert', split_axis=0, concat_axis=0, tiled=True)  39 us
    all_gather x1, waiting for transfers between devices, shards(): gathered = lax.all_gather(packed, 'expert', axis=1, tiled=True)  33.4 us
    all_to_all x1, starting transfers between devices, shards(): lax.all_to_all(send_all, 'expert', split_axis=0, concat_axis=0, tiled=True)  16.8 us
    all_to_all x1, starting transfers between devices, shards(): lax.all_to_all(jnp.concatenate([input_rows.reshape(devices, CAP, model_wi...  13.9 us
    unnamed x35, local copies, waits for them, and re-layouts  7.69 us
  transfers between devices with their start and end apart: 5, of which 3 were waited for; matrix products, arithmetic and copies ran while one was open for 18% of the time, Pallas kernels for 29%

profile of v6, /device:TPU:1, one launch (start us, length us, event | category | flops | bytes accessed | tf_op | source)
XLA Modules:
  0.0 362.1 jit_solution(1439806640315183016)
XLA Ops:
  7.3 1.6 pad_maximum_fusion.5
  9.0 0.7 fusion.79
  9.7 0.7 select_reduce_fusion.1
  10.4 0.2 fusion.30
  10.7 0.2 convolution_convert_fusion.3
  11.0 0.2 reshape.199
  11.2 1.3 convolution_convert_fusion.4
  12.4 0.2 reshape.198
  12.6 0.7 select_reduce_fusion
  13.3 0.1 fusion.54
  13.4 1.3 pad_maximum_fusion.2
  14.7 16.8 %all-to-all-start = ((bf16[32,2,4224]{2,1,0:T(2,128)(2,1)}), bf16[32,2,4224]{2,1,0:T(2,128)(2,1)S(1)}, u32[]{:S(2)}, u32[]{:S(2)}) async-start(bf16[32,2,4224]{2,1,0:T(2,128)(2,1)} %pad_maximum_fusion.2), calls=%async_computation | async-start | bytes 1081344 | tf_op jit(solution)/shard_map/all_to_all | solution.py:165
  31.5 0.1 copy.72
  31.7 0.1 copy.71
  31.8 0.7 pad_maximum_fusion.4
  32.5 39.0 %all-to-all-done = bf16[32,2,4224]{2,1,0:T(2,128)(2,1)S(1)} async-done(((bf16[32,2,4224]{2,1,0:T(2,128)(2,1)}), bf16[32,2,4224]{2,1,0:T(2,128)(2,1)S(1)}, u32[]{:S(2)}, u32[]{:S(2)}) %all-to-all-start) | async-done | bytes 540704 | tf_op jit(solution)/shard_map/all_to_all | solution.py:165
  71.5 33.4 %all-gather.3.cloned.1.call-done = bf16[2,2048,512]{2,1,0:T(8,128)(2,1)} async-done(((bf16[2,64,512]{2,1,0:T(8,128)(2,1)}), bf16[2,2048,512]{2,1,0:T(8,128)(2,1)}) %all-gather.3.cloned.1.call-update) | async-done | bytes 4194320 | tf_op jit(solution)/shard_map/all_gather | solution.py:121
  104.9 0.2 reduce-scatter.4.cloned.1.call-start
  105.2 1.1 reshape.211
  106.3 0.1 iota_compare_fusion
  106.5 1.3 add_divide_fusion
  107.7 0.4 fusion.80
  108.1 0.4 reshape.214
  108.5 0.1 reshape.209
  108.6 0.1 convert_reduce_fusion
  108.7 0.1 reshape.213
  108.8 6.3 %fusion.5 = (f32[2,8,64]{2,1,0:T(8,128)S(1)}, f32[2,2048,64,8]{1,2,3,0:T(8,128)}) fusion(pred[64,2048]{1,0:T(8,128)(4,1)S(1)} %iota_compare_fusion, bf16[2,8,8,8,256]{4,3,2,1,0:T(8,128)(2,1)} %bitcast.158, bf16[2,2048,512]{2,1,0:T(8,128)(2,1)} %all-gather.3.cloned.1.call-done), kind=kOutput, calls=%fused_computation.9 | convolution fusion | flops 1080032256 | bytes 11145216 | tf_op jit(solution)/shard_map/sphd,srd->shpr/dot_general | solution.py:177
  115.1 56.4 %all-gather.5.cloned.1.call-done = bf16[1,2048,768]{1,2,0:T(8,128)(2,1)} async-done(((bf16[1,128,768]{1,2,0:T(8,128)(2,1)}), bf16[1,2048,768]{1,2,0:T(8,128)(2,1)}) %all-gather.5.cloned.1.call-update) | async-done | bytes 3145744 | tf_op jit(solution)/shard_map/all_gather | solution.py:170
  171.5 1.7 fusion.36
  173.2 1.7 fusion.39
  174.8 1.7 multiply_convert_fusion.2
  176.5 0.5 convolution_convert_fusion
  177.0 0.5 convolution_convert_fusion.1
  177.5 0.5 convolution_convert_fusion.2
  178.0 1.8 pad_maximum_fusion.1
  179.8 4.7 %copy.94 = bf16[2048,768]{1,0:T(8,128)(2,1)} copy(bf16[2048,768]{0,1:T(8,128)(2,1)} %pad_maximum_fusion.1) | data formatting | bytes 6291456
  184.5 4.7 %exponential_reduce_fusion = f32[2,8,64]{2,1,0:T(8,128)S(1)} fusion(f32[2,2048,64,8]{1,2,3,0:T(8,128)} %get-tuple-element.67, f32[2,8,64]{2,1,0:T(8,128)S(1)} %get-tuple-element.66, pred[64,2048]{1,0:T(8,128)(4,1)S(1)} %iota_compare_fusion), kind=kLoop, calls=%fused_computation.8 | loop fusion | flops 8387584 | bytes 8527872 | tf_op jit(solution)/shard_map/reduce_sum | solution.py:185
  189.3 6.5 %multiply_reduce_fusion = (f32[2,64,8]{1,2,0:T(8,128)S(1)}, bf16[2,64,8,256]{3,1,2,0:T(8,128)(2,1)S(1)}, bf16[2,8,8,8,256]{4,3,2,1,0:T(8,128)(2,1)}) fusion(f32[2,8,8,8,256]{4,3,2,1,0:T(8,128)S(1)} %bitcast.154, f32[2,8,8,8,256]{4,3,2,1,0:T(8,128)S(1)} %bitcast.153, f32[2,2048,64,8]{1,2,3,0:T(8,128)} %get-tuple-element.67, ...), kind=kOutput, calls=%fused_computation.49 | convolution fusion | flops 1084750848 | bytes 13770752 | tf_op jit(solution)/shard_map/shpr,srd->sphd/dot_general | solution.py:188
  195.7 2.2 bitcast_convert_fusion
  197.9 4.5 %fusion.2 = bf16[2,8,64,2048]{3,2,1,0:T(8,128)(2,1)} fusion(f32[2,2048,64,8]{1,2,3,0:T(8,128)S(1)} %bitcast.146, bf16[2,64,8,256]{3,1,2,0:T(8,128)(2,1)S(1)} %get-tuple-element.52, f32[2,8,64]{2,1,0:T(8,128)S(1)} %bitcast.161, f32[2,8,64]{2,1,0:T(8,128)S(1)} %log_add_fusion, pred[64,2048]{1,0:T(8,128)(4,1)S(1)} %iota_compare_fusion, ...), kind=kOutput, calls=%fused_computation.3 | convolution fusion | flops 1088421888 | bytes 15351808 | tf_op jit(solution)/shard_map/sphd,srd->shpr/dot_general | solution.py:202
  202.4 1.6 fusion.29
  204.1 0.1 convert_element_type.153
  204.2 1.5 fusion.34
  205.7 1.5 fusion.8
  207.3 0.2 reshape.210
  207.6 1.0 pad_maximum_fusion.3
  208.6 13.9 %all-to-all-start.1 = ((bf16[32,2,2176]{2,1,0:T(2,128)(2,1)}), bf16[32,2,2176]{2,1,0:T(2,128)(2,1)S(1)}, u32[]{:S(2)}, u32[]{:S(2)}) async-start(bf16[32,2,2176]{2,1,0:T(2,128)(2,1)} %pad_maximum_fusion.3), calls=%async_computation.1 | async-start | bytes 557056 | tf_op jit(solution)/shard_map/all_to_all | solution.py:280
  222.5 4.3 %fusion.26 = bf16[2,8,8,8,256]{4,3,2,1,0:T(8,128)(2,1)S(1)} fusion(bf16[2,8,64,2048]{3,2,1,0:T(8,128)(2,1)} %fusion.2, bf16[2,2048,512]{2,1,0:T(8,128)(2,1)} %all-gather.3.cloned.1.call-done), kind=kOutput, calls=%fused_computation.38 | convolution fusion | flops 1074003968 | bytes 6815744 | tf_op jit(solution)/shard_map/shpr,srd->sphd/dot_general | solution.py:208
  226.7 0.8 copy.101
  227.6 1.3 bitcast_convert_fusion.1
  228.9 2.5 pad_maximum_fusion
  231.4 6.2 %copy.78 = bf16[2,2048,512]{2,1,0:T(8,128)(2,1)} copy(bf16[2,2048,512]{1,2,0:T(8,128)(2,1)} %pad_maximum_fusion) | data formatting | bytes 8388608 | tf_op jit(solution)/shard_map/concatenate | solution.py:219
  237.7 4.7 %copy.79 = bf16[32,2,64,512]{3,2,1,0:T(8,128)(2,1)} copy(bf16[32,2,64,512]{3,2,0,1:T(8,128)(2,1)} %bitcast.143) | data formatting | bytes 8388608 | tf_op jit(solution)/shard_map/transpose | solution.py:218
  242.3 105.2 %shard_map.187 = bf16[4,32,512]{2,1,0:T(8,128)(2,1)} custom-call(bf16[32,4,32,512]{3,2,1,0:T(8,128)(2,1)} %bitcast.144), custom_call_target="tpu_custom_call" | custom-call | tf_op jit(solution)/shard_map/pallas_call | solution.py:83
  347.6 0.8 copy.102
  348.4 1.5 fusion.81
  350.2 0.2 slice.65
  350.3 0.1 multiply_reduce_fusion.1
  350.5 0.6 select_convert_fusion
  351.1 1.1 fusion.7
  352.2 1.1 copy.95
  353.3 0.7 slice_bitcast_fusion
  354.0 0.8 copy.88
  354.8 0.8 copy.89
  (49 shorter events, 0.7 us)
Async XLA Ops:
  7.2 3.6 copy-start
  7.2 24.3 %copy-start.8 = (bf16[1,128,256]{2,1,0:T(8,128)(2,1)S(1)}, bf16[1,128,256]{2,1,0:T(8,128)(2,1)}, u32[]{:S(2)}) copy-start(bf16[1,128,256]{2,1,0:T(8,128)(2,1)} %param.22) | copy-start | bytes 196612
  7.2 24.5 %copy-start.9 = (bf16[1,128,256]{2,1,0:T(8,128)(2,1)S(1)}, bf16[1,128,256]{2,1,0:T(8,128)(2,1)}, u32[]{:S(2)}) copy-start(bf16[1,128,256]{2,1,0:T(8,128)(2,1)} %param.21) | copy-start | bytes 196612
  7.2 24.6 %copy-start.10 = (bf16[1,256,128]{2,1,0:T(8,128)(2,1)S(1)}, bf16[1,256,128]{2,1,0:T(8,128)(2,1)}, u32[]{:S(2)}) copy-start(bf16[1,256,128]{2,1,0:T(8,128)(2,1)} %param.23) | copy-start | bytes 196612
  7.2 98.0 %copy-start.4 = (bf16[2,64,2048]{2,1,0:T(8,128)(2,1)S(1)}, bf16[2,64,2048]{2,1,0:T(8,128)(2,1)}, u32[]{:S(2)}) copy-start(bf16[2,64,2048]{2,1,0:T(8,128)(2,1)} %param.16) | copy-start | bytes 1572868
  7.2 99.2 %copy-start.5 = (bf16[2,64,2048]{2,1,0:T(8,128)(2,1)S(1)}, bf16[2,64,2048]{2,1,0:T(8,128)(2,1)}, u32[]{:S(2)}) copy-start(bf16[2,64,2048]{2,1,0:T(8,128)(2,1)} %param.15) | copy-start | bytes 1572868
  7.2 97.7 %all-gather.3.cloned.1.call-start = ((), (), s32[]{:S(2)}) async-start(), calls=%async_computation.3 | async-start | bytes 4325376 | tf_op jit(solution)/shard_map/all_gather | solution.py:121
  14.7 56.8 %all-to-all-start = ((bf16[32,2,4224]{2,1,0:T(2,128)(2,1)}), bf16[32,2,4224]{2,1,0:T(2,128)(2,1)S(1)}, u32[]{:S(2)}, u32[]{:S(2)}) async-start(bf16[32,2,4224]{2,1,0:T(2,128)(2,1)} %pad_maximum_fusion.2), calls=%async_computation | async-start | bytes 1081344 | tf_op jit(solution)/shard_map/all_to_all | solution.py:165
  31.5 140.0 %all-gather.5.cloned.1.call-start = ((), (), s32[]{:S(2)}) async-start(), calls=%async_computation.4 | async-start | bytes 3342336 | tf_op jit(solution)/shard_map/all_gather | solution.py:170
  104.9 247.3 %reduce-scatter.4.cloned.1.call-start = ((), (), s32[]{:S(2)}) async-start(), calls=%async_computation.5 | async-start | bytes 3342336
  184.5 4.7 %copy-start.2 = (f32[2,64,2048]{2,1,0:T(8,128)S(1)}, f32[2,64,2048]{2,1,0:T(8,128)}, u32[]{:S(2)}) copy-start(f32[2,64,2048]{2,1,0:T(8,128)} %reshape.211) | copy-start | bytes 3145732
  184.5 4.7 %copy-start.3 = (f32[2,64,2048]{2,1,0:T(8,128)S(1)}, f32[2,64,2048]{2,1,0:T(8,128)}, u32[]{:S(2)}) copy-start(f32[2,64,2048]{2,1,0:T(8,128)} %add_divide_fusion) | copy-start | bytes 3145732
  184.5 11.2 %slice-start = ((s8[8388608]{0:T(1024)(128)(4,1)}), s8[4194304]{0:T(1024)(128)(4,1)S(1)}, s32[]{:S(2)}) async-start(s8[8388608]{0:T(1024)(128)(4,1)} %bitcast.145), calls=%async_computation.6 | async-start | bytes 8388608
  189.3 6.5 %slice-start.1 = ((s8[8388608]{0:T(1024)(128)(4,1)}), s8[4194304]{0:T(1024)(128)(4,1)S(1)}, s32[]{:S(2)}) async-start(s8[8388608]{0:T(1024)(128)(4,1)} %bitcast.145), calls=%async_computation.7 | async-start | bytes 8388608
  195.7 2.2 copy-start.11
  208.6 141.4 %all-to-all-start.1 = ((bf16[32,2,2176]{2,1,0:T(2,128)(2,1)}), bf16[32,2,2176]{2,1,0:T(2,128)(2,1)S(1)}, u32[]{:S(2)}, u32[]{:S(2)}) async-start(bf16[32,2,2176]{2,1,0:T(2,128)(2,1)} %pad_maximum_fusion.3), calls=%async_computation.1 | async-start | bytes 557056 | tf_op jit(solution)/shard_map/all_to_all | solution.py:280
  222.4 5.2 %copy-start.1 = (bf16[2,8,64,2048]{3,2,1,0:T(8,128)(2,1)S(1)}, bf16[2,8,64,2048]{3,2,1,0:T(8,128)(2,1)}, u32[]{:S(2)}) copy-start(bf16[2,8,64,2048]{3,2,1,0:T(8,128)(2,1)} %fusion.2) | copy-start | bytes 12582916
  222.4 5.1 %copy-start.7 = (bf16[2,64,2048]{2,1,0:T(8,128)(2,1)S(1)}, bf16[2,64,2048]{2,1,0:T(8,128)(2,1)}, u32[]{:S(2)}) copy-start(bf16[2,64,2048]{2,1,0:T(8,128)(2,1)} %param.12) | copy-start | bytes 1572868
  242.3 105.2 %copy-start.6 = (bf16[2,8,8,8,256]{4,3,2,1,0:T(8,128)(2,1)S(1)}, bf16[2,8,8,8,256]{4,3,2,1,0:T(8,128)(2,1)}, u32[]{:S(2)}) copy-start(bf16[2,8,8,8,256]{4,3,2,1,0:T(8,128)(2,1)} %get-tuple-element.55) | copy-start | bytes 1572868
Sparse Core Ops, SparseCore 0:
  10.8 94.0 all-gather.2
  108.5 62.9 all-gather.4
  184.6 89.6 reduce-scatter.3

commit v7 on v6

--- a/solution.py
+++ b/solution.py
@@ -118,7 +118,6 @@
     score_scale = HEAD ** (-0.5)
     queries = query_rows.reshape(seq_count, shard_len, HEADS, HEAD)
     packed = jnp.concatenate([key_rows, value_rows], axis=2)
-    gathered = lax.all_gather(packed, "expert", axis=1, tiled=True)
 
     token_count, model_width = moe_input.shape
     live_slot = routes < devices
@@ -163,11 +162,12 @@
         [gate_proj, up_proj, jnp.transpose(down_proj, (0, 2, 1))], axis=2
     )
     recv_all = lax.all_to_all(send_all, "expert", split_axis=0, concat_axis=0, tiled=True)
-    gathered, recv_all, weight_cat = lax.optimization_barrier((gathered, recv_all, weight_cat))
+    weight_full = lax.all_gather(weight_cat, "dp", axis=1, tiled=True)[0]
+    packed, recv_all = lax.optimization_barrier((packed, recv_all))
+    gathered = lax.all_gather(packed, "expert", axis=1, tiled=True)
     rows_in = recv_all[:, :, :model_cols]
     grads_in = recv_all[:, :, model_cols : 2 * model_cols]
     weights_in = recv_all[:, :, 2 * model_cols]
-    weight_full = lax.all_gather(weight_cat, "dp", axis=1, tiled=True)[0]
     gate_mat = weight_full[:, :hidden_cols]
     up_mat = weight_full[:, hidden_cols : 2 * hidden_cols]
     down_mat = jnp.transpose(weight_full[:, 2 * hidden_cols :])
@@ -249,8 +249,7 @@
     ).astype(jnp.bfloat16)
     hidden_width = hidden.shape[1]
     contract_first = (((0,), (0,)), ((), ()))
-    summed = lax.psum_scatter(
-        jnp.concatenate(
+    group_cat = jnp.concatenate(
             [
                 lax.dot_general(
                     flat_rows, gate_rows, contract_first, preferred_element_type=jnp.float32
@@ -263,11 +262,11 @@
                 ),
             ],
             axis=1,
-        ).astype(jnp.bfloat16),
-        "dp",
-        scatter_dimension=0,
-        tiled=True,
-    ).astype(jnp.float32)
+        ).astype(jnp.bfloat16)
+    gathered, group_cat = lax.optimization_barrier((gathered, group_cat))
+    summed = lax.psum_scatter(group_cat, "dp", scatter_dimension=0, tiled=True).astype(
+        jnp.float32
+    )
     gate_proj_grad = summed[:, :hidden_width][None]
     up_proj_grad = summed[:, hidden_width : 2 * hidden_width][None]
     down_proj_grad = jnp.transpose(summed[:, 2 * hidden_width :])[None]

time: 363 us -> 330 us (0.909)
  waiting for transfers between devices: 129 us -> 106 us
  matrix products: 38.9 us -> 29.9 us
  other arithmetic: 19.7 us -> 15.9 us
    all_gather x1, waiting for transfers between devices: 56.4 us -> 15 us  [shards(): weight_full = lax.all_gather(weight_cat, 'dp', axis=1, tiled=True)[0]]
    all_gather x1, waiting for transfers between devices: 33.4 us -> 57.8 us  [shards(): gathered = lax.all_gather(packed, 'expert', axis=1, tiled=True)]
    all_to_all x1, waiting for transfers between devices: 39 us -> 33.5 us  [shards(): lax.all_to_all(send_all, 'expert', split_axis=0, concat_axis=0, tiled=True)]
    dot_general x1, matrix products: 6.45 us -> 2.06 us  [shards(): jnp.einsum('shpr,srd->sphd', probs_low, values_all, preferred_element_typ...]
    unnamed x35 -> x27, local copies, waits for them, and re-layouts: 7.69 us -> 9.62 us
  transfers between devices with their start and end apart: 5 -> 5, of which waited for: 3 -> 3; matrix products, arithmetic and copies ran while one was open for 18% -> 19% of each run, Pallas kernels for 29% -> 32%
where the time goes in v7:
time: 330 us; the launch traced here: 328 us
  waiting for transfers between devices  106 us (32%)
  Pallas kernels  106 us (32%)
  starting transfers between devices  30.9 us (9%)
  matrix products  29.9 us (9%)
  local copies, waits for them, and re-layouts  25.3 us (8%)
  other arithmetic  15.9 us (5%)
  between operations  14.2 us (4%)
    pallas_call x1, Pallas kernels, pair_return(): pl.pallas_call(pair_chain_kernel, out_shape=jax.ShapeDtypeStruct(pair_buf...  106 us
    all_gather x1, waiting for transfers between devices, shards(): gathered = lax.all_gather(packed, 'expert', axis=1, tiled=True)  57.8 us
    all_to_all x1, waiting for transfers between devices, shards(): lax.all_to_all(send_all, 'expert', split_axis=0, concat_axis=0, tiled=True)  33.5 us
    all_to_all x1, starting transfers between devices, shards(): lax.all_to_all(send_all, 'expert', split_axis=0, concat_axis=0, tiled=True)  16.7 us
    all_gather x1, waiting for transfers between devices, shards(): weight_full = lax.all_gather(weight_cat, 'dp', axis=1, tiled=True)[0]  15 us
    all_to_all x1, starting transfers between devices, shards(): lax.all_to_all(jnp.concatenate([input_rows.reshape(devices, CAP, model_wi...  13.9 us
    unnamed x27, local copies, waits for them, and re-layouts  9.62 us
  transfers between devices with their start and end apart: 5, of which 3 were waited for; matrix products, arithmetic and copies ran while one was open for 19% of the time, Pallas kernels for 32%

profile of v7, /device:TPU:1, one launch (start us, length us, event | category | flops | bytes accessed | tf_op | source)
XLA Modules:
  0.0 328.5 jit_solution(16653120295628429074)
XLA Ops:
  7.3 1.0 copy.82
  8.3 1.0 copy.83
  9.3 1.5 pad_maximum_fusion.4
  10.8 0.7 fusion.65
  11.6 0.7 select_reduce_fusion.1
  12.3 0.2 fusion.16
  12.6 0.2 convolution_convert_fusion.3
  12.8 0.2 reshape.199
  13.0 1.3 convolution_convert_fusion.4
  14.3 0.2 reshape.198
  14.5 0.7 select_reduce_fusion
  15.2 0.1 fusion.40
  15.3 1.3 pad_maximum_fusion.2
  16.6 16.7 %all-to-all-start = ((bf16[32,2,4224]{2,1,0:T(2,128)(2,1)}), bf16[32,2,4224]{2,1,0:T(2,128)(2,1)S(1)}, u32[]{:S(2)}, u32[]{:S(2)}) async-start(bf16[32,2,4224]{2,1,0:T(2,128)(2,1)} %pad_maximum_fusion.2), calls=%async_computation | async-start | bytes 1081344 | tf_op jit(solution)/shard_map/all_to_all | solution.py:164
  33.4 0.7 pad_maximum_fusion.5
  34.1 33.5 %all-to-all-done = bf16[32,2,4224]{2,1,0:T(2,128)(2,1)S(1)} async-done(((bf16[32,2,4224]{2,1,0:T(2,128)(2,1)}), bf16[32,2,4224]{2,1,0:T(2,128)(2,1)S(1)}, u32[]{:S(2)}, u32[]{:S(2)}) %all-to-all-start) | async-done | bytes 540704 | tf_op jit(solution)/shard_map/all_to_all | solution.py:164
  67.6 0.3 add_divide_fusion
  67.9 0.1 convert_reduce_fusion
  68.0 0.1 reshape.213
  68.1 0.4 fusion.66
  68.6 0.4 reshape.214
  69.0 15.0 %all-gather.5.cloned.1.call-done = bf16[1,2048,768]{1,2,0:T(8,128)(2,1)} async-done(((bf16[1,128,768]{1,2,0:T(8,128)(2,1)}), bf16[1,2048,768]{1,2,0:T(8,128)(2,1)}) %all-gather.5.cloned.1.call-update) | async-done | bytes 3145744 | tf_op jit(solution)/shard_map/all_gather | solution.py:165
  84.0 1.7 fusion.22
  85.6 1.7 fusion.25
  87.3 1.7 multiply_convert_fusion.2
  89.0 1.6 fusion.15
  90.6 0.1 convert_element_type.153
  90.7 1.5 fusion.20
  92.3 1.5 fusion.8
  93.8 0.2 reshape.210
  94.1 1.0 pad_maximum_fusion.3
  95.1 13.9 %all-to-all-start.1 = ((bf16[32,2,2176]{2,1,0:T(2,128)(2,1)}), bf16[32,2,2176]{2,1,0:T(2,128)(2,1)S(1)}, u32[]{:S(2)}, u32[]{:S(2)}) async-start(bf16[32,2,2176]{2,1,0:T(2,128)(2,1)} %pad_maximum_fusion.3), calls=%async_computation.1 | async-start | bytes 557056 | tf_op jit(solution)/shard_map/all_to_all | solution.py:279
  109.0 0.2 reduce-scatter.4.cloned.1.call-start
  109.2 0.5 convolution_convert_fusion.1
  109.7 0.5 convolution_convert_fusion.2
  110.1 0.5 convolution_convert_fusion
  110.6 1.9 pad_maximum_fusion.1
  112.5 57.8 %all-gather.3.cloned.1.call-done = bf16[2,2048,512]{2,1,0:T(8,128)(2,1)} async-done(((bf16[2,64,512]{2,1,0:T(8,128)(2,1)}), bf16[2,2048,512]{2,1,0:T(8,128)(2,1)}) %all-gather.3.cloned.1.call-update) | async-done | bytes 4194320 | tf_op jit(solution)/shard_map/all_gather | solution.py:167
  170.3 4.6 %copy.94 = bf16[2048,768]{1,0:T(8,128)(2,1)} copy(bf16[2048,768]{0,1:T(8,128)(2,1)} %pad_maximum_fusion.1) | data formatting | bytes 6291456
  175.0 0.1 iota_compare_fusion
  175.1 1.1 reshape.211
  176.4 0.2 slice.67
  176.6 0.1 multiply_reduce_fusion.1
  176.7 0.6 select_convert_fusion
  177.3 1.1 fusion.7
  178.5 3.1 fusion.5
  181.6 2.2 exponential_reduce_fusion
  183.9 0.3 copy-done.9
  184.1 2.1 multiply_reduce_fusion
  186.2 0.8 copy.102
  187.0 3.2 fusion.2
  190.2 1.3 bitcast_convert_fusion.1
  191.6 2.2 bitcast_convert_fusion
  193.7 2.3 pad_maximum_fusion
  196.0 6.3 %copy.76 = bf16[2,2048,512]{2,1,0:T(8,128)(2,1)} copy(bf16[2,2048,512]{1,2,0:T(8,128)(2,1)} %pad_maximum_fusion) | data formatting | bytes 8388608 | tf_op jit(solution)/shard_map/concatenate | solution.py:219
  202.3 4.7 %copy.77 = bf16[32,2,64,512]{3,2,1,0:T(8,128)(2,1)} copy(bf16[32,2,64,512]{3,2,0,1:T(8,128)(2,1)} %bitcast.141) | data formatting | bytes 8388608 | tf_op jit(solution)/shard_map/transpose | solution.py:218
  207.0 106.0 %shard_map.187 = bf16[4,32,512]{2,1,0:T(8,128)(2,1)} custom-call(bf16[32,4,32,512]{3,2,1,0:T(8,128)(2,1)} %bitcast.142), custom_call_target="tpu_custom_call" | custom-call | tf_op jit(solution)/shard_map/pallas_call | solution.py:83
  313.0 4.1 %fusion.14 = bf16[2,8,8,8,256]{4,3,2,1,0:T(8,128)(2,1)S(1)} fusion(bf16[2,8,64,2048]{3,2,1,0:T(8,128)(2,1)} %copy-done.1, bf16[2,2048,512]{2,1,0:T(8,128)(2,1)} %all-gather.3.cloned.1.call-done), kind=kOutput, calls=%fused_computation.32 | convolution fusion | flops 1074003968 | bytes 6815744 | tf_op jit(solution)/shard_map/shpr,srd->sphd/dot_general | solution.py:208
  317.1 0.8 copy.101
  318.0 0.7 fusion.67
  318.6 1.1 copy.95
  319.7 0.7 slice_bitcast_fusion.12
  320.4 0.8 copy.89
  321.2 0.8 copy.88
  (40 shorter events, 0.8 us)
Async XLA Ops:
  7.2 5.4 %copy-start = (bf16[128,2048]{1,0:T(8,128)(2,1)S(1)}, bf16[128,2048]{1,0:T(8,128)(2,1)}, u32[]{:S(2)}) copy-start(bf16[128,2048]{1,0:T(8,128)(2,1)} %param.18) | copy-start | bytes 1572868
  7.2 26.2 %copy-start.7 = (bf16[2,64,256]{2,1,0:T(8,128)(2,1)S(1)}, bf16[2,64,256]{2,1,0:T(8,128)(2,1)}, u32[]{:S(2)}) copy-start(bf16[2,64,256]{2,1,0:T(8,128)(2,1)} %param.14) | copy-start | bytes 196612
  7.2 26.2 %copy-start.8 = (bf16[2,64,256]{2,1,0:T(8,128)(2,1)S(1)}, bf16[2,64,256]{2,1,0:T(8,128)(2,1)}, u32[]{:S(2)}) copy-start(bf16[2,64,256]{2,1,0:T(8,128)(2,1)} %param.13) | copy-start | bytes 196612
  7.2 60.4 %copy-start.3 = (bf16[2,64,2048]{2,1,0:T(8,128)(2,1)S(1)}, bf16[2,64,2048]{2,1,0:T(8,128)(2,1)}, u32[]{:S(2)}) copy-start(bf16[2,64,2048]{2,1,0:T(8,128)(2,1)} %param.15) | copy-start | bytes 1572868
  7.2 76.7 %all-gather.5.cloned.1.call-start = ((), (), s32[]{:S(2)}) async-start(), calls=%async_computation.4 | async-start | bytes 3342336 | tf_op jit(solution)/shard_map/all_gather | solution.py:165
  16.6 51.0 %all-to-all-start = ((bf16[32,2,4224]{2,1,0:T(2,128)(2,1)}), bf16[32,2,4224]{2,1,0:T(2,128)(2,1)S(1)}, u32[]{:S(2)}, u32[]{:S(2)}) async-start(bf16[32,2,4224]{2,1,0:T(2,128)(2,1)} %pad_maximum_fusion.2), calls=%async_computation | async-start | bytes 1081344 | tf_op jit(solution)/shard_map/all_to_all | solution.py:164
  33.3 136.9 %all-gather.3.cloned.1.call-start = ((), (), s32[]{:S(2)}) async-start(), calls=%async_computation.3 | async-start | bytes 4325376 | tf_op jit(solution)/shard_map/all_gather | solution.py:167
  95.1 81.1 %all-to-all-start.1 = ((bf16[32,2,2176]{2,1,0:T(2,128)(2,1)}), bf16[32,2,2176]{2,1,0:T(2,128)(2,1)S(1)}, u32[]{:S(2)}, u32[]{:S(2)}) async-start(bf16[32,2,2176]{2,1,0:T(2,128)(2,1)} %pad_maximum_fusion.3), calls=%async_computation.1 | async-start | bytes 557056 | tf_op jit(solution)/shard_map/all_to_all | solution.py:279
  109.0 209.7 %reduce-scatter.4.cloned.1.call-start = ((), (), s32[]{:S(2)}) async-start(), calls=%async_computation.5 | async-start | bytes 3342336
  112.5 62.6 %copy-start.4 = (bf16[2,64,2048]{2,1,0:T(8,128)(2,1)S(1)}, bf16[2,64,2048]{2,1,0:T(8,128)(2,1)}, u32[]{:S(2)}) copy-start(bf16[2,64,2048]{2,1,0:T(8,128)(2,1)} %param.16) | copy-start | bytes 1572868
  181.6 2.3 copy-start.2
  181.6 2.5 copy-start.9
  187.0 3.2 copy-start.6
  190.2 3.5 %copy-start.1 = (bf16[2,8,64,2048]{3,2,1,0:T(8,128)(2,1)}, bf16[2,8,64,2048]{3,2,1,0:T(8,128)(2,1)S(1)}, u32[]{:S(2)}) copy-start(bf16[2,8,64,2048]{3,2,1,0:T(8,128)(2,1)S(1)} %fusion.2) | copy-start | bytes 12582916
  313.0 5.0 %copy-start.5 = (bf16[4,32,512]{2,1,0:T(8,128)(2,1)S(1)}, bf16[4,32,512]{2,1,0:T(8,128)(2,1)}, u32[]{:S(2)}) copy-start(bf16[4,32,512]{2,1,0:T(8,128)(2,1)} %shard_map.187) | copy-start | bytes 393220
Sparse Core Ops, SparseCore 0:
  11.6 72.2 all-gather.4
  86.7 83.5 all-gather.2
  175.1 83.6 reduce-scatter.3

commit v8 on v7

--- a/solution.py
+++ b/solution.py
@@ -12,7 +12,10 @@
 
 
 def pair_chain_kernel(parts_ref, out_ref, sendbuf, recvbuf, send_sems, recv_sems):
-    devices, seqs = parts_ref.shape[0], parts_ref.shape[1]
+    devices, chunks, rows = sendbuf.shape[0], sendbuf.shape[1], sendbuf.shape[2]
+    seqs = parts_ref.shape[0]
+    pieces = chunks // seqs
+    block_rows = rows * pieces
     me = lax.axis_index("expert")
     row = lax.axis_index("dp")
     mesh_ids = pl.DeviceIdType.MESH
@@ -21,75 +24,85 @@
     upper = lax.rem(me + 1, devices)
     lower = lax.rem(me + devices - 1, devices)
 
-    def link(block, seq, peer):
+    def link(block, chunk, peer):
         return pltpu.make_async_remote_copy(
-            src_ref=sendbuf.at[block, seq],
-            dst_ref=recvbuf.at[block, seq],
-            send_sem=send_sems.at[block, seq],
-            recv_sem=recv_sems.at[block, seq],
+            src_ref=sendbuf.at[block, chunk],
+            dst_ref=recvbuf.at[block, chunk],
+            send_sem=send_sems.at[block, chunk],
+            recv_sem=recv_sems.at[block, chunk],
             device_id=(row, peer),
             device_id_type=mesh_ids,
         )
+
+    def own_part(block, chunk):
+        start = pl.multiple_of(block * block_rows + (chunk % pieces) * rows, rows)
+        return parts_ref[chunk // pieces, pl.ds(start, rows), :]
 
     barrier = pltpu.get_barrier_semaphore()
     for peer in (upper, lower):
         pl.semaphore_signal(barrier, inc=1, device_id=(row, peer), device_id_type=mesh_ids)
     pl.semaphore_wait(barrier, 2)
 
-    for seq in range(seqs):
+    for chunk in range(chunks):
+        seq, piece = chunk // pieces, chunk % pieces
+        out_rows = slice(piece * rows, (piece + 1) * rows)
 
         @pl.when(has_upper)
         def _():
-            link(me, seq, upper).wait_recv()
-            out_ref[seq] = (
-                parts_ref[me, seq].astype(jnp.float32) + recvbuf[me, seq].astype(jnp.float32)
+            link(me, chunk, upper).wait_recv()
+            out_ref[seq, out_rows, :] = (
+                own_part(me, chunk).astype(jnp.float32) + recvbuf[me, chunk].astype(jnp.float32)
             ).astype(out_ref.dtype)
 
         @pl.when(is_top)
         def _():
-            out_ref[seq] = parts_ref[me, seq]
+            out_ref[seq, out_rows, :] = own_part(me, chunk)
 
     def forward(step, carry):
         block = me - 1 - step
-        for seq in range(seqs):
+        for chunk in range(chunks):
 
             @pl.when(has_upper)
             def _():
-                link(block, seq, upper).wait_recv()
-                sendbuf[block, seq] = (
-                    parts_ref[block, seq].astype(jnp.float32)
-                    + recvbuf[block, seq].astype(jnp.float32)
+                link(block, chunk, upper).wait_recv()
+                sendbuf[block, chunk] = (
+                    own_part(block, chunk).astype(jnp.float32)
+                    + recvbuf[block, chunk].astype(jnp.float32)
                 ).astype(sendbuf.dtype)
 
             @pl.when(is_top)
             def _():
-                sendbuf[block, seq] = parts_ref[block, seq].astype(sendbuf.dtype)
-
-            link(block, seq, lower).start()
+                sendbuf[block, chunk] = own_part(block, chunk).astype(sendbuf.dtype)
+
+            link(block, chunk, lower).start()
         return carry
 
     lax.fori_loop(0, me, forward, 0)
 
     def finish(step, carry):
         block = me - 1 - step
-        for seq in range(seqs):
-            link(block, seq, lower).wait_send()
+        for chunk in range(chunks):
+            link(block, chunk, lower).wait_send()
         return carry
 
     lax.fori_loop(0, me, finish, 0)
 
 
-def pair_return(pair_buffer):
+def pair_return(pair_buffer, devices, pieces):
+    seqs, total_rows, width = pair_buffer.shape
+    block_rows = total_rows // devices
+    chunks = seqs * pieces
+    slots = (devices, chunks, block_rows // pieces, width)
     return pl.pallas_call(
         pair_chain_kernel,
-        out_shape=jax.ShapeDtypeStruct(pair_buffer.shape[1:], pair_buffer.dtype),
+        out_shape=jax.ShapeDtypeStruct((seqs, block_rows, width), pair_buffer.dtype),
         in_specs=[pl.BlockSpec(memory_space=pltpu.VMEM)],
         out_specs=pl.BlockSpec(memory_space=pltpu.VMEM),
         scratch_shapes=[
-            pltpu.VMEM(pair_buffer.shape, CHAIN_DTYPE),
-            pltpu.VMEM(pair_buffer.shape, CHAIN_DTYPE),
-            pltpu.SemaphoreType.DMA(pair_buffer.shape[:2]),
-            pltpu.SemaphoreType.DMA(pair_buffer.shape[:2]),
+            pltpu.VMEM(slots, CHAIN_DTYPE),
+            pltpu.VMEM(slots, CHAIN_DTYPE),
+            pltpu.SemaphoreType.DMA(slots[:2]),
+            pltpu.SemaphoreType.DMA(slots[:2]),
         ],
         compiler_params=pltpu.CompilerParams(collective_id=0, has_side_effects=True),
     )(pair_buffer)
@@ -214,15 +227,7 @@
     value_part = jnp.einsum(
         "shpr,sphd->srd", probs_low, context_grad, preferred_element_type=jnp.float32
     ).astype(jnp.bfloat16)
-    pair_buffer = (
-        jnp.moveaxis(
-            jnp.concatenate([key_part, value_part], axis=2).reshape(
-                seq_count, devices, shard_len, 2 * HEAD
-            ),
-            1,
-            0,
-        )
-    )
+    pair_buffer = jnp.concatenate([key_part, value_part], axis=2)
     query_grad = query_total.astype(jnp.bfloat16).reshape(seq_count, shard_len, row_width)
     flat_rows = rows_in.reshape(devices * CAP, model_width)
     flat_grads = grads_in.reshape(devices * CAP, model_width)
@@ -270,10 +275,7 @@
     gate_proj_grad = summed[:, :hidden_width][None]
     up_proj_grad = summed[:, hidden_width : 2 * hidden_width][None]
     down_proj_grad = jnp.transpose(summed[:, 2 * hidden_width :])[None]
-    chunks = 4
-    pair_total = pair_return(
-        pair_buffer.reshape(devices, chunks, seq_count * shard_len // chunks, 2 * HEAD)
-    ).reshape(seq_count, shard_len, 2 * HEAD)
+    pair_total = pair_return(pair_buffer, devices, 2)
     key_grad = pair_total[:, :, :HEAD]
     value_grad = pair_total[:, :, HEAD:]
     back_all = lax.all_to_all(

time: 330 us -> 319 us (0.967)
  local copies, waits for them, and re-layouts: 25.3 us -> 14.5 us
    all_gather x1, waiting for transfers between devices: 57.8 us -> 35.3 us  [shards(): gathered = lax.all_gather(packed, 'expert', axis=1, tiled=True)]
    all_to_all x1, waiting for transfers between devices: 0.01 us -> 22.4 us  [shards(): lax.all_to_all(jnp.concatenate([input_rows.reshape(devices, CAP, model_wi...]
    concatenate x1 -> x0, local copies, waits for them, and re-layouts: 6.31 us -> none  [shards(): jnp.concatenate([key_part, value_part], axis=2)]
    transpose x1 -> x0, local copies, waits for them, and re-layouts: 4.69 us -> none  [shards(): jnp.moveaxis(jnp.concatenate([key_part, value_part], axis=2).reshape(seq_...]
  transfers between devices with their start and end apart: 5 -> 5, of which waited for: 3 -> 4; matrix products, arithmetic and copies ran while one was open for 19% -> 16% of each run, Pallas kernels for 32% -> 33%
where the time goes in v8:
time: 319 us; the launch traced here: 318 us
  Pallas kernels  107 us (34%)
  waiting for transfers between devices  105 us (33%)
  matrix products  31.3 us (10%)
  starting transfers between devices  30.9 us (10%)
  other arithmetic  15.9 us (5%)
  local copies, waits for them, and re-layouts  14.5 us (5%)
  between operations  14.2 us (4%)
    pallas_call x1, Pallas kernels, pair_return(): pl.pallas_call(pair_chain_kernel, out_shape=jax.ShapeDtypeStruct((seqs, b...  107 us
    all_gather x1, waiting for transfers between devices, shards(): gathered = lax.all_gather(packed, 'expert', axis=1, tiled=True)  35.3 us
    all_to_all x1, waiting for transfers between devices, shards(): lax.all_to_all(send_all, 'expert', split_axis=0, concat_axis=0, tiled=True)  33.5 us
    all_to_all x1, waiting for transfers between devices, shards(): lax.all_to_all(jnp.concatenate([input_rows.reshape(devices, CAP, model_wi...  22.4 us
    all_to_all x1, starting transfers between devices, shards(): lax.all_to_all(send_all, 'expert', split_axis=0, concat_axis=0, tiled=True)  16.8 us
    all_to_all x1, starting transfers between devices, shards(): lax.all_to_all(jnp.concatenate([input_rows.reshape(devices, CAP, model_wi...  13.9 us
    all_gather x1, waiting for transfers between devices, shards(): weight_full = lax.all_gather(weight_cat, 'dp', axis=1, tiled=True)[0]  13.7 us
    unnamed x27, local copies, waits for them, and re-layouts  9.86 us
  transfers between devices with their start and end apart: 5, of which 4 were waited for; matrix products, arithmetic and copies ran while one was open for 16% of the time, Pallas kernels for 33%

profile of v8, /device:TPU:1, one launch (start us, length us, event | category | flops | bytes accessed | tf_op | source)
XLA Modules:
  0.0 318.5 jit_solution(4649345593571088218)
XLA Ops:
  7.3 1.1 copy.83
  8.3 1.0 copy.84
  9.3 1.5 pad_maximum_fusion.4
  10.9 0.7 fusion.65
  11.6 0.7 select_reduce_fusion.1
  12.3 0.2 fusion.16
  12.6 0.2 convolution_convert_fusion.3
  12.9 0.2 reshape.190
  13.1 1.3 convolution_convert_fusion.4
  14.3 0.2 reshape.189
  14.5 0.7 select_reduce_fusion
  15.2 0.1 fusion.40
  15.4 1.3 pad_maximum_fusion.2
  16.6 16.8 %all-to-all-start = ((bf16[32,2,4224]{2,1,0:T(2,128)(2,1)}), bf16[32,2,4224]{2,1,0:T(2,128)(2,1)S(1)}, u32[]{:S(2)}, u32[]{:S(2)}) async-start(bf16[32,2,4224]{2,1,0:T(2,128)(2,1)} %pad_maximum_fusion.2), calls=%async_computation | async-start | bytes 1081344 | tf_op jit(solution)/shard_map/all_to_all | solution.py:177
  33.5 0.7 pad_maximum_fusion.5
  34.1 33.5 %all-to-all-done = bf16[32,2,4224]{2,1,0:T(2,128)(2,1)S(1)} async-done(((bf16[32,2,4224]{2,1,0:T(2,128)(2,1)}), bf16[32,2,4224]{2,1,0:T(2,128)(2,1)S(1)}, u32[]{:S(2)}, u32[]{:S(2)}) %all-to-all-start) | async-done | bytes 540704 | tf_op jit(solution)/shard_map/all_to_all | solution.py:177
  67.6 0.1 reshape.199
  67.8 0.1 iota_compare_fusion
  67.9 1.3 add_divide_fusion
  69.2 0.1 convert_reduce_fusion
  69.3 0.1 reshape.201
  69.4 0.4 fusion.66
  69.9 0.4 reshape.202
  70.2 13.7 %all-gather.5.cloned.1.call-done = bf16[1,2048,768]{1,2,0:T(8,128)(2,1)} async-done(((bf16[1,128,768]{1,2,0:T(8,128)(2,1)}), bf16[1,2048,768]{1,2,0:T(8,128)(2,1)}) %all-gather.5.cloned.1.call-update) | async-done | bytes 3145744 | tf_op jit(solution)/shard_map/all_gather | solution.py:178
  84.0 1.7 fusion.22
  85.6 1.7 fusion.25
  87.3 1.7 multiply_convert_fusion.2
  89.0 1.6 fusion.15
  90.6 0.1 convert_element_type.153
  90.8 1.5 fusion.20
  92.3 1.5 fusion.8
  93.8 0.2 reshape.198
  94.1 1.0 pad_maximum_fusion.3
  95.1 13.9 %all-to-all-start.1 = ((bf16[32,2,2176]{2,1,0:T(2,128)(2,1)}), bf16[32,2,2176]{2,1,0:T(2,128)(2,1)S(1)}, u32[]{:S(2)}, u32[]{:S(2)}) async-start(bf16[32,2,2176]{2,1,0:T(2,128)(2,1)} %pad_maximum_fusion.3), calls=%async_computation.1 | async-start | bytes 557056 | tf_op jit(solution)/shard_map/all_to_all | solution.py:281
  109.0 0.2 reduce-scatter.4.cloned.1.call-start
  109.2 0.5 convolution_convert_fusion.1
  109.7 0.5 convolution_convert_fusion.2
  110.1 0.5 convolution_convert_fusion
  110.6 1.9 pad_maximum_fusion.1
  112.5 22.4 %all-to-all-done.1 = bf16[32,2,2176]{2,1,0:T(2,128)(2,1)S(1)} async-done(((bf16[32,2,2176]{2,1,0:T(2,128)(2,1)}), bf16[32,2,2176]{2,1,0:T(2,128)(2,1)S(1)}, u32[]{:S(2)}, u32[]{:S(2)}) %all-to-all-start.1) | async-done | bytes 278560 | tf_op jit(solution)/shard_map/all_to_all | solution.py:281
  135.0 35.3 %all-gather.3.cloned.1.call-done = bf16[2,2048,512]{2,1,0:T(8,128)(2,1)} async-done(((bf16[2,64,512]{2,1,0:T(8,128)(2,1)}), bf16[2,2048,512]{2,1,0:T(8,128)(2,1)}) %all-gather.3.cloned.1.call-update) | async-done | bytes 4194320 | tf_op jit(solution)/shard_map/all_gather | solution.py:180
  170.3 4.7 %copy.97 = bf16[2048,768]{1,0:T(8,128)(2,1)} copy(bf16[2048,768]{0,1:T(8,128)(2,1)} %pad_maximum_fusion.1) | data formatting | bytes 6291456
  175.1 0.2 slice.65
  175.3 0.1 multiply_reduce_fusion.1
  175.4 0.6 select_convert_fusion
  176.0 1.1 fusion.7
  177.2 3.1 fusion.5
  180.3 2.2 exponential_reduce_fusion
  182.6 0.3 copy-done.7
  182.8 2.1 multiply_reduce_fusion
  184.9 0.8 copy.105
  185.7 3.2 %fusion.2 = bf16[2,8,64,2048]{3,2,1,0:T(8,128)(2,1)S(1)} fusion(f32[2,2048,64,8]{1,2,3,0:T(8,128)S(1)} %get-tuple-element.67, bf16[2,64,8,256]{3,1,2,0:T(8,128)(2,1)S(1)} %get-tuple-element.52, f32[2,8,64]{2,1,0:T(8,128)S(1)} %bitcast.147, f32[2,8,64]{2,1,0:T(8,128)S(1)} %log_add_fusion, pred[64,2048]{1,0:T(8,128)(4,1)S(1)} %iota_compare_fusion, ...), kind=kOutput, calls=%fused_computation.3 | convolution fusion | flops 1088421888 | bytes 15351808 | tf_op jit(solution)/shard_map/sphd,srd->shpr/dot_general | solution.py:215
  189.0 1.8 bitcast_convert_fusion.1
  190.8 0.2 copy-done.9
  190.9 3.1 bitcast_convert_fusion
  194.0 2.3 pad_maximum_fusion.parts_ref
  196.3 106.7 %shard_map.187 = bf16[2,64,512]{2,1,0:T(8,128)(2,1)} custom-call(bf16[2,2048,512]{2,1,0:T(8,128)(2,1)} %pad_maximum_fusion.parts_ref), custom_call_target="tpu_custom_call" | custom-call | tf_op jit(solution)/shard_map/pallas_call | solution.py:96
  303.0 4.1 %fusion.14 = bf16[2,8,8,8,256]{4,3,2,1,0:T(8,128)(2,1)S(1)} fusion(bf16[2,8,64,2048]{3,2,1,0:T(8,128)(2,1)} %copy-done.9, bf16[2,2048,512]{2,1,0:T(8,128)(2,1)} %all-gather.3.cloned.1.call-done), kind=kOutput, calls=%fused_computation.32 | convolution fusion | flops 1074003968 | bytes 6815744 | tf_op jit(solution)/shard_map/shpr,srd->sphd/dot_general | solution.py:221
  307.1 0.8 copy.104
  308.0 0.7 fusion.67
  308.6 1.1 copy.98
  309.8 0.7 slice_bitcast_fusion.12
  310.4 0.8 copy.90
  311.2 0.8 copy.89
  (38 shorter events, 0.8 us)
Async XLA Ops:
  7.2 5.5 %copy-start = (bf16[128,2048]{1,0:T(8,128)(2,1)S(1)}, bf16[128,2048]{1,0:T(8,128)(2,1)}, u32[]{:S(2)}) copy-start(bf16[128,2048]{1,0:T(8,128)(2,1)} %param.18) | copy-start | bytes 1572868
  7.2 26.2 %copy-start.5 = (bf16[2,64,256]{2,1,0:T(8,128)(2,1)S(1)}, bf16[2,64,256]{2,1,0:T(8,128)(2,1)}, u32[]{:S(2)}) copy-start(bf16[2,64,256]{2,1,0:T(8,128)(2,1)} %param.14) | copy-start | bytes 196612
  7.2 26.2 %copy-start.6 = (bf16[2,64,256]{2,1,0:T(8,128)(2,1)S(1)}, bf16[2,64,256]{2,1,0:T(8,128)(2,1)}, u32[]{:S(2)}) copy-start(bf16[2,64,256]{2,1,0:T(8,128)(2,1)} %param.13) | copy-start | bytes 196612
  7.2 60.4 %copy-start.2 = (bf16[2,64,2048]{2,1,0:T(8,128)(2,1)S(1)}, bf16[2,64,2048]{2,1,0:T(8,128)(2,1)}, u32[]{:S(2)}) copy-start(bf16[2,64,2048]{2,1,0:T(8,128)(2,1)} %param.16) | copy-start | bytes 1572868
  7.2 60.7 %copy-start.3 = (bf16[2,64,2048]{2,1,0:T(8,128)(2,1)S(1)}, bf16[2,64,2048]{2,1,0:T(8,128)(2,1)}, u32[]{:S(2)}) copy-start(bf16[2,64,2048]{2,1,0:T(8,128)(2,1)} %param.15) | copy-start | bytes 1572868
  7.2 76.7 %all-gather.5.cloned.1.call-start = ((), (), s32[]{:S(2)}) async-start(), calls=%async_computation.4 | async-start | bytes 3342336 | tf_op jit(solution)/shard_map/all_gather | solution.py:178
  16.6 51.0 %all-to-all-start = ((bf16[32,2,4224]{2,1,0:T(2,128)(2,1)}), bf16[32,2,4224]{2,1,0:T(2,128)(2,1)S(1)}, u32[]{:S(2)}, u32[]{:S(2)}) async-start(bf16[32,2,4224]{2,1,0:T(2,128)(2,1)} %pad_maximum_fusion.2), calls=%async_computation | async-start | bytes 1081344 | tf_op jit(solution)/shard_map/all_to_all | solution.py:177
  33.4 136.9 %all-gather.3.cloned.1.call-start = ((), (), s32[]{:S(2)}) async-start(), calls=%async_computation.3 | async-start | bytes 4325376 | tf_op jit(solution)/shard_map/all_gather | solution.py:180
  95.1 39.8 %all-to-all-start.1 = ((bf16[32,2,2176]{2,1,0:T(2,128)(2,1)}), bf16[32,2,2176]{2,1,0:T(2,128)(2,1)S(1)}, u32[]{:S(2)}, u32[]{:S(2)}) async-start(bf16[32,2,2176]{2,1,0:T(2,128)(2,1)} %pad_maximum_fusion.3), calls=%async_computation.1 | async-start | bytes 557056 | tf_op jit(solution)/shard_map/all_to_all | solution.py:281
  109.0 199.7 %reduce-scatter.4.cloned.1.call-start = ((), (), s32[]{:S(2)}) async-start(), calls=%async_computation.5 | async-start | bytes 3342336
  180.3 2.3 copy-start.1
  180.3 2.5 copy-start.7
  185.7 3.2 %copy-start.8 = (bf16[2,64,2048]{2,1,0:T(8,128)(2,1)S(1)}, bf16[2,64,2048]{2,1,0:T(8,128)(2,1)}, u32[]{:S(2)}) copy-start(bf16[2,64,2048]{2,1,0:T(8,128)(2,1)} %param.12) | copy-start | bytes 1572868
  189.0 2.0 copy-start.9
  303.0 5.0 %copy-start.4 = (bf16[2,64,512]{2,1,0:T(8,128)(2,1)S(1)}, bf16[2,64,512]{2,1,0:T(8,128)(2,1)}, u32[]{:S(2)}) copy-start(bf16[2,64,512]{2,1,0:T(8,128)(2,1)} %shard_map.187) | copy-start | bytes 393220
Sparse Core Ops, SparseCore 0:
  11.6 72.2 all-gather.4
  86.7 83.5 all-gather.2
  175.1 83.6 reduce-scatter.3

commit v9 on v8

--- a/solution.py
+++ b/solution.py
@@ -275,7 +275,7 @@
     gate_proj_grad = summed[:, :hidden_width][None]
     up_proj_grad = summed[:, hidden_width : 2 * hidden_width][None]
     down_proj_grad = jnp.transpose(summed[:, 2 * hidden_width :])[None]
-    pair_total = pair_return(pair_buffer, devices, 2)
+    pair_total = pair_return(pair_buffer, devices, 4)
     key_grad = pair_total[:, :, :HEAD]
     value_grad = pair_total[:, :, HEAD:]
     back_all = lax.all_to_all(

time: 319 us -> 319 us (level)
  no operation moved by 1% of the time
where the time goes in v9:
time: 319 us; the launch traced here: 318 us
  Pallas kernels  106 us (33%)
  waiting for transfers between devices  105 us (33%)
  matrix products  31.3 us (10%)
  starting transfers between devices  30.9 us (10%)
  other arithmetic  15.9 us (5%)
  local copies, waits for them, and re-layouts  14.5 us (5%)
  between operations  14.2 us (4%)
    pallas_call x1, Pallas kernels, pair_return(): pl.pallas_call(pair_chain_kernel, out_shape=jax.ShapeDtypeStruct((seqs, b...  106 us
    all_gather x1, waiting for transfers between devices, shards(): gathered = lax.all_gather(packed, 'expert', axis=1, tiled=True)  35.3 us
    all_to_all x1, waiting for transfers between devices, shards(): lax.all_to_all(send_all, 'expert', split_axis=0, concat_axis=0, tiled=True)  33.5 us
    all_to_all x1, waiting for transfers between devices, shards(): lax.all_to_all(jnp.concatenate([input_rows.reshape(devices, CAP, model_wi...  22.4 us
    all_to_all x1, starting transfers between devices, shards(): lax.all_to_all(send_all, 'expert', split_axis=0, concat_axis=0, tiled=True)  16.8 us
    all_to_all x1, starting transfers between devices, shards(): lax.all_to_all(jnp.concatenate([input_rows.reshape(devices, CAP, model_wi...  13.9 us
    all_gather x1, waiting for transfers between devices, shards(): weight_full = lax.all_gather(weight_cat, 'dp', axis=1, tiled=True)[0]  13.7 us
    unnamed x27, local copies, waits for them, and re-layouts  9.86 us
  transfers between devices with their start and end apart: 5, of which 4 were waited for; matrix products, arithmetic and copies ran while one was open for 16% of the time, Pallas kernels for 33%

profile of v9, /device:TPU:1, one launch (start us, length us, event | category | flops | bytes accessed | tf_op | source)
XLA Modules:
  0.0 317.9 jit_solution(3840293450357512538)
XLA Ops:
  7.3 1.1 copy.83
  8.3 1.0 copy.84
  9.3 1.5 pad_maximum_fusion.4
  10.9 0.7 fusion.65
  11.6 0.7 select_reduce_fusion.1
  12.3 0.2 fusion.16
  12.6 0.2 convolution_convert_fusion.3
  12.9 0.2 reshape.190
  13.1 1.3 convolution_convert_fusion.4
  14.3 0.2 reshape.189
  14.5 0.7 select_reduce_fusion
  15.2 0.1 fusion.40
  15.4 1.3 pad_maximum_fusion.2
  16.6 16.8 %all-to-all-start = ((bf16[32,2,4224]{2,1,0:T(2,128)(2,1)}), bf16[32,2,4224]{2,1,0:T(2,128)(2,1)S(1)}, u32[]{:S(2)}, u32[]{:S(2)}) async-start(bf16[32,2,4224]{2,1,0:T(2,128)(2,1)} %pad_maximum_fusion.2), calls=%async_computation | async-start | bytes 1081344 | tf_op jit(solution)/shard_map/all_to_all | solution.py:177
  33.5 0.7 pad_maximum_fusion.5
  34.1 33.5 %all-to-all-done = bf16[32,2,4224]{2,1,0:T(2,128)(2,1)S(1)} async-done(((bf16[32,2,4224]{2,1,0:T(2,128)(2,1)}), bf16[32,2,4224]{2,1,0:T(2,128)(2,1)S(1)}, u32[]{:S(2)}, u32[]{:S(2)}) %all-to-all-start) | async-done | bytes 540704 | tf_op jit(solution)/shard_map/all_to_all | solution.py:177
  67.6 0.1 reshape.199
  67.8 0.1 iota_compare_fusion
  67.9 1.3 add_divide_fusion
  69.2 0.1 convert_reduce_fusion
  69.3 0.1 reshape.201
  69.4 0.4 fusion.66
  69.9 0.4 reshape.202
  70.2 13.7 %all-gather.5.cloned.1.call-done = bf16[1,2048,768]{1,2,0:T(8,128)(2,1)} async-done(((bf16[1,128,768]{1,2,0:T(8,128)(2,1)}), bf16[1,2048,768]{1,2,0:T(8,128)(2,1)}) %all-gather.5.cloned.1.call-update) | async-done | bytes 3145744 | tf_op jit(solution)/shard_map/all_gather | solution.py:178
  84.0 1.7 fusion.22
  85.6 1.7 fusion.25
  87.3 1.7 multiply_convert_fusion.2
  89.0 1.6 fusion.15
  90.6 0.1 convert_element_type.153
  90.8 1.5 fusion.20
  92.3 1.5 fusion.8
  93.8 0.2 reshape.198
  94.1 1.0 pad_maximum_fusion.3
  95.1 13.9 %all-to-all-start.1 = ((bf16[32,2,2176]{2,1,0:T(2,128)(2,1)}), bf16[32,2,2176]{2,1,0:T(2,128)(2,1)S(1)}, u32[]{:S(2)}, u32[]{:S(2)}) async-start(bf16[32,2,2176]{2,1,0:T(2,128)(2,1)} %pad_maximum_fusion.3), calls=%async_computation.1 | async-start | bytes 557056 | tf_op jit(solution)/shard_map/all_to_all | solution.py:281
  109.0 0.2 reduce-scatter.4.cloned.1.call-start
  109.2 0.5 convolution_convert_fusion.1
  109.7 0.5 convolution_convert_fusion.2
  110.1 0.5 convolution_convert_fusion
  110.6 1.9 pad_maximum_fusion.1
  112.5 22.4 %all-to-all-done.1 = bf16[32,2,2176]{2,1,0:T(2,128)(2,1)S(1)} async-done(((bf16[32,2,2176]{2,1,0:T(2,128)(2,1)}), bf16[32,2,2176]{2,1,0:T(2,128)(2,1)S(1)}, u32[]{:S(2)}, u32[]{:S(2)}) %all-to-all-start.1) | async-done | bytes 278560 | tf_op jit(solution)/shard_map/all_to_all | solution.py:281
  135.0 35.3 %all-gather.3.cloned.1.call-done = bf16[2,2048,512]{2,1,0:T(8,128)(2,1)} async-done(((bf16[2,64,512]{2,1,0:T(8,128)(2,1)}), bf16[2,2048,512]{2,1,0:T(8,128)(2,1)}) %all-gather.3.cloned.1.call-update) | async-done | bytes 4194320 | tf_op jit(solution)/shard_map/all_gather | solution.py:180
  170.3 4.7 %copy.97 = bf16[2048,768]{1,0:T(8,128)(2,1)} copy(bf16[2048,768]{0,1:T(8,128)(2,1)} %pad_maximum_fusion.1) | data formatting | bytes 6291456
  175.1 0.2 slice.65
  175.3 0.1 multiply_reduce_fusion.1
  175.4 0.6 select_convert_fusion
  176.0 1.1 fusion.7
  177.2 3.1 fusion.5
  180.3 2.2 exponential_reduce_fusion
  182.6 0.3 copy-done.7
  182.8 2.1 multiply_reduce_fusion
  184.9 0.8 copy.105
  185.7 3.2 %fusion.2 = bf16[2,8,64,2048]{3,2,1,0:T(8,128)(2,1)S(1)} fusion(f32[2,2048,64,8]{1,2,3,0:T(8,128)S(1)} %get-tuple-element.67, bf16[2,64,8,256]{3,1,2,0:T(8,128)(2,1)S(1)} %get-tuple-element.52, f32[2,8,64]{2,1,0:T(8,128)S(1)} %bitcast.147, f32[2,8,64]{2,1,0:T(8,128)S(1)} %log_add_fusion, pred[64,2048]{1,0:T(8,128)(4,1)S(1)} %iota_compare_fusion, ...), kind=kOutput, calls=%fused_computation.3 | convolution fusion | flops 1088421888 | bytes 15351808 | tf_op jit(solution)/shard_map/sphd,srd->shpr/dot_general | solution.py:215
  189.0 1.8 bitcast_convert_fusion.1
  190.8 0.2 copy-done.9
  190.9 3.1 bitcast_convert_fusion
  194.0 2.3 pad_maximum_fusion.parts_ref
  196.3 106.1 %shard_map.187 = bf16[2,64,512]{2,1,0:T(8,128)(2,1)} custom-call(bf16[2,2048,512]{2,1,0:T(8,128)(2,1)} %pad_maximum_fusion.parts_ref), custom_call_target="tpu_custom_call" | custom-call | tf_op jit(solution)/shard_map/pallas_call | solution.py:96
  302.4 4.1 %fusion.14 = bf16[2,8,8,8,256]{4,3,2,1,0:T(8,128)(2,1)S(1)} fusion(bf16[2,8,64,2048]{3,2,1,0:T(8,128)(2,1)} %copy-done.9, bf16[2,2048,512]{2,1,0:T(8,128)(2,1)} %all-gather.3.cloned.1.call-done), kind=kOutput, calls=%fused_computation.32 | convolution fusion | flops 1074003968 | bytes 6815744 | tf_op jit(solution)/shard_map/shpr,srd->sphd/dot_general | solution.py:221
  306.6 0.8 copy.104
  307.4 0.7 fusion.67
  308.1 1.1 copy.98
  309.2 0.7 slice_bitcast_fusion.12
  309.9 0.8 copy.90
  310.6 0.8 copy.89
  (38 shorter events, 0.8 us)
Async XLA Ops:
  7.2 5.5 %copy-start = (bf16[128,2048]{1,0:T(8,128)(2,1)S(1)}, bf16[128,2048]{1,0:T(8,128)(2,1)}, u32[]{:S(2)}) copy-start(bf16[128,2048]{1,0:T(8,128)(2,1)} %param.18) | copy-start | bytes 1572868
  7.2 26.2 %copy-start.5 = (bf16[2,64,256]{2,1,0:T(8,128)(2,1)S(1)}, bf16[2,64,256]{2,1,0:T(8,128)(2,1)}, u32[]{:S(2)}) copy-start(bf16[2,64,256]{2,1,0:T(8,128)(2,1)} %param.14) | copy-start | bytes 196612
  7.2 26.2 %copy-start.6 = (bf16[2,64,256]{2,1,0:T(8,128)(2,1)S(1)}, bf16[2,64,256]{2,1,0:T(8,128)(2,1)}, u32[]{:S(2)}) copy-start(bf16[2,64,256]{2,1,0:T(8,128)(2,1)} %param.13) | copy-start | bytes 196612
  7.2 60.4 %copy-start.2 = (bf16[2,64,2048]{2,1,0:T(8,128)(2,1)S(1)}, bf16[2,64,2048]{2,1,0:T(8,128)(2,1)}, u32[]{:S(2)}) copy-start(bf16[2,64,2048]{2,1,0:T(8,128)(2,1)} %param.16) | copy-start | bytes 1572868
  7.2 60.7 %copy-start.3 = (bf16[2,64,2048]{2,1,0:T(8,128)(2,1)S(1)}, bf16[2,64,2048]{2,1,0:T(8,128)(2,1)}, u32[]{:S(2)}) copy-start(bf16[2,64,2048]{2,1,0:T(8,128)(2,1)} %param.15) | copy-start | bytes 1572868
  7.2 76.7 %all-gather.5.cloned.1.call-start = ((), (), s32[]{:S(2)}) async-start(), calls=%async_computation.4 | async-start | bytes 3342336 | tf_op jit(solution)/shard_map/all_gather | solution.py:178
  16.6 51.0 %all-to-all-start = ((bf16[32,2,4224]{2,1,0:T(2,128)(2,1)}), bf16[32,2,4224]{2,1,0:T(2,128)(2,1)S(1)}, u32[]{:S(2)}, u32[]{:S(2)}) async-start(bf16[32,2,4224]{2,1,0:T(2,128)(2,1)} %pad_maximum_fusion.2), calls=%async_computation | async-start | bytes 1081344 | tf_op jit(solution)/shard_map/all_to_all | solution.py:177
  33.4 136.9 %all-gather.3.cloned.1.call-start = ((), (), s32[]{:S(2)}) async-start(), calls=%async_computation.3 | async-start | bytes 4325376 | tf_op jit(solution)/shard_map/all_gather | solution.py:180
  95.1 39.8 %all-to-all-start.1 = ((bf16[32,2,2176]{2,1,0:T(2,128)(2,1)}), bf16[32,2,2176]{2,1,0:T(2,128)(2,1)S(1)}, u32[]{:S(2)}, u32[]{:S(2)}) async-start(bf16[32,2,2176]{2,1,0:T(2,128)(2,1)} %pad_maximum_fusion.3), calls=%async_computation.1 | async-start | bytes 557056 | tf_op jit(solution)/shard_map/all_to_all | solution.py:281
  109.0 199.1 %reduce-scatter.4.cloned.1.call-start = ((), (), s32[]{:S(2)}) async-start(), calls=%async_computation.5 | async-start | bytes 3342336
  180.3 2.3 copy-start.1
  180.3 2.5 copy-start.7
  185.7 3.2 %copy-start.8 = (bf16[2,64,2048]{2,1,0:T(8,128)(2,1)S(1)}, bf16[2,64,2048]{2,1,0:T(8,128)(2,1)}, u32[]{:S(2)}) copy-start(bf16[2,64,2048]{2,1,0:T(8,128)(2,1)} %param.12) | copy-start | bytes 1572868
  189.0 2.0 copy-start.9
  302.4 5.0 %copy-start.4 = (bf16[2,64,512]{2,1,0:T(8,128)(2,1)S(1)}, bf16[2,64,512]{2,1,0:T(8,128)(2,1)}, u32[]{:S(2)}) copy-start(bf16[2,64,512]{2,1,0:T(8,128)(2,1)} %shard_map.187) | copy-start | bytes 393220
Sparse Core Ops, SparseCore 0:
  11.6 72.2 all-gather.4
  86.7 83.5 all-gather.2
  175.1 83.6 reduce-scatter.3

commit v10 on v9

--- a/solution.py
+++ b/solution.py
@@ -175,9 +175,9 @@
         [gate_proj, up_proj, jnp.transpose(down_proj, (0, 2, 1))], axis=2
     )
     recv_all = lax.all_to_all(send_all, "expert", split_axis=0, concat_axis=0, tiled=True)
+    gathered = lax.all_gather(packed, "expert", axis=1, tiled=True)
+    gathered, recv_all, weight_cat = lax.optimization_barrier((gathered, recv_all, weight_cat))
     weight_full = lax.all_gather(weight_cat, "dp", axis=1, tiled=True)[0]
-    packed, recv_all = lax.optimization_barrier((packed, recv_all))
-    gathered = lax.all_gather(packed, "expert", axis=1, tiled=True)
     rows_in = recv_all[:, :, :model_cols]
     grads_in = recv_all[:, :, model_cols : 2 * model_cols]
     weights_in = recv_all[:, :, 2 * model_cols]
@@ -268,7 +268,6 @@
             ],
             axis=1,
         ).astype(jnp.bfloat16)
-    gathered, group_cat = lax.optimization_barrier((gathered, group_cat))
     summed = lax.psum_scatter(group_cat, "dp", scatter_dimension=0, tiled=True).astype(
         jnp.float32
     )

time: 319 us -> 350 us (1.097)
  waiting for transfers between devices: 105 us -> 127 us
  matrix products: 31.3 us -> 37.4 us
    all_gather x1, waiting for transfers between devices: 13.7 us -> 54.3 us  [shards(): weight_full = lax.all_gather(weight_cat, 'dp', axis=1, tiled=True)[0]]
    all_to_all x1, waiting for transfers between devices: 22.4 us -> 0.01 us  [shards(): lax.all_to_all(jnp.concatenate([input_rows.reshape(devices, CAP, model_wi...]
    all_to_all x1, waiting for transfers between devices: 33.5 us -> 39 us  [shards(): lax.all_to_all(send_all, 'expert', split_axis=0, concat_axis=0, tiled=True)]
    dot_general x1, matrix products: 2.06 us -> 6.45 us  [shards(): jnp.einsum('shpr,srd->sphd', probs_low, values_all, preferred_element_typ...]
    unnamed x27 -> x35, local copies, waits for them, and re-layouts: 9.86 us -> 11.7 us
  transfers between devices with their start and end apart: 5 -> 5, of which waited for: 4 -> 3; matrix products, arithmetic and copies ran while one was open for 16% -> 14% of each run, Pallas kernels for 33% -> 30%
where the time goes in v10:
time: 350 us; the launch traced here: 349 us
  waiting for transfers between devices  127 us (36%)
  Pallas kernels  106 us (30%)
  matrix products  37.4 us (11%)
  starting transfers between devices  30.8 us (9%)
  local copies, waits for them, and re-layouts  17.3 us (5%)
  other arithmetic  17 us (5%)
  between operations  14.2 us (4%)
    pallas_call x1, Pallas kernels, pair_return(): pl.pallas_call(pair_chain_kernel, out_shape=jax.ShapeDtypeStruct((seqs, b...  106 us
    all_gather x1, waiting for transfers between devices, shards(): weight_full = lax.all_gather(weight_cat, 'dp', axis=1, tiled=True)[0]  54.3 us
    all_to_all x1, waiting for transfers between devices, shards(): lax.all_to_all(send_all, 'expert', split_axis=0, concat_axis=0, tiled=True)  39 us
    all_gather x1, waiting for transfers between devices, shards(): gathered = lax.all_gather(packed, 'expert', axis=1, tiled=True)  33.4 us
    all_to_all x1, starting transfers between devices, shards(): lax.all_to_all(send_all, 'expert', split_axis=0, concat_axis=0, tiled=True)  16.8 us
    all_to_all x1, starting transfers between devices, shards(): lax.all_to_all(jnp.concatenate([input_rows.reshape(devices, CAP, model_wi...  13.9 us
    unnamed x35, local copies, waits for them, and re-layouts  11.7 us
  transfers between devices with their start and end apart: 5, of which 3 were waited for; matrix products, arithmetic and copies ran while one was open for 14% of the time, Pallas kernels for 30%

profile of v10, /device:TPU:1, one launch (start us, length us, event | category | flops | bytes accessed | tf_op | source)
XLA Modules:
  0.0 349.3 jit_solution(9321966289199784166)
XLA Ops:
  7.3 1.6 pad_maximum_fusion.5
  9.0 0.7 fusion.79
  9.7 0.7 select_reduce_fusion.1
  10.4 0.2 fusion.30
  10.7 0.2 convolution_convert_fusion.3
  11.0 0.2 reshape.190
  11.2 1.3 convolution_convert_fusion.4
  12.4 0.2 reshape.189
  12.6 0.7 select_reduce_fusion
  13.3 0.1 fusion.54
  13.4 1.3 pad_maximum_fusion.2
  14.7 16.8 %all-to-all-start = ((bf16[32,2,4224]{2,1,0:T(2,128)(2,1)}), bf16[32,2,4224]{2,1,0:T(2,128)(2,1)S(1)}, u32[]{:S(2)}, u32[]{:S(2)}) async-start(bf16[32,2,4224]{2,1,0:T(2,128)(2,1)} %pad_maximum_fusion.2), calls=%async_computation | async-start | bytes 1081344 | tf_op jit(solution)/shard_map/all_to_all | solution.py:177
  31.5 0.1 copy.73
  31.7 0.1 copy.72
  31.8 0.7 pad_maximum_fusion.4
  32.5 39.0 %all-to-all-done = bf16[32,2,4224]{2,1,0:T(2,128)(2,1)S(1)} async-done(((bf16[32,2,4224]{2,1,0:T(2,128)(2,1)}), bf16[32,2,4224]{2,1,0:T(2,128)(2,1)S(1)}, u32[]{:S(2)}, u32[]{:S(2)}) %all-to-all-start) | async-done | bytes 540704 | tf_op jit(solution)/shard_map/all_to_all | solution.py:177
  71.5 33.4 %all-gather.3.cloned.1.call-done = bf16[2,2048,512]{2,1,0:T(8,128)(2,1)} async-done(((bf16[2,64,512]{2,1,0:T(8,128)(2,1)}), bf16[2,2048,512]{2,1,0:T(8,128)(2,1)}) %all-gather.3.cloned.1.call-update) | async-done | bytes 4194320 | tf_op jit(solution)/shard_map/all_gather | solution.py:178
  105.0 1.1 reshape.199
  106.1 0.1 iota_compare_fusion
  106.3 1.3 add_divide_fusion
  107.6 0.4 fusion.80
  107.9 0.4 reshape.202
  108.3 0.1 reshape.197
  108.4 0.1 convert_reduce_fusion
  108.5 0.1 reshape.201
  108.6 3.2 fusion.5
  111.8 3.2 copy-done.1
  115.0 2.2 exponential_reduce_fusion
  117.2 54.3 %all-gather.5.cloned.1.call-done = bf16[1,2048,768]{1,2,0:T(8,128)(2,1)} async-done(((bf16[1,128,768]{1,2,0:T(8,128)(2,1)}), bf16[1,2048,768]{1,2,0:T(8,128)(2,1)}) %all-gather.5.cloned.1.call-update) | async-done | bytes 3145744 | tf_op jit(solution)/shard_map/all_gather | solution.py:180
  171.5 1.7 fusion.36
  173.2 1.7 fusion.39
  174.8 1.7 multiply_convert_fusion.2
  176.5 0.5 convolution_convert_fusion
  177.0 0.5 convolution_convert_fusion.1
  177.5 0.5 convolution_convert_fusion.2
  178.0 1.8 pad_maximum_fusion.1
  179.8 4.9 %copy.97 = bf16[2048,768]{1,0:T(8,128)(2,1)} copy(bf16[2048,768]{0,1:T(8,128)(2,1)} %pad_maximum_fusion.1) | data formatting | bytes 6291456
  184.7 6.5 %multiply_reduce_fusion = (f32[2,64,8]{1,2,0:T(8,128)S(1)}, bf16[2,64,8,256]{3,1,2,0:T(8,128)(2,1)S(1)}, bf16[2,8,8,8,256]{4,3,2,1,0:T(8,128)(2,1)}) fusion(f32[2,8,8,8,256]{4,3,2,1,0:T(8,128)S(1)} %bitcast.145, f32[2,8,8,8,256]{4,3,2,1,0:T(8,128)S(1)} %bitcast.144, f32[2,2048,64,8]{1,2,3,0:T(8,128)} %copy-done.1, f32[2,8,64]{2,1,0:T(8,128)S(1)} %log_add_fusion, ...), kind=kOutput, calls=%fused_computation.49 | convolution fusion | flops 1084750848 | bytes 13770752 | tf_op jit(solution)/shard_map/shpr,srd->sphd/dot_general | solution.py:201
  191.2 5.5 %fusion.2 = bf16[2,8,64,2048]{3,2,1,0:T(8,128)(2,1)S(1)} fusion(f32[2,2048,64,8]{1,2,3,0:T(8,128)} %copy-done.1, bf16[2,64,8,256]{3,1,2,0:T(8,128)(2,1)S(1)} %get-tuple-element.52, f32[2,8,64]{2,1,0:T(8,128)S(1)} %bitcast.151, f32[2,8,64]{2,1,0:T(8,128)S(1)} %log_add_fusion, pred[64,2048]{1,0:T(8,128)(4,1)S(1)} %iota_compare_fusion, ...), kind=kOutput, calls=%fused_computation.3 | convolution fusion | flops 1088421888 | bytes 15351808 | tf_op jit(solution)/shard_map/sphd,srd->shpr/dot_general | solution.py:215
  196.7 1.3 fusion.26
  197.9 0.7 copy-done.11
  198.6 0.8 copy.104
  199.5 3.1 bitcast_convert_fusion
  202.6 1.6 fusion.29
  204.2 0.1 convert_element_type.153
  204.3 1.5 fusion.34
  205.9 1.5 fusion.8
  207.4 0.2 reshape.198
  207.7 1.0 pad_maximum_fusion.3
  208.7 13.9 %all-to-all-start.1 = ((bf16[32,2,2176]{2,1,0:T(2,128)(2,1)}), bf16[32,2,2176]{2,1,0:T(2,128)(2,1)S(1)}, u32[]{:S(2)}, u32[]{:S(2)}) async-start(bf16[32,2,2176]{2,1,0:T(2,128)(2,1)} %pad_maximum_fusion.3), calls=%async_computation.1 | async-start | bytes 557056 | tf_op jit(solution)/shard_map/all_to_all | solution.py:280
  222.5 4.1 %bitcast_convert_fusion.1 = bf16[2,2048,256]{2,1,0:T(8,128)(2,1)S(1)} fusion(bf16[2,8,64,2048]{3,2,1,0:T(8,128)(2,1)} %copy-done.11, bf16[2,8,8,8,256]{4,3,2,1,0:T(8,128)(2,1)} %bitcast.150), kind=kOutput, calls=%fused_computation.13 | convolution fusion | flops 1074790400 | bytes 6815744 | tf_op jit(solution)/shard_map/shpr,sphd->srd/dot_general | solution.py:224
  226.6 2.3 pad_maximum_fusion.parts_ref
  228.9 105.9 %shard_map.187 = bf16[2,64,512]{2,1,0:T(8,128)(2,1)} custom-call(bf16[2,2048,512]{2,1,0:T(8,128)(2,1)} %pad_maximum_fusion.parts_ref), custom_call_target="tpu_custom_call" | custom-call | tf_op jit(solution)/shard_map/pallas_call | solution.py:96
  334.8 0.8 copy.105
  335.6 1.5 fusion.81
  337.2 0.1 copy.100
  337.4 0.2 slice.63
  337.6 0.1 multiply_reduce_fusion.1
  337.7 0.6 select_convert_fusion
  338.3 1.1 fusion.7
  339.4 1.1 copy.98
  340.6 0.7 slice_bitcast_fusion
  341.2 0.8 copy.89
  342.0 0.8 copy.90
  (47 shorter events, 0.6 us)
Async XLA Ops:
  7.2 3.6 %copy-start = (bf16[128,2048]{1,0:T(8,128)(2,1)S(1)}, bf16[128,2048]{1,0:T(8,128)(2,1)}, u32[]{:S(2)}) copy-start(bf16[128,2048]{1,0:T(8,128)(2,1)} %param.18) | copy-start | bytes 1572868
  7.2 24.3 %copy-start.7 = (bf16[1,128,256]{2,1,0:T(8,128)(2,1)S(1)}, bf16[1,128,256]{2,1,0:T(8,128)(2,1)}, u32[]{:S(2)}) copy-start(bf16[1,128,256]{2,1,0:T(8,128)(2,1)} %param.22) | copy-start | bytes 196612
  7.2 24.5 %copy-start.8 = (bf16[1,128,256]{2,1,0:T(8,128)(2,1)S(1)}, bf16[1,128,256]{2,1,0:T(8,128)(2,1)}, u32[]{:S(2)}) copy-start(bf16[1,128,256]{2,1,0:T(8,128)(2,1)} %param.21) | copy-start | bytes 196612
  7.2 24.6 %copy-start.9 = (bf16[1,256,128]{2,1,0:T(8,128)(2,1)S(1)}, bf16[1,256,128]{2,1,0:T(8,128)(2,1)}, u32[]{:S(2)}) copy-start(bf16[1,256,128]{2,1,0:T(8,128)(2,1)} %param.23) | copy-start | bytes 196612
  7.2 97.8 %copy-start.4 = (bf16[2,64,2048]{2,1,0:T(8,128)(2,1)S(1)}, bf16[2,64,2048]{2,1,0:T(8,128)(2,1)}, u32[]{:S(2)}) copy-start(bf16[2,64,2048]{2,1,0:T(8,128)(2,1)} %param.16) | copy-start | bytes 1572868
  7.2 99.0 %copy-start.5 = (bf16[2,64,2048]{2,1,0:T(8,128)(2,1)S(1)}, bf16[2,64,2048]{2,1,0:T(8,128)(2,1)}, u32[]{:S(2)}) copy-start(bf16[2,64,2048]{2,1,0:T(8,128)(2,1)} %param.15) | copy-start | bytes 1572868
  7.2 97.7 %all-gather.3.cloned.1.call-start = ((), (), s32[]{:S(2)}) async-start(), calls=%async_computation.3 | async-start | bytes 4325376 | tf_op jit(solution)/shard_map/all_gather | solution.py:178
  14.7 56.8 %all-to-all-start = ((bf16[32,2,4224]{2,1,0:T(2,128)(2,1)}), bf16[32,2,4224]{2,1,0:T(2,128)(2,1)S(1)}, u32[]{:S(2)}, u32[]{:S(2)}) async-start(bf16[32,2,4224]{2,1,0:T(2,128)(2,1)} %pad_maximum_fusion.2), calls=%async_computation | async-start | bytes 1081344 | tf_op jit(solution)/shard_map/all_to_all | solution.py:177
  31.5 140.0 %all-gather.5.cloned.1.call-start = ((), (), s32[]{:S(2)}) async-start(), calls=%async_computation.4 | async-start | bytes 3342336 | tf_op jit(solution)/shard_map/all_gather | solution.py:180
  104.9 234.5 %reduce-scatter.4.cloned.1.call-start = ((), (), s32[]{:S(2)}) async-start(), calls=%async_computation.5 | async-start | bytes 3342336
  111.8 3.2 copy-start.1
  179.8 4.9 %copy-start.2 = (f32[2,64,2048]{2,1,0:T(8,128)S(1)}, f32[2,64,2048]{2,1,0:T(8,128)}, u32[]{:S(2)}) copy-start(f32[2,64,2048]{2,1,0:T(8,128)} %reshape.199) | copy-start | bytes 3145732
  179.8 4.9 %copy-start.3 = (f32[2,64,2048]{2,1,0:T(8,128)S(1)}, f32[2,64,2048]{2,1,0:T(8,128)}, u32[]{:S(2)}) copy-start(f32[2,64,2048]{2,1,0:T(8,128)} %add_divide_fusion) | copy-start | bytes 3145732
  184.7 6.5 %copy-start.10 = (bf16[2,2048,512]{2,1,0:T(8,128)(2,1)S(1)}, bf16[2,2048,512]{2,1,0:T(8,128)(2,1)}, u32[]{:S(2)}) copy-start(bf16[2,2048,512]{2,1,0:T(8,128)(2,1)} %all-gather.3.cloned.1.call-done) | copy-start | bytes 12582916
  184.7 14.8 %slice-start = ((s8[8388608]{0:T(1024)(128)(4,1)}), s8[4194304]{0:T(1024)(128)(4,1)S(1)}, s32[]{:S(2)}) async-start(s8[8388608]{0:T(1024)(128)(4,1)} %bitcast.136), calls=%async_computation.6 | async-start | bytes 8388608
  191.2 8.3 %slice-start.1 = ((s8[8388608]{0:T(1024)(128)(4,1)}), s8[4194304]{0:T(1024)(128)(4,1)S(1)}, s32[]{:S(2)}) async-start(s8[8388608]{0:T(1024)(128)(4,1)} %bitcast.136), calls=%async_computation.7 | async-start | bytes 8388608
  196.7 2.0 copy-start.11
  208.7 128.5 %all-to-all-start.1 = ((bf16[32,2,2176]{2,1,0:T(2,128)(2,1)}), bf16[32,2,2176]{2,1,0:T(2,128)(2,1)S(1)}, u32[]{:S(2)}, u32[]{:S(2)}) async-start(bf16[32,2,2176]{2,1,0:T(2,128)(2,1)} %pad_maximum_fusion.3), calls=%async_computation.1 | async-start | bytes 557056 | tf_op jit(solution)/shard_map/all_to_all | solution.py:280
  228.9 105.9 %copy-start.6 = (bf16[2,8,8,8,256]{4,3,2,1,0:T(8,128)(2,1)S(1)}, bf16[2,8,8,8,256]{4,3,2,1,0:T(8,128)(2,1)}, u32[]{:S(2)}) copy-start(bf16[2,8,8,8,256]{4,3,2,1,0:T(8,128)(2,1)} %get-tuple-element.55) | copy-start | bytes 1572868
Sparse Core Ops, SparseCore 0:
  10.8 94.0 all-gather.2
  108.5 62.9 all-gather.4
  184.8 89.6 reduce-scatter.3

commit v11 on v9

--- a/solution.py
+++ b/solution.py
@@ -175,8 +175,14 @@
         [gate_proj, up_proj, jnp.transpose(down_proj, (0, 2, 1))], axis=2
     )
     recv_all = lax.all_to_all(send_all, "expert", split_axis=0, concat_axis=0, tiled=True)
-    weight_full = lax.all_gather(weight_cat, "dp", axis=1, tiled=True)[0]
-    packed, recv_all = lax.optimization_barrier((packed, recv_all))
+    groups = lax.axis_size("dp")
+    weight_full = lax.all_to_all(
+        jnp.broadcast_to(weight_cat, (groups,) + weight_cat.shape[1:]),
+        "dp",
+        split_axis=0,
+        concat_axis=0,
+        tiled=True,
+    ).reshape(groups * weight_cat.shape[1], weight_cat.shape[2])
     gathered = lax.all_gather(packed, "expert", axis=1, tiled=True)
     rows_in = recv_all[:, :, :model_cols]
     grads_in = recv_all[:, :, model_cols : 2 * model_cols]

time: 319 us -> 314 us (0.984)
    all_to_all x0 -> x1, waiting for transfers between devices: none -> 43.1 us  [shards(): lax.all_to_all(jnp.broadcast_to(weight_cat, (groups,) + weight_cat.shape[...]
    all_gather x1, waiting for transfers between devices: 35.3 us -> 0.01 us  [shards(): gathered = lax.all_gather(packed, 'expert', axis=1, tiled=True)]
    all_gather x1 -> x0, waiting for transfers between devices: 13.7 us -> none  [shards(): weight_full = lax.all_gather(weight_cat, 'dp', axis=1, tiled=True)[0]]
    all_to_all x1, starting transfers between devices: 13.9 us -> 5.33 us  [shards(): lax.all_to_all(jnp.concatenate([input_rows.reshape(devices, CAP, model_wi...]
    all_to_all x0 -> x1, starting transfers between devices: none -> 7.03 us  [shards(): lax.all_to_all(jnp.broadcast_to(weight_cat, (groups,) + weight_cat.shape[...]
    all_to_all x1, waiting for transfers between devices: 33.5 us -> 39.5 us  [shards(): lax.all_to_all(send_all, 'expert', split_axis=0, concat_axis=0, tiled=True)]
    all_to_all x1, waiting for transfers between devices: 22.4 us -> 19.1 us  [shards(): lax.all_to_all(jnp.concatenate([input_rows.reshape(devices, CAP, model_wi...]
  transfers between devices with their start and end apart: 5 -> 5, of which waited for: 4 -> 3; matrix products, arithmetic and copies ran while one was open for 16% -> 16% of each run, Pallas kernels for 33% -> 34%
where the time goes in v11:
time: 314 us; the launch traced here: 313 us
  Pallas kernels  107 us (34%)
  waiting for transfers between devices  102 us (32%)
  starting transfers between devices  29.4 us (9%)
  matrix products  28.5 us (9%)
  other arithmetic  16.3 us (5%)
  local copies, waits for them, and re-layouts  16.2 us (5%)
  between operations  14.5 us (5%)
    pallas_call x1, Pallas kernels, pair_return(): pl.pallas_call(pair_chain_kernel, out_shape=jax.ShapeDtypeStruct((seqs, b...  107 us
    all_to_all x1, waiting for transfers between devices, shards(): lax.all_to_all(jnp.broadcast_to(weight_cat, (groups,) + weight_cat.shape[...  43.1 us
    all_to_all x1, waiting for transfers between devices, shards(): lax.all_to_all(send_all, 'expert', split_axis=0, concat_axis=0, tiled=True)  39.5 us
    all_to_all x1, waiting for transfers between devices, shards(): lax.all_to_all(jnp.concatenate([input_rows.reshape(devices, CAP, model_wi...  19.1 us
    all_to_all x1, starting transfers between devices, shards(): lax.all_to_all(send_all, 'expert', split_axis=0, concat_axis=0, tiled=True)  16.7 us
    unnamed x27, local copies, waits for them, and re-layouts  8.42 us
    all_to_all x1, starting transfers between devices, shards(): lax.all_to_all(jnp.broadcast_to(weight_cat, (groups,) + weight_cat.shape[...  7.03 us
  transfers between devices with their start and end apart: 5, of which 3 were waited for; matrix products, arithmetic and copies ran while one was open for 16% of the time, Pallas kernels for 34%

profile of v11, /device:TPU:1, one launch (start us, length us, event | category | flops | bytes accessed | tf_op | source)
XLA Modules:
  0.0 313.2 jit_solution(11357350889365778631)
XLA Ops:
  7.3 1.6 pad_maximum_fusion.4
  8.9 0.7 fusion.64
  9.6 0.7 select_reduce_fusion.1
  10.3 0.2 fusion.16
  10.5 0.7 select_reduce_fusion
  11.3 0.1 fusion.40
  11.5 0.2 convolution_convert_fusion.3
  11.7 0.2 reshape.199
  11.9 1.3 convolution_convert_fusion.4
  13.2 0.2 reshape.198
  13.4 1.3 pad_maximum_fusion.2
  14.6 16.7 %all-to-all-start = ((bf16[32,2,4224]{2,1,0:T(2,128)(2,1)}), bf16[32,2,4224]{2,1,0:T(2,128)(2,1)S(1)}, u32[]{:S(2)}, u32[]{:S(2)}) async-start(bf16[32,2,4224]{2,1,0:T(2,128)(2,1)} %pad_maximum_fusion.2), calls=%async_computation | async-start | bytes 1081344 | tf_op jit(solution)/shard_map/all_to_all | solution.py:177
  31.4 0.1 copy.87
  31.5 0.1 copy.86
  31.7 0.1 copy.88
  31.9 39.5 %all-to-all-done = bf16[32,2,4224]{2,1,0:T(2,128)(2,1)S(1)} async-done(((bf16[32,2,4224]{2,1,0:T(2,128)(2,1)}), bf16[32,2,4224]{2,1,0:T(2,128)(2,1)S(1)}, u32[]{:S(2)}, u32[]{:S(2)}) %all-to-all-start) | async-done | bytes 540704 | tf_op jit(solution)/shard_map/all_to_all | solution.py:177
  71.3 2.0 broadcast_in_dim.106
  73.4 7.0 %all-to-all-start.1 = ((bf16[16,128,768]{2,1,0:T(8,128)(2,1)}), bf16[16,128,768]{2,1,0:T(8,128)(2,1)}, u32[]{:S(2)}, u32[]{:S(2)}) async-start(bf16[16,128,768]{2,1,0:T(8,128)(2,1)} %broadcast_in_dim.106), calls=%async_computation.1 | async-start | bytes 6291456 | tf_op jit(solution)/shard_map/all_to_all | solution.py:179
  80.4 1.1 reshape.203
  81.5 0.1 iota_compare_fusion
  81.7 1.3 add_divide_fusion
  82.9 0.4 fusion.66
  83.3 0.4 reshape.206
  83.8 0.1 convert_reduce_fusion
  83.9 0.1 reshape.205
  84.0 43.1 %all-to-all-done.1 = bf16[16,128,768]{2,1,0:T(8,128)(2,1)} async-done(((bf16[16,128,768]{2,1,0:T(8,128)(2,1)}), bf16[16,128,768]{2,1,0:T(8,128)(2,1)}, u32[]{:S(2)}, u32[]{:S(2)}) %all-to-all-start.1) | async-done | bytes 3145760 | tf_op jit(solution)/shard_map/all_to_all | solution.py:179
  127.1 1.5 fusion.22
  128.7 1.5 fusion.25
  130.2 1.6 multiply_convert_fusion.2
  131.8 1.8 fusion.15
  133.5 0.1 convert_element_type.153
  133.7 1.7 fusion.20
  135.3 1.7 fusion.8
  137.0 0.2 reshape.202
  137.3 1.0 pad_maximum_fusion.3
  138.3 5.3 %all-to-all-start.2 = ((bf16[32,2,2176]{2,1,0:T(2,128)(2,1)}), bf16[32,2,2176]{2,1,0:T(2,128)(2,1)S(1)}, u32[]{:S(2)}, u32[]{:S(2)}) async-start(bf16[32,2,2176]{2,1,0:T(2,128)(2,1)} %pad_maximum_fusion.3), calls=%async_computation.2 | async-start | bytes 557056 | tf_op jit(solution)/shard_map/all_to_all | solution.py:287
  143.6 0.2 reduce-scatter.4.cloned.1.call-start
  143.8 0.5 convolution_convert_fusion.1
  144.3 0.5 convolution_convert_fusion.2
  144.8 0.5 convolution_convert_fusion
  145.3 1.9 pad_maximum_fusion.1
  147.2 19.1 %all-to-all-done.2 = bf16[32,2,2176]{2,1,0:T(2,128)(2,1)S(1)} async-done(((bf16[32,2,2176]{2,1,0:T(2,128)(2,1)}), bf16[32,2,2176]{2,1,0:T(2,128)(2,1)S(1)}, u32[]{:S(2)}, u32[]{:S(2)}) %all-to-all-start.2) | async-done | bytes 278560 | tf_op jit(solution)/shard_map/all_to_all | solution.py:287
  166.4 4.7 %copy.101 = bf16[2048,768]{1,0:T(8,128)(2,1)} copy(bf16[2048,768]{0,1:T(8,128)(2,1)} %pad_maximum_fusion.1) | data formatting | bytes 6291456
  171.2 0.2 slice.68
  171.4 0.1 multiply_reduce_fusion.1
  171.5 0.6 select_convert_fusion
  172.1 1.1 fusion.7
  173.3 3.1 fusion.5
  176.4 2.2 exponential_reduce_fusion
  178.6 0.7 copy-done.8
  179.4 2.1 multiply_reduce_fusion
  181.5 3.3 %fusion.2 = bf16[2,8,64,2048]{3,2,1,0:T(8,128)(2,1)S(1)} fusion(f32[2,2048,64,8]{1,2,3,0:T(8,128)S(1)} %get-tuple-element.63, bf16[2,64,8,256]{3,1,2,0:T(8,128)(2,1)S(1)} %get-tuple-element.50, f32[2,8,64]{2,1,0:T(8,128)S(1)} %bitcast.143, f32[2,8,64]{2,1,0:T(8,128)S(1)} %log_add_fusion, pred[64,2048]{1,0:T(8,128)(4,1)S(1)} %iota_compare_fusion, ...), kind=kOutput, calls=%fused_computation.3 | convolution fusion | flops 1088421888 | bytes 15351808 | tf_op jit(solution)/shard_map/sphd,srd->shpr/dot_general | solution.py:221
  184.7 1.2 fusion.14
  186.0 0.8 copy.108
  186.8 1.8 bitcast_convert_fusion.1
  188.6 3.1 bitcast_convert_fusion
  191.7 2.3 pad_maximum_fusion.parts_ref
  194.0 106.6 %shard_map.187 = bf16[2,64,512]{2,1,0:T(8,128)(2,1)} custom-call(bf16[2,2048,512]{2,1,0:T(8,128)(2,1)} %pad_maximum_fusion.parts_ref), custom_call_target="tpu_custom_call" | custom-call | tf_op jit(solution)/shard_map/pallas_call | solution.py:96
  300.6 0.8 copy.109
  301.5 1.5 fusion.67
  303.0 1.1 copy.102
  304.1 0.7 slice_bitcast_fusion.12
  304.8 0.8 copy.93
  305.6 0.8 copy.94
  (39 shorter events, 0.7 us)
Async XLA Ops:
  7.2 4.3 %copy-start = (bf16[128,2048]{1,0:T(8,128)(2,1)S(1)}, bf16[128,2048]{1,0:T(8,128)(2,1)}, u32[]{:S(2)}) copy-start(bf16[128,2048]{1,0:T(8,128)(2,1)} %param.18) | copy-start | bytes 1572868
  7.2 24.2 %copy-start.5 = (bf16[1,128,256]{2,1,0:T(8,128)(2,1)S(1)}, bf16[1,128,256]{2,1,0:T(8,128)(2,1)}, u32[]{:S(2)}) copy-start(bf16[1,128,256]{2,1,0:T(8,128)(2,1)} %param.22) | copy-start | bytes 196612
  7.2 24.3 %copy-start.6 = (bf16[1,128,256]{2,1,0:T(8,128)(2,1)S(1)}, bf16[1,128,256]{2,1,0:T(8,128)(2,1)}, u32[]{:S(2)}) copy-start(bf16[1,128,256]{2,1,0:T(8,128)(2,1)} %param.21) | copy-start | bytes 196612
  7.2 24.4 %copy-start.7 = (bf16[1,256,128]{2,1,0:T(8,128)(2,1)S(1)}, bf16[1,256,128]{2,1,0:T(8,128)(2,1)}, u32[]{:S(2)}) copy-start(bf16[1,256,128]{2,1,0:T(8,128)(2,1)} %param.23) | copy-start | bytes 196612
  7.2 159.2 %all-gather.2.cloned.1.call-start = ((), (), s32[]{:S(2)}) async-start(), calls=%async_computation.4 | async-start | bytes 4325376 | tf_op jit(solution)/shard_map/all_gather | solution.py:186
  14.6 56.7 %all-to-all-start = ((bf16[32,2,4224]{2,1,0:T(2,128)(2,1)}), bf16[32,2,4224]{2,1,0:T(2,128)(2,1)S(1)}, u32[]{:S(2)}, u32[]{:S(2)}) async-start(bf16[32,2,4224]{2,1,0:T(2,128)(2,1)} %pad_maximum_fusion.2), calls=%async_computation | async-start | bytes 1081344 | tf_op jit(solution)/shard_map/all_to_all | solution.py:177
  31.8 48.6 %copy-start.3 = (bf16[2,64,2048]{2,1,0:T(8,128)(2,1)S(1)}, bf16[2,64,2048]{2,1,0:T(8,128)(2,1)}, u32[]{:S(2)}) copy-start(bf16[2,64,2048]{2,1,0:T(8,128)(2,1)} %param.16) | copy-start | bytes 1572868
  73.4 8.3 %copy-start.4 = (bf16[2,64,2048]{2,1,0:T(8,128)(2,1)S(1)}, bf16[2,64,2048]{2,1,0:T(8,128)(2,1)}, u32[]{:S(2)}) copy-start(bf16[2,64,2048]{2,1,0:T(8,128)(2,1)} %param.15) | copy-start | bytes 1572868
  73.4 53.8 %all-to-all-start.1 = ((bf16[16,128,768]{2,1,0:T(8,128)(2,1)}), bf16[16,128,768]{2,1,0:T(8,128)(2,1)}, u32[]{:S(2)}, u32[]{:S(2)}) async-start(bf16[16,128,768]{2,1,0:T(8,128)(2,1)} %broadcast_in_dim.106), calls=%async_computation.1 | async-start | bytes 6291456 | tf_op jit(solution)/shard_map/all_to_all | solution.py:179
  138.3 28.0 %all-to-all-start.2 = ((bf16[32,2,2176]{2,1,0:T(2,128)(2,1)}), bf16[32,2,2176]{2,1,0:T(2,128)(2,1)S(1)}, u32[]{:S(2)}, u32[]{:S(2)}) async-start(bf16[32,2,2176]{2,1,0:T(2,128)(2,1)} %pad_maximum_fusion.3), calls=%async_computation.2 | async-start | bytes 557056 | tf_op jit(solution)/shard_map/all_to_all | solution.py:287
  143.6 159.4 %reduce-scatter.4.cloned.1.call-start = ((), (), s32[]{:S(2)}) async-start(), calls=%async_computation.5 | async-start | bytes 3342336
  166.4 6.9 %copy-start.9 = (bf16[2,64,2048]{2,1,0:T(8,128)(2,1)S(1)}, bf16[2,64,2048]{2,1,0:T(8,128)(2,1)}, u32[]{:S(2)}) copy-start(bf16[2,64,2048]{2,1,0:T(8,128)(2,1)} %param.12) | copy-start | bytes 1572868
  176.4 2.3 copy-start.1
  176.4 2.3 copy-start.2
  176.4 3.0 copy-start.8
Sparse Core Ops, SparseCore 0:
  10.8 94.2 all-gather.1
  171.3 78.4 reduce-scatter.3

commit v12 on v11

--- a/solution.py
+++ b/solution.py
@@ -284,14 +284,16 @@
     pair_total = pair_return(pair_buffer, devices, 4)
     key_grad = pair_total[:, :, :HEAD]
     value_grad = pair_total[:, :, HEAD:]
-    back_all = lax.all_to_all(
-        jnp.concatenate(
+    back_send = jnp.concatenate(
             [
                 input_rows.reshape(devices, CAP, model_width),
                 jnp.broadcast_to(weight_back.reshape(devices, CAP, 1), (devices, CAP, pad_cols)),
             ],
             axis=2,
-        ),
+        )
+    pair_total, back_send = lax.optimization_barrier((pair_total, back_send))
+    back_all = lax.all_to_all(
+        back_send,
         "expert",
         split_axis=0,
         concat_axis=0,

time: 314 us -> 313 us (level)
  waiting for transfers between devices: 102 us -> 98.8 us
    unnamed x27 -> x31, local copies, waits for them, and re-layouts: 8.42 us -> 8.5 us
  transfers between devices with their start and end apart: 5 -> 5, of which waited for: 3 -> 3; matrix products, arithmetic and copies ran while one was open for 16% -> 17% of each run, Pallas kernels for 34% -> 35%
where the time goes in v12:
time: 313 us; the launch traced here: 312 us
  Pallas kernels  108 us (35%)
  waiting for transfers between devices  98.8 us (32%)
  matrix products  31.3 us (10%)
  starting transfers between devices  27.7 us (9%)
  other arithmetic  16.5 us (5%)
  local copies, waits for them, and re-layouts  15.4 us (5%)
  between operations  14.5 us (5%)
    pallas_call x1, Pallas kernels, pair_return(): pl.pallas_call(pair_chain_kernel, out_shape=jax.ShapeDtypeStruct((seqs, b...  108 us
    all_to_all x1, waiting for transfers between devices, shards(): lax.all_to_all(jnp.broadcast_to(weight_cat, (groups,) + weight_cat.shape[...  43.1 us
    all_to_all x1, waiting for transfers between devices, shards(): lax.all_to_all(send_all, 'expert', split_axis=0, concat_axis=0, tiled=True)  39.5 us
    all_to_all x1, starting transfers between devices, shards(): lax.all_to_all(send_all, 'expert', split_axis=0, concat_axis=0, tiled=True)  16.7 us
    all_to_all x1, waiting for transfers between devices, shards(): lax.all_to_all(back_send, 'expert', split_axis=0, concat_axis=0, tiled=True)  16.2 us
    unnamed x31, local copies, waits for them, and re-layouts  8.5 us
    all_to_all x1, starting transfers between devices, shards(): lax.all_to_all(jnp.broadcast_to(weight_cat, (groups,) + weight_cat.shape[...  7.03 us
  transfers between devices with their start and end apart: 5, of which 3 were waited for; matrix products, arithmetic and copies ran while one was open for 17% of the time, Pallas kernels for 35%

profile of v12, /device:TPU:1, one launch (start us, length us, event | category | flops | bytes accessed | tf_op | source)
XLA Modules:
  0.0 311.7 jit_solution(14582769271452425845)
XLA Ops:
  7.3 1.6 pad_maximum_fusion.4
  8.9 0.7 fusion.64
  9.6 0.7 select_reduce_fusion.1
  10.3 0.2 fusion.16
  10.5 0.7 select_reduce_fusion
  11.3 0.1 fusion.40
  11.5 0.2 convolution_convert_fusion.3
  11.7 0.2 reshape.199
  11.9 1.3 convolution_convert_fusion.4
  13.2 0.2 reshape.198
  13.4 1.3 pad_maximum_fusion.2
  14.6 16.7 %all-to-all-start = ((bf16[32,2,4224]{2,1,0:T(2,128)(2,1)}), bf16[32,2,4224]{2,1,0:T(2,128)(2,1)S(1)}, u32[]{:S(2)}, u32[]{:S(2)}) async-start(bf16[32,2,4224]{2,1,0:T(2,128)(2,1)} %pad_maximum_fusion.2), calls=%async_computation | async-start | bytes 1081344 | tf_op jit(solution)/shard_map/all_to_all | solution.py:177
  31.4 0.1 copy.87
  31.5 0.1 copy.86
  31.7 0.1 copy.88
  31.9 39.5 %all-to-all-done = bf16[32,2,4224]{2,1,0:T(2,128)(2,1)S(1)} async-done(((bf16[32,2,4224]{2,1,0:T(2,128)(2,1)}), bf16[32,2,4224]{2,1,0:T(2,128)(2,1)S(1)}, u32[]{:S(2)}, u32[]{:S(2)}) %all-to-all-start) | async-done | bytes 540704 | tf_op jit(solution)/shard_map/all_to_all | solution.py:177
  71.3 2.0 broadcast_in_dim.106
  73.4 7.0 %all-to-all-start.1 = ((bf16[16,128,768]{2,1,0:T(8,128)(2,1)}), bf16[16,128,768]{2,1,0:T(8,128)(2,1)}, u32[]{:S(2)}, u32[]{:S(2)}) async-start(bf16[16,128,768]{2,1,0:T(8,128)(2,1)} %broadcast_in_dim.106), calls=%async_computation.1 | async-start | bytes 6291456 | tf_op jit(solution)/shard_map/all_to_all | solution.py:179
  80.5 1.1 reshape.203
  81.6 0.1 iota_compare_fusion
  81.7 1.3 add_divide_fusion
  83.0 0.4 fusion.66
  83.4 0.4 reshape.206
  83.8 0.1 convert_reduce_fusion
  83.9 0.1 reshape.205
  84.0 43.1 %all-to-all-done.1 = bf16[16,128,768]{2,1,0:T(8,128)(2,1)} async-done(((bf16[16,128,768]{2,1,0:T(8,128)(2,1)}), bf16[16,128,768]{2,1,0:T(8,128)(2,1)}, u32[]{:S(2)}, u32[]{:S(2)}) %all-to-all-start.1) | async-done | bytes 3145760 | tf_op jit(solution)/shard_map/all_to_all | solution.py:179
  127.1 1.5 fusion.22
  128.7 1.5 fusion.25
  130.2 1.6 multiply_convert_fusion.2
  131.8 1.8 fusion.15
  133.5 0.1 convert_element_type.153
  133.7 1.7 fusion.20
  135.3 1.7 fusion.8
  137.0 0.2 reshape.202
  137.2 0.5 convolution_convert_fusion.1
  137.7 0.5 convolution_convert_fusion.2
  138.1 0.5 convolution_convert_fusion
  138.6 2.0 pad_maximum_fusion.1
  140.7 1.0 pad_maximum_fusion.3
  141.7 4.7 %copy.101 = bf16[2048,768]{1,0:T(8,128)(2,1)} copy(bf16[2048,768]{0,1:T(8,128)(2,1)} %pad_maximum_fusion.1) | data formatting | bytes 6291456
  146.5 3.1 fusion.5
  149.6 2.2 exponential_reduce_fusion
  151.9 0.6 copy-done.9
  152.4 2.1 multiply_reduce_fusion
  154.5 3.3 %fusion.2 = bf16[2,8,64,2048]{3,2,1,0:T(8,128)(2,1)S(1)} fusion(f32[2,2048,64,8]{1,2,3,0:T(8,128)S(1)} %get-tuple-element.65, bf16[2,64,8,256]{3,1,2,0:T(8,128)(2,1)S(1)} %get-tuple-element.52, f32[2,8,64]{2,1,0:T(8,128)S(1)} %bitcast.143, f32[2,8,64]{2,1,0:T(8,128)S(1)} %log_add_fusion, pred[64,2048]{1,0:T(8,128)(4,1)S(1)} %iota_compare_fusion, ...), kind=kOutput, calls=%fused_computation.3 | convolution fusion | flops 1088421888 | bytes 15351808 | tf_op jit(solution)/shard_map/sphd,srd->shpr/dot_general | solution.py:221
  157.8 1.8 bitcast_convert_fusion.1
  159.5 0.2 copy-done.11
  159.7 3.1 bitcast_convert_fusion
  162.8 2.3 pad_maximum_fusion.parts_ref
  165.1 107.6 %shard_map.187 = bf16[2,64,512]{2,1,0:T(8,128)(2,1)} custom-call(bf16[2,2048,512]{2,1,0:T(8,128)(2,1)} %pad_maximum_fusion.parts_ref), custom_call_target="tpu_custom_call" | custom-call | tf_op jit(solution)/shard_map/pallas_call | solution.py:96
  272.7 3.9 %all-to-all-start.2 = ((bf16[32,2,2176]{2,1,0:T(2,128)(2,1)}), bf16[32,2,2176]{2,1,0:T(2,128)(2,1)S(1)}, u32[]{:S(2)}, u32[]{:S(2)}) async-start(bf16[32,2,2176]{2,1,0:T(2,128)(2,1)} %pad_maximum_fusion.3), calls=%async_computation.2 | async-start | bytes 557056 | tf_op jit(solution)/shard_map/all_to_all | solution.py:295
  276.6 4.1 %fusion.14 = bf16[2,8,8,8,256]{4,3,2,1,0:T(8,128)(2,1)S(1)} fusion(bf16[2,8,64,2048]{3,2,1,0:T(8,128)(2,1)} %copy-done.11, bf16[2,2048,512]{2,1,0:T(8,128)(2,1)} %all-gather.2.cloned.1.call-done), kind=kOutput, calls=%fused_computation.32 | convolution fusion | flops 1074003968 | bytes 6815744 | tf_op jit(solution)/shard_map/shpr,srd->sphd/dot_general | solution.py:227
  280.7 0.8 copy.108
  281.5 0.8 copy.109
  282.4 0.7 fusion.67
  283.1 16.2 %all-to-all-done.2 = bf16[32,2,2176]{2,1,0:T(2,128)(2,1)S(1)} async-done(((bf16[32,2,2176]{2,1,0:T(2,128)(2,1)}), bf16[32,2,2176]{2,1,0:T(2,128)(2,1)S(1)}, u32[]{:S(2)}, u32[]{:S(2)}) %all-to-all-start.2) | async-done | bytes 278560 | tf_op jit(solution)/shard_map/all_to_all | solution.py:295
  299.4 0.2 slice.68
  299.6 0.1 multiply_reduce_fusion.1
  299.8 0.6 select_convert_fusion
  300.4 1.1 fusion.7
  301.5 1.1 copy.102
  302.6 0.7 slice_bitcast_fusion.12
  303.3 0.8 copy.93
  304.1 0.8 copy.94
  (43 shorter events, 0.8 us)
Async XLA Ops:
  7.2 4.3 %copy-start = (bf16[128,2048]{1,0:T(8,128)(2,1)S(1)}, bf16[128,2048]{1,0:T(8,128)(2,1)}, u32[]{:S(2)}) copy-start(bf16[128,2048]{1,0:T(8,128)(2,1)} %param.18) | copy-start | bytes 1572868
  7.2 24.2 %copy-start.6 = (bf16[1,128,256]{2,1,0:T(8,128)(2,1)S(1)}, bf16[1,128,256]{2,1,0:T(8,128)(2,1)}, u32[]{:S(2)}) copy-start(bf16[1,128,256]{2,1,0:T(8,128)(2,1)} %param.22) | copy-start | bytes 196612
  7.2 24.3 %copy-start.7 = (bf16[1,128,256]{2,1,0:T(8,128)(2,1)S(1)}, bf16[1,128,256]{2,1,0:T(8,128)(2,1)}, u32[]{:S(2)}) copy-start(bf16[1,128,256]{2,1,0:T(8,128)(2,1)} %param.21) | copy-start | bytes 196612
  7.2 24.4 %copy-start.8 = (bf16[1,256,128]{2,1,0:T(8,128)(2,1)S(1)}, bf16[1,256,128]{2,1,0:T(8,128)(2,1)}, u32[]{:S(2)}) copy-start(bf16[1,256,128]{2,1,0:T(8,128)(2,1)} %param.23) | copy-start | bytes 196612
  7.2 134.5 %all-gather.2.cloned.1.call-start = ((), (), s32[]{:S(2)}) async-start(), calls=%async_computation.4 | async-start | bytes 4325376 | tf_op jit(solution)/shard_map/all_gather | solution.py:186
  14.6 56.7 %all-to-all-start = ((bf16[32,2,4224]{2,1,0:T(2,128)(2,1)}), bf16[32,2,4224]{2,1,0:T(2,128)(2,1)S(1)}, u32[]{:S(2)}, u32[]{:S(2)}) async-start(bf16[32,2,4224]{2,1,0:T(2,128)(2,1)} %pad_maximum_fusion.2), calls=%async_computation | async-start | bytes 1081344 | tf_op jit(solution)/shard_map/all_to_all | solution.py:177
  31.8 48.6 %copy-start.3 = (bf16[2,64,2048]{2,1,0:T(8,128)(2,1)S(1)}, bf16[2,64,2048]{2,1,0:T(8,128)(2,1)}, u32[]{:S(2)}) copy-start(bf16[2,64,2048]{2,1,0:T(8,128)(2,1)} %param.16) | copy-start | bytes 1572868
  73.4 8.3 %copy-start.4 = (bf16[2,64,2048]{2,1,0:T(8,128)(2,1)S(1)}, bf16[2,64,2048]{2,1,0:T(8,128)(2,1)}, u32[]{:S(2)}) copy-start(bf16[2,64,2048]{2,1,0:T(8,128)(2,1)} %param.15) | copy-start | bytes 1572868
  73.4 53.8 %all-to-all-start.1 = ((bf16[16,128,768]{2,1,0:T(8,128)(2,1)}), bf16[16,128,768]{2,1,0:T(8,128)(2,1)}, u32[]{:S(2)}, u32[]{:S(2)}) async-start(bf16[16,128,768]{2,1,0:T(8,128)(2,1)} %broadcast_in_dim.106), calls=%async_computation.1 | async-start | bytes 6291456 | tf_op jit(solution)/shard_map/all_to_all | solution.py:179
  80.4 221.1 %reduce-scatter.4.cloned.1.call-start = ((), (), s32[]{:S(2)}) async-start(), calls=%async_computation.5 | async-start | bytes 3342336
  141.7 4.8 %copy-start.10 = (bf16[2,64,2048]{2,1,0:T(8,128)(2,1)S(1)}, bf16[2,64,2048]{2,1,0:T(8,128)(2,1)}, u32[]{:S(2)}) copy-start(bf16[2,64,2048]{2,1,0:T(8,128)(2,1)} %param.12) | copy-start | bytes 1572868
  149.6 2.3 copy-start.1
  149.6 2.3 copy-start.2
  149.6 2.8 copy-start.9
  157.8 2.0 copy-start.11
  272.7 26.6 %all-to-all-start.2 = ((bf16[32,2,2176]{2,1,0:T(2,128)(2,1)}), bf16[32,2,2176]{2,1,0:T(2,128)(2,1)S(1)}, u32[]{:S(2)}, u32[]{:S(2)}) async-start(bf16[32,2,2176]{2,1,0:T(2,128)(2,1)} %pad_maximum_fusion.3), calls=%async_computation.2 | async-start | bytes 557056 | tf_op jit(solution)/shard_map/all_to_all | solution.py:295
  276.6 5.8 %copy-start.5 = (bf16[2,64,512]{2,1,0:T(8,128)(2,1)S(1)}, bf16[2,64,512]{2,1,0:T(8,128)(2,1)}, u32[]{:S(2)}) copy-start(bf16[2,64,512]{2,1,0:T(8,128)(2,1)} %shard_map.187) | copy-start | bytes 393220
Sparse Core Ops, SparseCore 0:
  10.8 94.2 all-gather.1
  146.6 79.6 reduce-scatter.3
